TPU v7x, 32 devices: a whole 2x2x4 slice. The times are simulated.
32 devices in a mesh: view: 2 (over y), row: 2 (over x), col: 8 (over z, core).
Axes of the slice: x: 2, y: 2, z: 4, core: 2. Of those that a mesh axis runs over, the one named last changes fastest.
Arguments:
- inputs: bfloat16 [2, 512, 8192], P('view', 'col', 'row'), may hold values from -28 to 28, as said below
- weight: bfloat16 [8192, 8192], P('row', 'col'), may hold values from -0.0625 to 0.0625
Outputs:
- grad_hidden: bfloat16 [2, 512, 8192], P('view', 'col', 'row')
- grad_weight: float32 [8192, 8192], P('row', 'col')
Inputs may be any that keep to these rules, and one draw needn't show every extreme that they name: `inputs`: feature activations of the two views of a clip; each feature has its own scale.
All inputs are finite; a program needn't handle non-finite values.
Results may differ from a plain program's by a relative error of at most 0.025.
Values may be sent and summed in bfloat16 or wider, within the bound.
No kernel may reach another device: no remote copies, remote signals or barrier semaphores. Data moves between devices by JAX's collectives and lax.ppermute only.
A program may use at most 128 MiB of HBM per device.

v0:
```python
import math

import jax
import jax.numpy as jnp
from jax import lax
from jax.sharding import PartitionSpec as P


off_weight = 0.0051
norm_eps = 1e-05


def swap(block, axis, distance):
    count = lax.axis_size(axis)
    return lax.ppermute(block, axis, [(at, at ^ distance) for at in range(count)])


def chip_moves(block, moves):
    route = [(2 * a + core, 2 * b + core) for a, b in moves for core in (0, 1)]
    return lax.ppermute(block, "col", route)


def wide(block):
    return block.astype(jnp.float32)


def narrow(block):
    return block.astype(jnp.bfloat16)


def after(block, *earlier):
    return lax.optimization_barrier((block, *earlier))[0]


def add(first, second):
    return narrow(wide(first) + wide(second))


def sum_over(block, axis, distance=1):
    while distance < lax.axis_size(axis):
        block = add(block, swap(block, axis, distance))
        distance *= 2
    return block


def in_order(own, other, core):
    first = jnp.where(core == 0, own, other)
    second = jnp.where(core == 0, other, own)
    return jnp.concatenate([first, second], axis=0)


OUTER_PAIRS = [(0, 1), (1, 0), (2, 3), (3, 2)]
MIDDLE = [(1, 2), (2, 1)]
OUTWARD = [(1, 0), (2, 3)]
INWARD = [(0, 1), (3, 2)]


def shards(inputs, weight):
    columns = lax.axis_size("col")
    row = lax.axis_index("row")
    col = lax.axis_index("col")
    core = col % 2
    chip = col // 2
    local = inputs[0]
    share = local.shape[0]
    batch = share * columns
    width = weight.shape[1]
    line = columns == 8

    if line:
        halves = jnp.split(local, 2, axis=0)
        near = [chip_moves(part, OUTER_PAIRS) for part in halves]
        middle = [chip_moves(part, MIDDLE) for part in halves]
        across = [chip_moves(part, MIDDLE) for part in near]
        outward = [chip_moves(part, OUTWARD) for part in middle]
        last = [chip_moves(part, OUTWARD) for part in across]
        low = chip < 2
        chips = [
            chip,
            chip ^ 1,
            jnp.where(low, 2, 1),
            jnp.where(low, 3, 0),
        ]
        starts = [at * (2 * share) for at in chips]
        arrivals = [
            (0, 0, [(part,) for part in halves]),
            (1, 0, [(part,) for part in near]),
            (2, 0, list(zip(middle, outward))),
            (3, 0, [(across[0], last[0])]),
            (3, share // 2, [(across[1], last[1])]),
        ]
        places = []
        for at, shift, pieces in arrivals:
            size = len(pieces) * (share // 2)
            places.append(
                [(starts[at] + side * share + shift, size) for side in range(2)]
            )
    else:
        arrivals = [(0, 0, [(lax.all_gather(local, "col", axis=0, tiled=True),)])]
        places = [[(0, batch)]]

    pre = jnp.zeros((batch, width), jnp.float32)
    pre_other = jnp.zeros((batch, width), jnp.bfloat16)
    streams, own_blocks, parts, sent = [], [], [], []
    for at, (place, (_, _, pieces)) in enumerate(zip(places, arrivals)):
        merged = []
        for piece in pieces:
            newest = piece[-1]
            if at >= 1:
                newest = after(newest, parts[at - 1])
            if at >= 2:
                newest = after(newest, sent[at - 2])
            merged.append(piece[0] + newest if len(piece) == 2 else newest)
        stream = jnp.concatenate(merged, axis=0) if len(merged) > 1 else merged[0]
        streams.append(stream)
        block = in_order(stream, swap(stream, "col", 1), core) if line else stream
        own_blocks.append(block)
        product = jnp.dot(block, weight, preferred_element_type=jnp.float32)
        parts.append(narrow(product))
        total = wide(parts[at])
        distance = 1
        while distance < lax.axis_size("row"):
            total = total + wide(swap(narrow(total), "row", distance))
            distance *= 2
        sent.append(narrow(total))
        got = swap(sent[at], "view", 1)
        for side, (start, size) in enumerate(place):
            rows = slice(side * size, (side + 1) * size)
            pre = lax.dynamic_update_slice(pre, total[rows], (start, 0))
            pre_other = lax.dynamic_update_slice(pre_other, got[rows], (start, 0))

    def normalize(values):
        centred = values - jnp.mean(values, axis=0, keepdims=True)
        rstd = lax.rsqrt(jnp.mean(centred * centred, axis=0, keepdims=True) + norm_eps)
        return narrow(centred * rstd), rstd

    normed, rstd = normalize(pre)
    normed_other, _ = normalize(wide(pre_other))
    normed_f = wide(normed)
    other_f = wide(normed_other)
    diag = jnp.sum(normed_f * other_f, axis=0, keepdims=True) / batch

    rows = batch // lax.axis_size("row")
    mine = lax.dynamic_slice(normed_other, (row * rows, 0), (rows, width))
    gram = lax.dot_general(
        mine, normed_other, (((1,), (1,)), ((), ())), preferred_element_type=jnp.float32
    )
    on_diagonal = (
        lax.broadcasted_iota(jnp.int32, gram.shape, 0) + row * rows
        == lax.broadcasted_iota(jnp.int32, gram.shape, 1)
    )
    gram = narrow(jnp.where(on_diagonal, gram - width, gram))
    half = rows // 2
    keep = lax.dynamic_slice(gram, (core * half, 0), (half, batch))
    give = lax.dynamic_slice(gram, ((1 - core) * half, 0), (half, batch))
    piece = add(keep, swap(give, "col", 1))
    piece = sum_over(piece, "col", 2)
    if lax.axis_size("row") == 2:
        across_row = swap(piece, "row", 1)
        pair = jnp.concatenate([piece, across_row], axis=0)
        mate = swap(pair, "col", 1)
        gram = in_order(
            in_order(pair[:half], mate[:half], core),
            in_order(pair[half:], mate[half:], core),
            row,
        )
    else:
        gram = in_order(piece, swap(piece, "col", 1), core)
        gram = lax.all_gather(gram, "row", axis=0, tiled=True)
    mixed = (
        jnp.dot(gram, normed, preferred_element_type=jnp.float32)
        + (width * columns) * normed_f
    ) / batch
    scale_diag = 2.0 * (diag - 1.0) - 2.0 * off_weight * diag
    dnorm = 2.0 * off_weight * mixed + scale_diag * other_f
    inner = jnp.mean(dnorm * normed_f, axis=0, keepdims=True)
    dpre = narrow(
        rstd * (dnorm - jnp.mean(dnorm, axis=0, keepdims=True) - normed_f * inner)
    )

    def back(slope, side, sides):
        tall = weight.shape[0] // sides
        return narrow(
            lax.dot_general(
                slope,
                weight[side * tall : (side + 1) * tall],
                (((1,), (1,)), ((), ())),
                preferred_element_type=jnp.float32,
            )
        )

    if line:
        sides = 2

        def chip_sum(slope, side):
            part = back(slope, side, sides)
            tall = part.shape[1]
            give = lax.dynamic_slice(part, ((1 - core) * share, 0), (share, tall))
            keep = lax.dynamic_slice(part, (core * share, 0), (share, tall))
            got = swap(give, "col", 1)
            return wide(keep) + wide(got)

        sums = [[None] * sides for _ in range(4)]
        for at in (3, 2, 1, 0):
            slope = lax.dynamic_slice(dpre, (starts[at], 0), (2 * share, width))
            for side in range(sides):
                sums[at][side] = chip_sum(slope, side)
        first_out = narrow(sums[3][0])
        late = narrow(sums[0][1])
        results = []
        for side in range(sides):
            far = sums[3][side]
            far_in = chip_moves(narrow(far), INWARD)
            far_across = chip_moves(narrow(far + wide(far_in)), MIDDLE)
            mid = sums[2][side]
            mid_in = chip_moves(narrow(mid), INWARD)
            mid_across = chip_moves(narrow(mid + wide(mid_in)), MIDDLE)
            close = sums[1][side] + wide(far_across)
            closed = chip_moves(narrow(close), OUTER_PAIRS)
            results.append(narrow(sums[0][side] + wide(closed) + wide(mid_across)))
        grad_hidden = jnp.concatenate(results, axis=1)
    else:
        grad_hidden = lax.psum_scatter(
            back(dpre, 0, 1), "col", scatter_dimension=0, tiled=True
        )
        first_out = late = grad_hidden

    dpre_other = swap(after(dpre, first_out), "view", 1)
    clips = list(own_blocks)
    slopes = [
        lax.dynamic_slice(dpre, (start, 0), (size, width))
        for place in places
        for start, size in place
    ]
    for at, stream in enumerate(streams):
        if at >= 2:
            stream = after(stream, pre_other)
        got = swap(stream, "view", 1)
        got = after(got, late)
        if line:
            clips += [got, swap(got, "col", 1)]
            (first, size), (second, _) = places[at]
            order = [
                jnp.where(core == 0, first, second),
                jnp.where(core == 0, second, first),
            ]
        else:
            clips.append(got)
            order, size = [0], batch
        slopes += [
            lax.dynamic_slice(dpre_other, (start, 0), (size, width)) for start in order
        ]
    clips, slopes = jnp.concatenate(clips, axis=0), jnp.concatenate(slopes, axis=0)
    grad_weight = lax.dot_general(
        clips, slopes, (((0,), (0,)), ((), ())), preferred_element_type=jnp.float32
    )
    grad_weight = grad_weight / math.sqrt(2.0 * batch)
    return (grad_hidden[None], grad_weight)


def solution(mesh):
    return jax.shard_map(
        shards,
        mesh=mesh,
        in_specs=(P("view", "col", "row"), P("row", "col")),
        out_specs=(P("view", "col", "row"), P("row", "col")),
        check_vma=False,
    )
```

profile of v0, /device:TPU:0, one launch (start us, length us, event | category | flops | bytes accessed | tf_op | source)
XLA Modules:
  0.0 238.9 jit_solution(2775096066769155070)
XLA Ops:
  3.0 5.5 %collective-permute-start.2 = (bf16[32,4096]{1,0:T(8,128)(2,1)S(1)}, bf16[32,4096]{1,0:T(8,128)(2,1)S(1)}, u32[]{:S(2)}, u32[]{:S(2)}) collective-permute-start(bf16[32,4096]{1,0:T(8,128)(2,1)S(1)} %get-tuple-element.75), channel_id=1, source_target_pairs={{0,2},{1,3},{2,0},{3,1},{4,6},{5,7},{6,4},{7,5},{8,10},{9,11},{10,... | collective-permute-start | bytes 786440 | tf_op jit(solution)/shard_map/ppermute | solution.py:20
  9.1 1.8 collective-permute-start.3
  12.2 3.4 %collective-permute-done.2 = bf16[32,4096]{1,0:T(8,128)(2,1)S(1)} collective-permute-done((bf16[32,4096]{1,0:T(8,128)(2,1)S(1)}, bf16[32,4096]{1,0:T(8,128)(2,1)S(1)}, u32[]{:S(2)}, u32[]{:S(2)}) %collective-permute-start.2) | collective-permute-done | bytes 262176 | tf_op jit(solution)/shard_map/ppermute | solution.py:20
  17.6 3.6 %collective-permute-done.3 = bf16[32,4096]{1,0:T(8,128)(2,1)S(1)} collective-permute-done((bf16[32,4096]{1,0:T(8,128)(2,1)S(1)}, bf16[32,4096]{1,0:T(8,128)(2,1)S(1)}, u32[]{:S(2)}, u32[]{:S(2)}) %collective-permute-start.3) | collective-permute-done | bytes 262176 | tf_op jit(solution)/shard_map/ppermute | solution.py:20
  22.3 4.9 %convolution_convert_fusion.2 = bf16[128,1024]{1,0:T(8,128)(2,1)S(1)} fusion(bf16[4096,1024]{1,0:T(8,128)(2,1)} %param.3, bf16[64,4096]{1,0:T(8,128)(2,1)S(1)} %get-tuple-element.59, bf16[64,4096]{1,0:T(8,128)(2,1)S(1)} %get-tuple-element.61), kind=kOutput, calls=%fused_computation.48 | convolution fusion | flops 1075970048 | bytes 9699328 | tf_op jit(solution)/shard_map/dot_general | solution.py:118
  27.1 1.6 collective-permute-start.1
  30.1 4.4 %collective-permute-done.1 = bf16[128,1024]{1,0:T(8,128)(2,1)S(1)} collective-permute-done((bf16[128,1024]{1,0:T(8,128)(2,1)S(1)}, bf16[128,1024]{1,0:T(8,128)(2,1)S(1)}, u32[]{:S(2)}, u32[]{:S(2)}) %collective-permute-start.1) | collective-permute-done | bytes 262176 | tf_op jit(solution)/shard_map/ppermute | solution.py:15
  36.4 1.6 collective-permute-start.20
  39.6 1.6 collective-permute-start.5
  41.5 1.5 collective-permute-done.20
  43.2 2.9 %collective-permute-done.5 = bf16[128,1024]{1,0:T(8,128)(2,1)S(1)} collective-permute-done((bf16[128,1024]{1,0:T(8,128)(2,1)S(1)}, bf16[128,1024]{1,0:T(8,128)(2,1)S(1)}, u32[]{:S(2)}, u32[]{:S(2)}) %collective-permute-start.5) | collective-permute-done | bytes 262176 | tf_op jit(solution)/shard_map/ppermute | solution.py:15
  48.4 1.6 collective-permute-start.11
  50.1 2.5 %collective-permute-done.21 = bf16[128,1024]{1,0:T(8,128)(2,1)S(1)} collective-permute-done((bf16[128,1024]{1,0:T(8,128)(2,1)S(1)}, bf16[128,1024]{1,0:T(8,128)(2,1)S(1)}, u32[]{:S(2)}, u32[]{:S(2)}) %collective-permute-start.21) | collective-permute-done | bytes 262176 | tf_op jit(solution)/shard_map/ppermute | solution.py:15
  52.8 1.6 convolution_convert_fusion.4
  54.4 1.5 collective-permute-start.15
  56.8 2.6 %collective-permute-done.15 = bf16[64,1024]{1,0:T(8,128)(2,1)S(1)} collective-permute-done((bf16[64,1024]{1,0:T(8,128)(2,1)S(1)}, bf16[64,1024]{1,0:T(8,128)(2,1)S(1)}, u32[]{:S(2)}, u32[]{:S(2)}) %collective-permute-start.15) | collective-permute-done | bytes 131104 | tf_op jit(solution)/shard_map/ppermute | solution.py:15
  60.8 1.6 convolution_convert_fusion.3
  62.4 1.8 copy-done.12
  65.3 3.9 %collective-permute-done.19 = bf16[64,1024]{1,0:T(8,128)(2,1)S(1)} collective-permute-done((bf16[64,1024]{1,0:T(8,128)(2,1)S(1)}, bf16[64,1024]{1,0:T(8,128)(2,1)S(1)}, u32[]{:S(2)}, u32[]{:S(2)}) %collective-permute-start.19) | collective-permute-done | bytes 131104 | tf_op jit(solution)/shard_map/ppermute | solution.py:15
  70.7 4.0 %collective-permute-done.24 = bf16[64,1024]{1,0:T(8,128)(2,1)S(1)} collective-permute-done((bf16[64,1024]{1,0:T(8,128)(2,1)S(1)}, bf16[64,1024]{1,0:T(8,128)(2,1)S(1)}, u32[]{:S(2)}, u32[]{:S(2)}) %collective-permute-start.24) | collective-permute-done | bytes 131104 | tf_op jit(solution)/shard_map/ppermute | solution.py:15
  75.3 1.5 fusion.47
  79.0 1.7 constant_dynamic-slice_fusion.8
  80.7 1.6 collective-permute-done.25
  83.2 4.3 %collective-permute-start.26 = (bf16[128,512]{1,0:T(8,128)(2,1)S(1)}, bf16[128,512]{1,0:T(8,128)(2,1)S(1)}, u32[]{:S(2)}, u32[]{:S(2)}) collective-permute-start(bf16[128,512]{1,0:T(8,128)(2,1)S(1)} %add_convert_fusion.10), channel_id=1, source_target_pairs={{0,2},{1,3},{2,0},{3,1},{4,6},{5,7},{6,4},{7,5},{8,10},{9,11},{10,... | collective-permute-start | bytes 393224 | tf_op jit(solution)/shard_map/ppermute | solution.py:15
  87.5 3.8 %collective-permute-done.26 = bf16[128,512]{1,0:T(8,128)(2,1)S(1)} collective-permute-done((bf16[128,512]{1,0:T(8,128)(2,1)S(1)}, bf16[128,512]{1,0:T(8,128)(2,1)S(1)}, u32[]{:S(2)}, u32[]{:S(2)}) %collective-permute-start.26) | collective-permute-done | bytes 131104 | tf_op jit(solution)/shard_map/ppermute | solution.py:15
  91.4 1.7 collective-permute-start.27
  93.1 7.0 %collective-permute-done.27 = bf16[128,512]{1,0:T(8,128)(2,1)S(1)} collective-permute-done((bf16[128,512]{1,0:T(8,128)(2,1)S(1)}, bf16[128,512]{1,0:T(8,128)(2,1)S(1)}, u32[]{:S(2)}, u32[]{:S(2)}) %collective-permute-start.27) | collective-permute-done | bytes 131104 | tf_op jit(solution)/shard_map/ppermute | solution.py:15
  101.2 4.0 %collective-permute-done.28 = bf16[128,512]{1,0:T(8,128)(2,1)S(1)} collective-permute-done((bf16[128,512]{1,0:T(8,128)(2,1)S(1)}, bf16[128,512]{1,0:T(8,128)(2,1)S(1)}, u32[]{:S(2)}, u32[]{:S(2)}) %collective-permute-start.28) | collective-permute-done | bytes 131104 | tf_op jit(solution)/shard_map/ppermute | solution.py:15
  111.1 4.1 %fusion.36 = bf16[128,2048]{1,0:T(8,128)(2,1)S(1)} fusion(bf16[4096,1024]{1,0:T(8,128)(2,1)} %param.3, bf16[512,1024]{1,0:T(8,128)(2,1)S(1)} %fusion.51, s32[]{:T(128)S(6)} %select_n.266), kind=kOutput, calls=%fused_computation.32 | convolution fusion | flops 537133056 | bytes 4980740 | tf_op jit(solution)/shard_map/dot_general | solution.py:184
  116.8 1.5 fusion.27
  118.3 1.5 fusion.24
  119.8 1.5 fusion.30
  121.4 1.5 fusion.33
  122.9 1.5 fusion.21
  131.3 6.1 %collective-permute-done.42 = bf16[64,2048]{1,0:T(8,128)(2,1)S(1)} collective-permute-done((bf16[64,2048]{1,0:T(8,128)(2,1)S(1)}, bf16[64,2048]{1,0:T(8,128)(2,1)S(1)}, u32[]{:S(2)}, u32[]{:S(2)}) %collective-permute-start.42) | collective-permute-done | bytes 262176 | tf_op jit(solution)/shard_map/ppermute | solution.py:20
  137.4 4.4 %collective-permute-start.46 = (bf16[64,2048]{1,0:T(8,128)(2,1)S(1)}, bf16[64,2048]{1,0:T(8,128)(2,1)S(1)}, u32[]{:S(2)}, u32[]{:S(2)}) collective-permute-start(bf16[64,2048]{1,0:T(8,128)(2,1)S(1)} %fusion.79), channel_id=1, source_target_pairs={{0,2},{1,3},{6,4},{7,5},{8,10},{9,11},{14,12},{15,13},{16,18},{17,... | collective-permute-start | bytes 786440 | tf_op jit(solution)/shard_map/ppermute | solution.py:20
  141.9 5.2 %collective-permute-done.46 = bf16[64,2048]{1,0:T(8,128)(2,1)S(1)} collective-permute-done((bf16[64,2048]{1,0:T(8,128)(2,1)S(1)}, bf16[64,2048]{1,0:T(8,128)(2,1)S(1)}, u32[]{:S(2)}, u32[]{:S(2)}) %collective-permute-start.46) | collective-permute-done | bytes 262176 | tf_op jit(solution)/shard_map/ppermute | solution.py:20
  147.1 4.4 %collective-permute-start.37 = (bf16[64,2048]{1,0:T(8,128)(2,1)S(1)}, bf16[64,2048]{1,0:T(8,128)(2,1)S(1)}, u32[]{:S(2)}, u32[]{:S(2)}) collective-permute-start(bf16[64,2048]{1,0:T(8,128)(2,1)S(1)} %fusion.76), channel_id=1, source_target_pairs={{0,2},{1,3},{6,4},{7,5},{8,10},{9,11},{14,12},{15,13},{16,18},{17,... | collective-permute-start | bytes 786440 | tf_op jit(solution)/shard_map/ppermute | solution.py:20
  151.6 4.4 %collective-permute-done.37 = bf16[64,2048]{1,0:T(8,128)(2,1)S(1)} collective-permute-done((bf16[64,2048]{1,0:T(8,128)(2,1)S(1)}, bf16[64,2048]{1,0:T(8,128)(2,1)S(1)}, u32[]{:S(2)}, u32[]{:S(2)}) %collective-permute-start.37) | collective-permute-done | bytes 262176 | tf_op jit(solution)/shard_map/ppermute | solution.py:20
  156.0 4.4 %collective-permute-start.33 = (bf16[64,2048]{1,0:T(8,128)(2,1)S(1)}, bf16[64,2048]{1,0:T(8,128)(2,1)S(1)}, u32[]{:S(2)}, u32[]{:S(2)}) collective-permute-start(bf16[64,2048]{1,0:T(8,128)(2,1)S(1)} %fusion.75), channel_id=1, source_target_pairs={{0,2},{1,3},{6,4},{7,5},{8,10},{9,11},{14,12},{15,13},{16,18},{17,... | collective-permute-start | bytes 786440 | tf_op jit(solution)/shard_map/ppermute | solution.py:20
  160.5 3.7 %collective-permute-done.33 = bf16[64,2048]{1,0:T(8,128)(2,1)S(1)} collective-permute-done((bf16[64,2048]{1,0:T(8,128)(2,1)S(1)}, bf16[64,2048]{1,0:T(8,128)(2,1)S(1)}, u32[]{:S(2)}, u32[]{:S(2)}) %collective-permute-start.33) | collective-permute-done | bytes 262176 | tf_op jit(solution)/shard_map/ppermute | solution.py:20
  167.3 16.2 %collective-permute-start.44 = (bf16[64,2048]{1,0:T(8,128)(2,1)S(1)}, bf16[64,2048]{1,0:T(8,128)(2,1)S(1)}, u32[]{:S(2)}, u32[]{:S(2)}) collective-permute-start(bf16[64,2048]{1,0:T(8,128)(2,1)S(1)} %add_convert_fusion.2), channel_id=1, source_target_pairs={{0,2},{1,3},{2,0},{3,1},{4,6},{5,7},{6,4},{7,5},{8,10},{9,11},{10,... | collective-permute-start | bytes 786440 | tf_op jit(solution)/shard_map/ppermute | solution.py:20
  185.7 2.1 collective-permute-done.44
  190.2 2.7 %collective-permute-done.54 = bf16[32,4096]{1,0:T(8,128)(2,1)S(1)} collective-permute-done((bf16[32,4096]{1,0:T(8,128)(2,1)S(1)}, bf16[32,4096]{1,0:T(8,128)(2,1)S(1)}, u32[]{:S(2)}, u32[]{:S(2)}) %collective-permute-start.54) | collective-permute-done | bytes 262176 | tf_op jit(solution)/shard_map/ppermute | solution.py:15
  193.8 4.7 %collective-permute-done.56 = bf16[32,4096]{1,0:T(8,128)(2,1)S(1)} collective-permute-done((bf16[32,4096]{1,0:T(8,128)(2,1)S(1)}, bf16[32,4096]{1,0:T(8,128)(2,1)S(1)}, u32[]{:S(2)}, u32[]{:S(2)}) %collective-permute-start.56) | collective-permute-done | bytes 262176 | tf_op jit(solution)/shard_map/ppermute | solution.py:15
  199.6 10.1 %collective-permute-done.52 = bf16[64,4096]{1,0:T(8,128)(2,1)S(1)} collective-permute-done((bf16[64,4096]{1,0:T(8,128)(2,1)S(1)}, bf16[64,4096]{1,0:T(8,128)(2,1)S(1)}, u32[]{:S(2)}, u32[]{:S(2)}) %collective-permute-start.52) | collective-permute-done | bytes 524320 | tf_op jit(solution)/shard_map/ppermute | solution.py:15
  211.7 13.4 %collective-permute-done.58 = bf16[512,1024]{1,0:T(8,128)(2,1)S(1)} collective-permute-done((bf16[512,1024]{1,0:T(8,128)(2,1)S(1)}, bf16[512,1024]{1,0:T(8,128)(2,1)S(1)}, u32[]{:S(2)}, u32[]{:S(2)}) %collective-permute-start.58) | collective-permute-done | bytes 1048608 | tf_op jit(solution)/shard_map/ppermute | solution.py:15
  227.2 11.6 %convolution_multiply_fusion = f32[4096,1024]{1,0:T(8,128)} fusion(bf16[1024,4096]{1,0:T(8,128)(2,1)S(1)} %constant_dynamic-update-slice_fusion.2, bf16[1024,1024]{1,0:T(8,128)(2,1)S(1)} %constant_dynamic-update-slice_fusion.22), kind=kOutput, calls=%fused_computation | convolution fusion | flops 8594128896 | bytes 27262976 | tf_op jit(solution)/shard_map/dot_general | solution.py:254
  (244 shorter events, 52.3 us)
Async XLA Ops:
  1.8 20.1 %collective-permute-start = (bf16[64,4096]{1,0:T(8,128)(2,1)S(1)}, bf16[64,4096]{1,0:T(8,128)(2,1)S(1)}, u32[]{:S(2)}, u32[]{:S(2)}) collective-permute-start(bf16[64,4096]{1,0:T(8,128)(2,1)S(1)} %pad_maximum_fusion), channel_id=1, source_target_pairs={{0,1},{1,0},{2,3},{3,2},{4,5},{5,4},{6,7},{7,6},{8,9},{9,8},{10,11... | collective-permute-start | bytes 1572872 | tf_op jit(solution)/shard_map/ppermute | solution.py:15
  2.3 8.6 %collective-permute-start.6 = (bf16[32,4096]{1,0:T(8,128)(2,1)S(1)}, bf16[32,4096]{1,0:T(8,128)(2,1)S(1)}, u32[]{:S(2)}, u32[]{:S(2)}) collective-permute-start(bf16[32,4096]{1,0:T(8,128)(2,1)S(1)} %get-tuple-element.75), channel_id=1, source_target_pairs={{2,4},{3,5},{4,2},{5,3},{10,12},{11,13},{12,10},{13,11},{18,20},{1... | collective-permute-start | bytes 786440 | tf_op jit(solution)/shard_map/ppermute | solution.py:20
  3.0 12.6 %collective-permute-start.2 = (bf16[32,4096]{1,0:T(8,128)(2,1)S(1)}, bf16[32,4096]{1,0:T(8,128)(2,1)S(1)}, u32[]{:S(2)}, u32[]{:S(2)}) collective-permute-start(bf16[32,4096]{1,0:T(8,128)(2,1)S(1)} %get-tuple-element.75), channel_id=1, source_target_pairs={{0,2},{1,3},{2,0},{3,1},{4,6},{5,7},{6,4},{7,5},{8,10},{9,11},{10,... | collective-permute-start | bytes 786440 | tf_op jit(solution)/shard_map/ppermute | solution.py:20
  8.4 7.8 %collective-permute-start.8 = (bf16[32,4096]{1,0:T(8,128)(2,1)S(1)}, bf16[32,4096]{1,0:T(8,128)(2,1)S(1)}, u32[]{:S(2)}, u32[]{:S(2)}) collective-permute-start(bf16[32,4096]{1,0:T(8,128)(2,1)S(1)} %get-tuple-element.76), channel_id=1, source_target_pairs={{2,4},{3,5},{4,2},{5,3},{10,12},{11,13},{12,10},{13,11},{18,20},{1... | collective-permute-start | bytes 786440 | tf_op jit(solution)/shard_map/ppermute | solution.py:20
  9.1 12.1 %collective-permute-start.3 = (bf16[32,4096]{1,0:T(8,128)(2,1)S(1)}, bf16[32,4096]{1,0:T(8,128)(2,1)S(1)}, u32[]{:S(2)}, u32[]{:S(2)}) collective-permute-start(bf16[32,4096]{1,0:T(8,128)(2,1)S(1)} %get-tuple-element.76), channel_id=1, source_target_pairs={{0,2},{1,3},{2,0},{3,1},{4,6},{5,7},{6,4},{7,5},{8,10},{9,11},{10,... | collective-permute-start | bytes 786440 | tf_op jit(solution)/shard_map/ppermute | solution.py:20
  10.9 30.3 %collective-permute-start.7 = (bf16[32,4096]{1,0:T(8,128)(2,1)S(1)}, bf16[32,4096]{1,0:T(8,128)(2,1)S(1)}, u32[]{:S(2)}, u32[]{:S(2)}) collective-permute-start(bf16[32,4096]{1,0:T(8,128)(2,1)S(1)} %collective-permute-done.6), channel_id=1, source_target_pairs={{2,0},{3,1},{4,6},{5,7},{10,8},{11,9},{12,14},{13,15},{18,16},{19,... | collective-permute-start | bytes 786440 | tf_op jit(solution)/shard_map/ppermute | solution.py:20
  15.6 13.1 %collective-permute-start.12 = (bf16[32,4096]{1,0:T(8,128)(2,1)S(1)}, bf16[32,4096]{1,0:T(8,128)(2,1)S(1)}, u32[]{:S(2)}, u32[]{:S(2)}) collective-permute-start(bf16[32,4096]{1,0:T(8,128)(2,1)S(1)} %collective-permute-done.2), channel_id=1, source_target_pairs={{2,4},{3,5},{4,2},{5,3},{10,12},{11,13},{12,10},{13,11},{18,20},{1... | collective-permute-start | bytes 786440 | tf_op jit(solution)/shard_map/ppermute | solution.py:20
  16.3 23.3 %collective-permute-start.9 = (bf16[32,4096]{1,0:T(8,128)(2,1)S(1)}, bf16[32,4096]{1,0:T(8,128)(2,1)S(1)}, u32[]{:S(2)}, u32[]{:S(2)}) collective-permute-start(bf16[32,4096]{1,0:T(8,128)(2,1)S(1)} %collective-permute-done.8), channel_id=1, source_target_pairs={{2,0},{3,1},{4,6},{5,7},{10,8},{11,9},{12,14},{13,15},{18,16},{19,... | collective-permute-start | bytes 786440 | tf_op jit(solution)/shard_map/ppermute | solution.py:20
  21.2 7.6 %collective-permute-start.16 = (bf16[32,4096]{1,0:T(8,128)(2,1)S(1)}, bf16[32,4096]{1,0:T(8,128)(2,1)S(1)}, u32[]{:S(2)}, u32[]{:S(2)}) collective-permute-start(bf16[32,4096]{1,0:T(8,128)(2,1)S(1)} %collective-permute-done.3), channel_id=1, source_target_pairs={{2,4},{3,5},{4,2},{5,3},{10,12},{11,13},{12,10},{13,11},{18,20},{1... | collective-permute-start | bytes 786440 | tf_op jit(solution)/shard_map/ppermute | solution.py:20
  27.1 7.4 %collective-permute-start.1 = (bf16[128,1024]{1,0:T(8,128)(2,1)S(1)}, bf16[128,1024]{1,0:T(8,128)(2,1)S(1)}, u32[]{:S(2)}, u32[]{:S(2)}) collective-permute-start(bf16[128,1024]{1,0:T(8,128)(2,1)S(1)} %convolution_convert_fusion.2), channel_id=1, source_target_pairs={{0,8},{8,0},{1,9},{9,1},{2,10},{10,2},{3,11},{11,3},{4,12},{12,4},... | collective-permute-start | bytes 786440 | tf_op jit(solution)/shard_map/ppermute | solution.py:15
  28.7 7.7 %collective-permute-start.4 = (bf16[64,4096]{1,0:T(8,128)(2,1)S(1)}, bf16[64,4096]{1,0:T(8,128)(2,1)S(1)}, u32[]{:S(2)}, u32[]{:S(2)}) collective-permute-start(bf16[64,4096]{1,0:T(8,128)(2,1)S(1)} %constant_dynamic-update-slice_fusion), channel_id=1, source_target_pairs={{0,1},{1,0},{2,3},{3,2},{4,5},{5,4},{6,7},{7,6},{8,9},{9,8},{10,11... | collective-permute-start | bytes 1572872 | tf_op jit(solution)/shard_map/ppermute | solution.py:15
  28.8 21.1 %collective-permute-start.13 = (bf16[32,4096]{1,0:T(8,128)(2,1)S(1)}, bf16[32,4096]{1,0:T(8,128)(2,1)S(1)}, u32[]{:S(2)}, u32[]{:S(2)}) collective-permute-start(bf16[32,4096]{1,0:T(8,128)(2,1)S(1)} %collective-permute-done.12), channel_id=1, source_target_pairs={{2,0},{3,1},{4,6},{5,7},{10,8},{11,9},{12,14},{13,15},{18,16},{19,... | collective-permute-start | bytes 786440 | tf_op jit(solution)/shard_map/ppermute | solution.py:20
  34.5 21.4 %collective-permute-start.17 = (bf16[32,4096]{1,0:T(8,128)(2,1)S(1)}, bf16[32,4096]{1,0:T(8,128)(2,1)S(1)}, u32[]{:S(2)}, u32[]{:S(2)}) collective-permute-start(bf16[32,4096]{1,0:T(8,128)(2,1)S(1)} %collective-permute-done.16), channel_id=1, source_target_pairs={{2,0},{3,1},{4,6},{5,7},{10,8},{11,9},{12,14},{13,15},{18,16},{19,... | collective-permute-start | bytes 786440 | tf_op jit(solution)/shard_map/ppermute | solution.py:20
  36.4 6.6 %collective-permute-start.20 = (bf16[128,1024]{1,0:T(8,128)(2,1)S(1)}, bf16[128,1024]{1,0:T(8,128)(2,1)S(1)}, u32[]{:S(2)}, u32[]{:S(2)}) collective-permute-start(bf16[128,1024]{1,0:T(8,128)(2,1)S(1)} %get-tuple-element.74), channel_id=1, source_target_pairs={{0,16},{16,0},{1,17},{17,1},{2,18},{18,2},{3,19},{19,3},{4,20},{20... | collective-permute-start | bytes 786440 | tf_op jit(solution)/shard_map/ppermute | solution.py:15
  39.6 6.4 %collective-permute-start.5 = (bf16[128,1024]{1,0:T(8,128)(2,1)S(1)}, bf16[128,1024]{1,0:T(8,128)(2,1)S(1)}, u32[]{:S(2)}, u32[]{:S(2)}) collective-permute-start(bf16[128,1024]{1,0:T(8,128)(2,1)S(1)} %convolution_convert_fusion.1), channel_id=1, source_target_pairs={{0,8},{8,0},{1,9},{9,1},{2,10},{10,2},{3,11},{11,3},{4,12},{12,4},... | collective-permute-start | bytes 786440 | tf_op jit(solution)/shard_map/ppermute | solution.py:15
  41.4 5.4 %collective-permute-start.10 = (bf16[64,4096]{1,0:T(8,128)(2,1)S(1)}, bf16[64,4096]{1,0:T(8,128)(2,1)S(1)}, u32[]{:S(2)}, u32[]{:S(2)}) collective-permute-start(bf16[64,4096]{1,0:T(8,128)(2,1)S(1)} %pad_maximum_fusion.1), channel_id=1, source_target_pairs={{0,1},{1,0},{2,3},{3,2},{4,5},{5,4},{6,7},{7,6},{8,9},{9,8},{10,11... | collective-permute-start | bytes 1572872 | tf_op jit(solution)/shard_map/ppermute | solution.py:15
  46.1 6.4 %collective-permute-start.21 = (bf16[128,1024]{1,0:T(8,128)(2,1)S(1)}, bf16[128,1024]{1,0:T(8,128)(2,1)S(1)}, u32[]{:S(2)}, u32[]{:S(2)}) collective-permute-start(bf16[128,1024]{1,0:T(8,128)(2,1)S(1)} %get-tuple-element.72), channel_id=1, source_target_pairs={{0,16},{16,0},{1,17},{17,1},{2,18},{18,2},{3,19},{19,3},{4,20},{20... | collective-permute-start | bytes 786440 | tf_op jit(solution)/shard_map/ppermute | solution.py:15
  48.4 7.6 %collective-permute-start.11 = (bf16[128,1024]{1,0:T(8,128)(2,1)S(1)}, bf16[128,1024]{1,0:T(8,128)(2,1)S(1)}, u32[]{:S(2)}, u32[]{:S(2)}) collective-permute-start(bf16[128,1024]{1,0:T(8,128)(2,1)S(1)} %convolution_convert_fusion), channel_id=1, source_target_pairs={{0,8},{8,0},{1,9},{9,1},{2,10},{10,2},{3,11},{11,3},{4,12},{12,4},... | collective-permute-start | bytes 786440 | tf_op jit(solution)/shard_map/ppermute | solution.py:15
  54.4 5.0 %collective-permute-start.15 = (bf16[64,1024]{1,0:T(8,128)(2,1)S(1)}, bf16[64,1024]{1,0:T(8,128)(2,1)S(1)}, u32[]{:S(2)}, u32[]{:S(2)}) collective-permute-start(bf16[64,1024]{1,0:T(8,128)(2,1)S(1)} %convolution_convert_fusion.4), channel_id=1, source_target_pairs={{0,8},{8,0},{1,9},{9,1},{2,10},{10,2},{3,11},{11,3},{4,12},{12,4},... | collective-permute-start | bytes 393224 | tf_op jit(solution)/shard_map/ppermute | solution.py:15
  56.0 9.1 %collective-permute-start.22 = (bf16[128,1024]{1,0:T(8,128)(2,1)S(1)}, bf16[128,1024]{1,0:T(8,128)(2,1)S(1)}, u32[]{:S(2)}, u32[]{:S(2)}) collective-permute-start(bf16[128,1024]{1,0:T(8,128)(2,1)S(1)} %get-tuple-element.70), channel_id=1, source_target_pairs={{0,16},{16,0},{1,17},{17,1},{2,18},{18,2},{3,19},{19,3},{4,20},{20... | collective-permute-start | bytes 786440 | tf_op jit(solution)/shard_map/ppermute | solution.py:15
  56.7 3.9 %collective-permute-start.18 = (bf16[32,4096]{1,0:T(8,128)(2,1)S(1)}, bf16[32,4096]{1,0:T(8,128)(2,1)S(1)}, u32[]{:S(2)}, u32[]{:S(2)}) collective-permute-start(bf16[32,4096]{1,0:T(8,128)(2,1)S(1)} %add.297), channel_id=1, source_target_pairs={{0,1},{1,0},{2,3},{3,2},{4,5},{5,4},{6,7},{7,6},{8,9},{9,8},{10,11... | collective-permute-start | bytes 786440 | tf_op jit(solution)/shard_map/ppermute | solution.py:15
  59.5 5.8 %collective-permute-start.23 = (bf16[64,1024]{1,0:T(8,128)(2,1)S(1)}, bf16[64,1024]{1,0:T(8,128)(2,1)S(1)}, u32[]{:S(2)}, u32[]{:S(2)}) collective-permute-start(bf16[64,1024]{1,0:T(8,128)(2,1)S(1)} %get-tuple-element.86), channel_id=1, source_target_pairs={{0,16},{16,0},{1,17},{17,1},{2,18},{18,2},{3,19},{19,3},{4,20},{20... | collective-permute-start | bytes 393224 | tf_op jit(solution)/shard_map/ppermute | solution.py:15
  64.2 5.0 %collective-permute-start.19 = (bf16[64,1024]{1,0:T(8,128)(2,1)S(1)}, bf16[64,1024]{1,0:T(8,128)(2,1)S(1)}, u32[]{:S(2)}, u32[]{:S(2)}) collective-permute-start(bf16[64,1024]{1,0:T(8,128)(2,1)S(1)} %convolution_convert_fusion.3), channel_id=1, source_target_pairs={{0,8},{8,0},{1,9},{9,1},{2,10},{10,2},{3,11},{11,3},{4,12},{12,4},... | collective-permute-start | bytes 393224 | tf_op jit(solution)/shard_map/ppermute | solution.py:15
  69.7 5.0 %collective-permute-start.24 = (bf16[64,1024]{1,0:T(8,128)(2,1)S(1)}, bf16[64,1024]{1,0:T(8,128)(2,1)S(1)}, u32[]{:S(2)}, u32[]{:S(2)}) collective-permute-start(bf16[64,1024]{1,0:T(8,128)(2,1)S(1)} %get-tuple-element.84), channel_id=1, source_target_pairs={{0,16},{16,0},{1,17},{17,1},{2,18},{18,2},{3,19},{19,3},{4,20},{20... | collective-permute-start | bytes 393224 | tf_op jit(solution)/shard_map/ppermute | solution.py:15
  83.2 8.1 %collective-permute-start.26 = (bf16[128,512]{1,0:T(8,128)(2,1)S(1)}, bf16[128,512]{1,0:T(8,128)(2,1)S(1)}, u32[]{:S(2)}, u32[]{:S(2)}) collective-permute-start(bf16[128,512]{1,0:T(8,128)(2,1)S(1)} %add_convert_fusion.10), channel_id=1, source_target_pairs={{0,2},{1,3},{2,0},{3,1},{4,6},{5,7},{6,4},{7,5},{8,10},{9,11},{10,... | collective-permute-start | bytes 393224 | tf_op jit(solution)/shard_map/ppermute | solution.py:15
  91.4 8.7 %collective-permute-start.27 = (bf16[128,512]{1,0:T(8,128)(2,1)S(1)}, bf16[128,512]{1,0:T(8,128)(2,1)S(1)}, u32[]{:S(2)}, u32[]{:S(2)}) collective-permute-start(bf16[128,512]{1,0:T(8,128)(2,1)S(1)} %add_convert_fusion.9), channel_id=1, source_target_pairs={{0,4},{1,5},{2,6},{3,7},{4,0},{5,1},{6,2},{7,3},{8,12},{9,13},{10,... | collective-permute-start | bytes 393224 | tf_op jit(solution)/shard_map/ppermute | solution.py:15
  100.1 5.0 %collective-permute-start.28 = (bf16[128,512]{1,0:T(8,128)(2,1)S(1)}, bf16[128,512]{1,0:T(8,128)(2,1)S(1)}, u32[]{:S(2)}, u32[]{:S(2)}) collective-permute-start(bf16[128,512]{1,0:T(8,128)(2,1)S(1)} %add_convert_fusion.8), channel_id=1, source_target_pairs={{0,8},{8,0},{1,9},{9,1},{2,10},{10,2},{3,11},{11,3},{4,12},{12,4},... | collective-permute-start | bytes 393224 | tf_op jit(solution)/shard_map/ppermute | solution.py:15
  106.0 83.0 %collective-permute-start.48 = (bf16[64,4096]{1,0:T(8,128)(2,1)S(1)}, bf16[64,4096]{1,0:T(8,128)(2,1)}, u32[]{:S(2)}, u32[]{:S(2)}) collective-permute-start(bf16[64,4096]{1,0:T(8,128)(2,1)S(1)} %copy-done.8), channel_id=1, source_target_pairs={{0,16},{16,0},{1,17},{17,1},{2,18},{18,2},{3,19},{19,3},{4,20},{20... | collective-permute-start | bytes 1572872 | tf_op jit(solution)/shard_map/ppermute | solution.py:15
  107.0 82.1 %collective-permute-start.50 = (bf16[64,4096]{1,0:T(8,128)(2,1)S(1)}, bf16[64,4096]{1,0:T(8,128)(2,1)S(1)}, u32[]{:S(2)}, u32[]{:S(2)}) collective-permute-start(bf16[64,4096]{1,0:T(8,128)(2,1)S(1)} %copy-done.2), channel_id=1, source_target_pairs={{0,16},{16,0},{1,17},{17,1},{2,18},{18,2},{3,19},{19,3},{4,20},{20... | collective-permute-start | bytes 1572872 | tf_op jit(solution)/shard_map/ppermute | solution.py:15
  128.6 55.0 %collective-permute-start.39 = (bf16[64,2048]{1,0:T(8,128)(2,1)S(1)}, bf16[64,2048]{1,0:T(8,128)(2,1)S(1)}, u32[]{:S(2)}, u32[]{:S(2)}) collective-permute-start(bf16[64,2048]{1,0:T(8,128)(2,1)S(1)} %constant_dynamic-slice_fusion.3), channel_id=1, source_target_pairs={{0,1},{1,0},{2,3},{3,2},{4,5},{5,4},{6,7},{7,6},{8,9},{9,8},{10,11... | collective-permute-start | bytes 786440 | tf_op jit(solution)/shard_map/ppermute | solution.py:15
  129.1 36.0 %collective-permute-start.40 = (bf16[64,2048]{1,0:T(8,128)(2,1)S(1)}, bf16[64,2048]{1,0:T(8,128)(2,1)S(1)}, u32[]{:S(2)}, u32[]{:S(2)}) collective-permute-start(bf16[64,2048]{1,0:T(8,128)(2,1)S(1)} %constant_dynamic-slice_fusion.2), channel_id=1, source_target_pairs={{0,1},{1,0},{2,3},{3,2},{4,5},{5,4},{6,7},{7,6},{8,9},{9,8},{10,11... | collective-permute-start | bytes 786440 | tf_op jit(solution)/shard_map/ppermute | solution.py:15
  129.9 7.5 %collective-permute-start.42 = (bf16[64,2048]{1,0:T(8,128)(2,1)S(1)}, bf16[64,2048]{1,0:T(8,128)(2,1)S(1)}, u32[]{:S(2)}, u32[]{:S(2)}) collective-permute-start(bf16[64,2048]{1,0:T(8,128)(2,1)S(1)} %fusion.78), channel_id=1, source_target_pairs={{0,2},{1,3},{6,4},{7,5},{8,10},{9,11},{14,12},{15,13},{16,18},{17,... | collective-permute-start | bytes 786440 | tf_op jit(solution)/shard_map/ppermute | solution.py:20
  137.4 9.7 %collective-permute-start.46 = (bf16[64,2048]{1,0:T(8,128)(2,1)S(1)}, bf16[64,2048]{1,0:T(8,128)(2,1)S(1)}, u32[]{:S(2)}, u32[]{:S(2)}) collective-permute-start(bf16[64,2048]{1,0:T(8,128)(2,1)S(1)} %fusion.79), channel_id=1, source_target_pairs={{0,2},{1,3},{6,4},{7,5},{8,10},{9,11},{14,12},{15,13},{16,18},{17,... | collective-permute-start | bytes 786440 | tf_op jit(solution)/shard_map/ppermute | solution.py:20
  147.1 8.9 %collective-permute-start.37 = (bf16[64,2048]{1,0:T(8,128)(2,1)S(1)}, bf16[64,2048]{1,0:T(8,128)(2,1)S(1)}, u32[]{:S(2)}, u32[]{:S(2)}) collective-permute-start(bf16[64,2048]{1,0:T(8,128)(2,1)S(1)} %fusion.76), channel_id=1, source_target_pairs={{0,2},{1,3},{6,4},{7,5},{8,10},{9,11},{14,12},{15,13},{16,18},{17,... | collective-permute-start | bytes 786440 | tf_op jit(solution)/shard_map/ppermute | solution.py:20
  156.0 8.3 %collective-permute-start.33 = (bf16[64,2048]{1,0:T(8,128)(2,1)S(1)}, bf16[64,2048]{1,0:T(8,128)(2,1)S(1)}, u32[]{:S(2)}, u32[]{:S(2)}) collective-permute-start(bf16[64,2048]{1,0:T(8,128)(2,1)S(1)} %fusion.75), channel_id=1, source_target_pairs={{0,2},{1,3},{6,4},{7,5},{8,10},{9,11},{14,12},{15,13},{16,18},{17,... | collective-permute-start | bytes 786440 | tf_op jit(solution)/shard_map/ppermute | solution.py:20
  166.6 18.0 %collective-permute-start.47 = (bf16[64,2048]{1,0:T(8,128)(2,1)S(1)}, bf16[64,2048]{1,0:T(8,128)(2,1)S(1)}, u32[]{:S(2)}, u32[]{:S(2)}) collective-permute-start(bf16[64,2048]{1,0:T(8,128)(2,1)S(1)} %add_convert_fusion.1), channel_id=1, source_target_pairs={{2,4},{3,5},{4,2},{5,3},{10,12},{11,13},{12,10},{13,11},{18,20},{1... | collective-permute-start | bytes 786440 | tf_op jit(solution)/shard_map/ppermute | solution.py:20
  167.3 20.5 %collective-permute-start.44 = (bf16[64,2048]{1,0:T(8,128)(2,1)S(1)}, bf16[64,2048]{1,0:T(8,128)(2,1)S(1)}, u32[]{:S(2)}, u32[]{:S(2)}) collective-permute-start(bf16[64,2048]{1,0:T(8,128)(2,1)S(1)} %add_convert_fusion.2), channel_id=1, source_target_pairs={{0,2},{1,3},{2,0},{3,1},{4,6},{5,7},{6,4},{7,5},{8,10},{9,11},{10,... | collective-permute-start | bytes 786440 | tf_op jit(solution)/shard_map/ppermute | solution.py:20
  183.6 9.2 %collective-permute-start.54 = (bf16[32,4096]{1,0:T(8,128)(2,1)S(1)}, bf16[32,4096]{1,0:T(8,128)(2,1)S(1)}, u32[]{:S(2)}, u32[]{:S(2)}) collective-permute-start(bf16[32,4096]{1,0:T(8,128)(2,1)S(1)} %add.292), channel_id=1, source_target_pairs={{0,16},{16,0},{1,17},{17,1},{2,18},{18,2},{3,19},{19,3},{4,20},{20... | collective-permute-start | bytes 786440 | tf_op jit(solution)/shard_map/ppermute | solution.py:15
  184.7 13.8 %collective-permute-start.56 = (bf16[32,4096]{1,0:T(8,128)(2,1)S(1)}, bf16[32,4096]{1,0:T(8,128)(2,1)S(1)}, u32[]{:S(2)}, u32[]{:S(2)}) collective-permute-start(bf16[32,4096]{1,0:T(8,128)(2,1)S(1)} %copy-done.4), channel_id=1, source_target_pairs={{0,16},{16,0},{1,17},{17,1},{2,18},{18,2},{3,19},{19,3},{4,20},{20... | collective-permute-start | bytes 786440 | tf_op jit(solution)/shard_map/ppermute | solution.py:15
  187.9 21.9 %collective-permute-start.52 = (bf16[64,4096]{1,0:T(8,128)(2,1)S(1)}, bf16[64,4096]{1,0:T(8,128)(2,1)S(1)}, u32[]{:S(2)}, u32[]{:S(2)}) collective-permute-start(bf16[64,4096]{1,0:T(8,128)(2,1)S(1)} %copy-done.10), channel_id=1, source_target_pairs={{0,16},{16,0},{1,17},{17,1},{2,18},{18,2},{3,19},{19,3},{4,20},{20... | collective-permute-start | bytes 1572872 | tf_op jit(solution)/shard_map/ppermute | solution.py:15
  189.0 20.8 %collective-permute-start.30 = (bf16[64,2048]{1,0:T(8,128)(2,1)S(1)}, bf16[64,2048]{1,0:T(8,128)(2,1)S(1)}, u32[]{:S(2)}, u32[]{:S(2)}) collective-permute-start(bf16[64,2048]{1,0:T(8,128)(2,1)S(1)} %constant_dynamic-slice_fusion.7), channel_id=1, source_target_pairs={{0,1},{1,0},{2,3},{3,2},{4,5},{5,4},{6,7},{7,6},{8,9},{9,8},{10,11... | collective-permute-start | bytes 786440 | tf_op jit(solution)/shard_map/ppermute | solution.py:15
  189.1 36.1 %collective-permute-start.58 = (bf16[512,1024]{1,0:T(8,128)(2,1)S(1)}, bf16[512,1024]{1,0:T(8,128)(2,1)S(1)}, u32[]{:S(2)}, u32[]{:S(2)}) collective-permute-start(bf16[512,1024]{1,0:T(8,128)(2,1)S(1)} %fusion.51), channel_id=1, source_target_pairs={{0,16},{16,0},{1,17},{17,1},{2,18},{18,2},{3,19},{19,3},{4,20},{20... | collective-permute-start | bytes 3145736 | tf_op jit(solution)/shard_map/ppermute | solution.py:15
  192.9 17.4 %collective-permute-start.38 = (bf16[64,2048]{1,0:T(8,128)(2,1)S(1)}, bf16[64,2048]{1,0:T(8,128)(2,1)S(1)}, u32[]{:S(2)}, u32[]{:S(2)}) collective-permute-start(bf16[64,2048]{1,0:T(8,128)(2,1)S(1)} %add_convert_fusion.5), channel_id=1, source_target_pairs={{2,4},{3,5},{4,2},{5,3},{10,12},{11,13},{12,10},{13,11},{18,20},{1... | collective-permute-start | bytes 786440 | tf_op jit(solution)/shard_map/ppermute | solution.py:20
  198.5 11.8 %collective-permute-start.35 = (bf16[64,2048]{1,0:T(8,128)(2,1)S(1)}, bf16[64,2048]{1,0:T(8,128)(2,1)S(1)}, u32[]{:S(2)}, u32[]{:S(2)}) collective-permute-start(bf16[64,2048]{1,0:T(8,128)(2,1)S(1)} %add_convert_fusion.6), channel_id=1, source_target_pairs={{0,2},{1,3},{2,0},{3,1},{4,6},{5,7},{6,4},{7,5},{8,10},{9,11},{10,... | collective-permute-start | bytes 786440 | tf_op jit(solution)/shard_map/ppermute | solution.py:20
  209.7 15.7 %collective-permute-start.49 = (bf16[64,4096]{1,0:T(8,128)(2,1)}, bf16[64,4096]{1,0:T(8,128)(2,1)S(1)}, u32[]{:S(2)}, u32[]{:S(2)}) collective-permute-start(bf16[64,4096]{1,0:T(8,128)(2,1)} %collective-permute-done.48), channel_id=1, source_target_pairs={{0,1},{1,0},{2,3},{3,2},{4,5},{5,4},{6,7},{7,6},{8,9},{9,8},{10,11... | collective-permute-start | bytes 1572872 | tf_op jit(solution)/shard_map/ppermute | solution.py:15
  209.7 17.4 %collective-permute-start.55 = (bf16[32,4096]{1,0:T(8,128)(2,1)S(1)}, bf16[32,4096]{1,0:T(8,128)(2,1)S(1)}, u32[]{:S(2)}, u32[]{:S(2)}) collective-permute-start(bf16[32,4096]{1,0:T(8,128)(2,1)S(1)} %collective-permute-done.54), channel_id=1, source_target_pairs={{0,1},{1,0},{2,3},{3,2},{4,5},{5,4},{6,7},{7,6},{8,9},{9,8},{10,11... | collective-permute-start | bytes 786440 | tf_op jit(solution)/shard_map/ppermute | solution.py:15
  210.2 17.0 %collective-permute-start.57 = (bf16[32,4096]{1,0:T(8,128)(2,1)S(1)}, bf16[32,4096]{1,0:T(8,128)(2,1)S(1)}, u32[]{:S(2)}, u32[]{:S(2)}) collective-permute-start(bf16[32,4096]{1,0:T(8,128)(2,1)S(1)} %collective-permute-done.56), channel_id=1, source_target_pairs={{0,1},{1,0},{2,3},{3,2},{4,5},{5,4},{6,7},{7,6},{8,9},{9,8},{10,11... | collective-permute-start | bytes 786440 | tf_op jit(solution)/shard_map/ppermute | solution.py:15
  210.3 15.2 %collective-permute-start.51 = (bf16[64,4096]{1,0:T(8,128)(2,1)S(1)}, bf16[64,4096]{1,0:T(8,128)(2,1)S(1)}, u32[]{:S(2)}, u32[]{:S(2)}) collective-permute-start(bf16[64,4096]{1,0:T(8,128)(2,1)S(1)} %collective-permute-done.50), channel_id=1, source_target_pairs={{0,1},{1,0},{2,3},{3,2},{4,5},{5,4},{6,7},{7,6},{8,9},{9,8},{10,11... | collective-permute-start | bytes 1572872 | tf_op jit(solution)/shard_map/ppermute | solution.py:15
  (30 other events, 442.0 us)
where the time goes:
time: 239 us
  waiting for transfers between devices  102 us (43%)
  starting transfers between devices  77.7 us (33%)
  matrix products  39.3 us (16%)
  other arithmetic  9.92 us (4%)
  local copies, waits for them, and re-layouts  8.22 us (3%)
    ppermute x39, waiting for transfers between devices, swap(): lax.ppermute(block, axis, [(at, at ^ distance) for at in range(count)])  73.1 us
    ppermute x20, starting transfers between devices, chip_moves(): return lax.ppermute(block, 'col', route)  48.8 us
    ppermute x39, starting transfers between devices, swap(): lax.ppermute(block, axis, [(at, at ^ distance) for at in range(count)])  28.9 us
    ppermute x20, waiting for transfers between devices, chip_moves(): return lax.ppermute(block, 'col', route)  28.7 us
    dot_general x8, matrix products, back(): lax.dot_general(slope, weight[side * tall:(side + 1) * tall], (((1,), (1,...  14.7 us
    dot_general x1, matrix products, shards(): lax.dot_general(clips, slopes, (((0,), (0,)), ((), ())), preferred_elemen...  11.6 us
    dot_general x5, matrix products, shards(): product = jnp.dot(block, weight, preferred_element_type=jnp.float32)  10.6 us
  transfers between devices with their start and end apart: 59, of which 27 were waited for; matrix products, arithmetic and copies ran while one was open for 14% of the time, Pallas kernels for 0%

commit v1 on v0

--- a/solution.py
+++ b/solution.py
@@ -34,13 +34,6 @@
 
 def add(first, second):
     return narrow(wide(first) + wide(second))
-
-
-def sum_over(block, axis, distance=1):
-    while distance < lax.axis_size(axis):
-        block = add(block, swap(block, axis, distance))
-        distance *= 2
-    return block
 
 
 def in_order(own, other, core):
@@ -68,11 +61,15 @@
     line = columns == 8
 
     if line:
+        own = in_order(local, swap(local, "col", 1), core)
+        own_part = narrow(
+            jnp.dot(own, weight, preferred_element_type=jnp.float32)
+        )
         halves = jnp.split(local, 2, axis=0)
+        middle = [chip_moves(part, MIDDLE) for part in halves]
         near = [chip_moves(part, OUTER_PAIRS) for part in halves]
-        middle = [chip_moves(part, MIDDLE) for part in halves]
-        across = [chip_moves(part, MIDDLE) for part in near]
-        outward = [chip_moves(part, OUTWARD) for part in middle]
+        across = [chip_moves(after(part, own_part), MIDDLE) for part in near]
+        outward = [chip_moves(after(part, own_part), OUTWARD) for part in middle]
         last = [chip_moves(part, OUTWARD) for part in across]
         low = chip < 2
         chips = [
@@ -83,7 +80,7 @@
         ]
         starts = [at * (2 * share) for at in chips]
         arrivals = [
-            (0, 0, [(part,) for part in halves]),
+            (0, 0, [(local,)]),
             (1, 0, [(part,) for part in near]),
             (2, 0, list(zip(middle, outward))),
             (3, 0, [(across[0], last[0])]),
@@ -91,7 +88,7 @@
         ]
         places = []
         for at, shift, pieces in arrivals:
-            size = len(pieces) * (share // 2)
+            size = sum(piece[0].shape[0] for piece in pieces)
             places.append(
                 [(starts[at] + side * share + shift, size) for side in range(2)]
             )
@@ -101,7 +98,7 @@
 
     pre = jnp.zeros((batch, width), jnp.float32)
     pre_other = jnp.zeros((batch, width), jnp.bfloat16)
-    streams, own_blocks, parts, sent = [], [], [], []
+    streams, own_blocks, parts, sent, arrived = [], [], [], [], []
     for at, (place, (_, _, pieces)) in enumerate(zip(places, arrivals)):
         merged = []
         for piece in pieces:
@@ -113,20 +110,27 @@
             merged.append(piece[0] + newest if len(piece) == 2 else newest)
         stream = jnp.concatenate(merged, axis=0) if len(merged) > 1 else merged[0]
         streams.append(stream)
-        block = in_order(stream, swap(stream, "col", 1), core) if line else stream
+        if line and at == 0:
+            block, part = own, own_part
+        else:
+            block = in_order(stream, swap(stream, "col", 1), core) if line else stream
+            part = narrow(jnp.dot(block, weight, preferred_element_type=jnp.float32))
         own_blocks.append(block)
-        product = jnp.dot(block, weight, preferred_element_type=jnp.float32)
-        parts.append(narrow(product))
+        parts.append(part)
         total = wide(parts[at])
         distance = 1
         while distance < lax.axis_size("row"):
             total = total + wide(swap(narrow(total), "row", distance))
             distance *= 2
         sent.append(narrow(total))
-        got = swap(sent[at], "view", 1)
+        arrived.append(swap(sent[at], "view", 1))
         for side, (start, size) in enumerate(place):
             rows = slice(side * size, (side + 1) * size)
             pre = lax.dynamic_update_slice(pre, total[rows], (start, 0))
+    for at, place in enumerate(places):
+        got = after(arrived[at], parts[-1]) if at + 1 < len(places) else arrived[at]
+        for side, (start, size) in enumerate(place):
+            rows = slice(side * size, (side + 1) * size)
             pre_other = lax.dynamic_update_slice(pre_other, got[rows], (start, 0))
 
     def normalize(values):
@@ -154,14 +158,17 @@
     keep = lax.dynamic_slice(gram, (core * half, 0), (half, batch))
     give = lax.dynamic_slice(gram, ((1 - core) * half, 0), (half, batch))
     piece = add(keep, swap(give, "col", 1))
-    piece = sum_over(piece, "col", 2)
+    begun = piece
+    distance = 2
+    while distance < columns:
+        moved = swap(piece, "col", distance)
+        piece = add(piece, moved)
+        distance *= 2
     if lax.axis_size("row") == 2:
         across_row = swap(piece, "row", 1)
-        pair = jnp.concatenate([piece, across_row], axis=0)
-        mate = swap(pair, "col", 1)
         gram = in_order(
-            in_order(pair[:half], mate[:half], core),
-            in_order(pair[half:], mate[half:], core),
+            in_order(piece, swap(piece, "col", 1), core),
+            in_order(across_row, swap(across_row, "col", 1), core),
             row,
         )
     else:
@@ -205,9 +212,8 @@
             slope = lax.dynamic_slice(dpre, (starts[at], 0), (2 * share, width))
             for side in range(sides):
                 sums[at][side] = chip_sum(slope, side)
+        results = []
         first_out = narrow(sums[3][0])
-        late = narrow(sums[0][1])
-        results = []
         for side in range(sides):
             far = sums[3][side]
             far_in = chip_moves(narrow(far), INWARD)
@@ -217,6 +223,7 @@
             mid_across = chip_moves(narrow(mid + wide(mid_in)), MIDDLE)
             close = sums[1][side] + wide(far_across)
             closed = chip_moves(narrow(close), OUTER_PAIRS)
+            late = far_across
             results.append(narrow(sums[0][side] + wide(closed) + wide(mid_across)))
         grad_hidden = jnp.concatenate(results, axis=1)
     else:
@@ -226,15 +233,14 @@
         first_out = late = grad_hidden
 
     dpre_other = swap(after(dpre, first_out), "view", 1)
-    clips = list(own_blocks)
+    clips = [after(block, late) for block in own_blocks]
     slopes = [
         lax.dynamic_slice(dpre, (start, 0), (size, width))
         for place in places
         for start, size in place
     ]
     for at, stream in enumerate(streams):
-        if at >= 2:
-            stream = after(stream, pre_other)
+        stream = after(stream, parts[0] if at == 0 else begun)
         got = swap(stream, "view", 1)
         got = after(got, late)
         if line:

time: 239 us -> 217 us (0.908)
  waiting for transfers between devices: 102 us -> 86.7 us
  matrix products: 39.3 us -> 36.3 us
  starting transfers between devices: 77.7 us -> 74.8 us
    ppermute x39 -> x40, waiting for transfers between devices: 73.1 us -> 45.3 us  [swap(): lax.ppermute(block, axis, [(at, at ^ distance) for at in range(count)])]
    ppermute x20, waiting for transfers between devices: 28.7 us -> 41.4 us  [chip_moves(): return lax.ppermute(block, 'col', route)]
    ppermute x39 -> x40, starting transfers between devices: 28.9 us -> 22.2 us  [swap(): lax.ppermute(block, axis, [(at, at ^ distance) for at in range(count)])]
    ppermute x20, starting transfers between devices: 48.8 us -> 52.7 us  [chip_moves(): return lax.ppermute(block, 'col', route)]
  transfers between devices with their start and end apart: 59 -> 60, of which waited for: 27 -> 33; matrix products, arithmetic and copies ran while one was open for 14% -> 18% of each run, Pallas kernels for 0% -> 0%
where the time goes in v1:
time: 217 us
  waiting for transfers between devices  86.7 us (40%)
  starting transfers between devices  74.8 us (34%)
  matrix products  36.3 us (17%)
  other arithmetic  8.82 us (4%)
  local copies, waits for them, and re-layouts  7.86 us (4%)
    ppermute x20, starting transfers between devices, chip_moves(): return lax.ppermute(block, 'col', route)  52.7 us
    ppermute x40, waiting for transfers between devices, swap(): lax.ppermute(block, axis, [(at, at ^ distance) for at in range(count)])  45.3 us
    ppermute x20, waiting for transfers between devices, chip_moves(): return lax.ppermute(block, 'col', route)  41.4 us
    ppermute x40, starting transfers between devices, swap(): lax.ppermute(block, axis, [(at, at ^ distance) for at in range(count)])  22.2 us
    dot_general x8, matrix products, back(): lax.dot_general(slope, weight[side * tall:(side + 1) * tall], (((1,), (1,...  12.3 us
    dot_general x1, matrix products, shards(): lax.dot_general(clips, slopes, (((0,), (0,)), ((), ())), preferred_elemen...  11.8 us
    dot_general x4, matrix products, shards(): part = narrow(jnp.dot(block, weight, preferred_element_type=jnp.float32))  5.74 us
    dot_general x1, matrix products, shards(): own_part = narrow(jnp.dot(own, weight, preferred_element_type=jnp.float32))  4.86 us
  transfers between devices with their start and end apart: 60, of which 33 were waited for; matrix products, arithmetic and copies ran while one was open for 18% of the time, Pallas kernels for 0%

profile of v1, /device:TPU:0, one launch (start us, length us, event | category | flops | bytes accessed | tf_op | source)
XLA Modules:
  0.0 216.6 jit_solution(645112835143130661)
XLA Ops:
  2.9 5.4 %collective-permute-start.2 = (bf16[32,4096]{1,0:T(8,128)(2,1)S(1)}, bf16[32,4096]{1,0:T(8,128)(2,1)S(1)}, u32[]{:S(2)}, u32[]{:S(2)}) collective-permute-start(bf16[32,4096]{1,0:T(8,128)(2,1)S(1)} %get-tuple-element.89), channel_id=1, source_target_pairs={{0,2},{1,3},{2,0},{3,1},{4,6},{5,7},{6,4},{7,5},{8,10},{9,11},{10,... | collective-permute-start | bytes 786440 | tf_op jit(solution)/shard_map/ppermute | solution.py:20
  9.1 1.8 collective-permute-start.3
  12.1 4.9 %convolution_convert_fusion.2 = bf16[128,1024]{1,0:T(8,128)(2,1)S(1)} fusion(bf16[4096,1024]{1,0:T(8,128)(2,1)} %param.3, bf16[64,4096]{1,0:T(8,128)(2,1)S(1)} %get-tuple-element.76, bf16[64,4096]{1,0:T(8,128)(2,1)S(1)} %get-tuple-element.75), kind=kOutput, calls=%fused_computation.48 | convolution fusion | flops 1075970048 | bytes 9699328 | tf_op jit(solution)/shard_map/dot_general | solution.py:66
  17.0 1.6 collective-permute-start.1
  25.5 1.5 collective-permute-done.4
  27.0 1.5 collective-permute-start.49
  29.9 10.6 %collective-permute-done.9 = bf16[32,4096]{1,0:T(8,128)(2,1)S(1)} collective-permute-done((bf16[32,4096]{1,0:T(8,128)(2,1)S(1)}, bf16[32,4096]{1,0:T(8,128)(2,1)S(1)}, u32[]{:S(2)}, u32[]{:S(2)}) %collective-permute-start.9) | collective-permute-done | bytes 262176 | tf_op jit(solution)/shard_map/ppermute | solution.py:20
  40.5 1.5 collective-permute-start.5
  43.4 1.5 collective-permute-start.20
  47.4 1.5 collective-permute-start.17
  49.0 1.6 collective-permute-start.21
  52.1 3.8 %collective-permute-done.13 = bf16[32,4096]{1,0:T(8,128)(2,1)S(1)} collective-permute-done((bf16[32,4096]{1,0:T(8,128)(2,1)S(1)}, bf16[32,4096]{1,0:T(8,128)(2,1)S(1)}, u32[]{:S(2)}, u32[]{:S(2)}) %collective-permute-start.13) | collective-permute-done | bytes 262176 | tf_op jit(solution)/shard_map/ppermute | solution.py:20
  56.2 1.5 collective-permute-done.14
  58.3 1.6 convolution_convert_fusion.4
  61.5 5.4 %collective-permute-done.11 = bf16[128,1024]{1,0:T(8,128)(2,1)S(1)} collective-permute-done((bf16[128,1024]{1,0:T(8,128)(2,1)S(1)}, bf16[128,1024]{1,0:T(8,128)(2,1)S(1)}, u32[]{:S(2)}, u32[]{:S(2)}) %collective-permute-start.11) | collective-permute-done | bytes 262176 | tf_op jit(solution)/shard_map/ppermute | solution.py:15
  68.9 1.4 collective-permute-done.18
  70.9 1.6 convolution_convert_fusion.3
  74.5 2.0 collective-permute-done.23
  76.5 1.4 collective-permute-done.19
  78.0 1.6 collective-permute-start.24
  80.0 3.1 %collective-permute-done.24 = bf16[64,1024]{1,0:T(8,128)(2,1)} collective-permute-done((bf16[64,1024]{1,0:T(8,128)(2,1)S(1)}, bf16[64,1024]{1,0:T(8,128)(2,1)}, u32[]{:S(2)}, u32[]{:S(2)}) %collective-permute-start.24) | collective-permute-done | bytes 131104 | tf_op jit(solution)/shard_map/ppermute | solution.py:15
  88.1 5.5 %collective-permute-done.26 = bf16[128,512]{1,0:T(8,128)(2,1)S(1)} collective-permute-done((bf16[128,512]{1,0:T(8,128)(2,1)S(1)}, bf16[128,512]{1,0:T(8,128)(2,1)S(1)}, u32[]{:S(2)}, u32[]{:S(2)}) %collective-permute-start.26) | collective-permute-done | bytes 131104 | tf_op jit(solution)/shard_map/ppermute | solution.py:15
  95.0 7.1 %collective-permute-done.27 = bf16[128,512]{1,0:T(8,128)(2,1)S(1)} collective-permute-done((bf16[128,512]{1,0:T(8,128)(2,1)S(1)}, bf16[128,512]{1,0:T(8,128)(2,1)S(1)}, u32[]{:S(2)}, u32[]{:S(2)}) %collective-permute-start.27) | collective-permute-done | bytes 131104 | tf_op jit(solution)/shard_map/ppermute | solution.py:15
  102.7 1.6 collective-permute-start.57
  104.8 2.8 %collective-permute-done.29 = bf16[128,512]{1,0:T(8,128)(2,1)S(1)} collective-permute-done((bf16[128,512]{1,0:T(8,128)(2,1)S(1)}, bf16[128,512]{1,0:T(8,128)(2,1)S(1)}, u32[]{:S(2)}, u32[]{:S(2)}) %collective-permute-start.29) | collective-permute-done | bytes 131104 | tf_op jit(solution)/shard_map/ppermute | solution.py:15
  107.6 1.5 collective-permute-start.53
  112.8 1.5 fusion.36
  114.3 1.7 fusion.39
  116.0 1.5 fusion.27
  117.5 1.5 fusion.24
  119.0 1.5 fusion.30
  120.6 1.5 fusion.33
  122.1 1.5 fusion.21
  123.6 1.5 fusion.18
  131.5 1.6 collective-permute-start.43
  133.2 5.8 %collective-permute-done.43 = bf16[64,2048]{1,0:T(8,128)(2,1)S(1)} collective-permute-done((bf16[64,2048]{1,0:T(8,128)(2,1)S(1)}, bf16[64,2048]{1,0:T(8,128)(2,1)S(1)}, u32[]{:S(2)}, u32[]{:S(2)}) %collective-permute-start.43) | collective-permute-done | bytes 262176 | tf_op jit(solution)/shard_map/ppermute | solution.py:20
  138.9 4.4 %collective-permute-start.47 = (bf16[64,2048]{1,0:T(8,128)(2,1)S(1)}, bf16[64,2048]{1,0:T(8,128)(2,1)S(1)}, u32[]{:S(2)}, u32[]{:S(2)}) collective-permute-start(bf16[64,2048]{1,0:T(8,128)(2,1)S(1)} %fusion.63), channel_id=1, source_target_pairs={{0,2},{1,3},{6,4},{7,5},{8,10},{9,11},{14,12},{15,13},{16,18},{17,... | collective-permute-start | bytes 786440 | tf_op jit(solution)/shard_map/ppermute | solution.py:20
  143.4 4.9 %collective-permute-done.47 = bf16[64,2048]{1,0:T(8,128)(2,1)S(1)} collective-permute-done((bf16[64,2048]{1,0:T(8,128)(2,1)S(1)}, bf16[64,2048]{1,0:T(8,128)(2,1)S(1)}, u32[]{:S(2)}, u32[]{:S(2)}) %collective-permute-start.47) | collective-permute-done | bytes 262176 | tf_op jit(solution)/shard_map/ppermute | solution.py:20
  148.3 4.4 %collective-permute-start.38 = (bf16[64,2048]{1,0:T(8,128)(2,1)S(1)}, bf16[64,2048]{1,0:T(8,128)(2,1)S(1)}, u32[]{:S(2)}, u32[]{:S(2)}) collective-permute-start(bf16[64,2048]{1,0:T(8,128)(2,1)S(1)} %fusion.61), channel_id=1, source_target_pairs={{0,2},{1,3},{6,4},{7,5},{8,10},{9,11},{14,12},{15,13},{16,18},{17,... | collective-permute-start | bytes 786440 | tf_op jit(solution)/shard_map/ppermute | solution.py:20
  152.8 4.0 %collective-permute-done.38 = bf16[64,2048]{1,0:T(8,128)(2,1)S(1)} collective-permute-done((bf16[64,2048]{1,0:T(8,128)(2,1)S(1)}, bf16[64,2048]{1,0:T(8,128)(2,1)S(1)}, u32[]{:S(2)}, u32[]{:S(2)}) %collective-permute-start.38) | collective-permute-done | bytes 262176 | tf_op jit(solution)/shard_map/ppermute | solution.py:20
  156.9 4.4 %collective-permute-start.34 = (bf16[64,2048]{1,0:T(8,128)(2,1)S(1)}, bf16[64,2048]{1,0:T(8,128)(2,1)S(1)}, u32[]{:S(2)}, u32[]{:S(2)}) collective-permute-start(bf16[64,2048]{1,0:T(8,128)(2,1)S(1)} %fusion.60), channel_id=1, source_target_pairs={{0,2},{1,3},{6,4},{7,5},{8,10},{9,11},{14,12},{15,13},{16,18},{17,... | collective-permute-start | bytes 786440 | tf_op jit(solution)/shard_map/ppermute | solution.py:20
  162.0 3.1 %collective-permute-done.34 = bf16[64,2048]{1,0:T(8,128)(2,1)S(1)} collective-permute-done((bf16[64,2048]{1,0:T(8,128)(2,1)S(1)}, bf16[64,2048]{1,0:T(8,128)(2,1)S(1)}, u32[]{:S(2)}, u32[]{:S(2)}) %collective-permute-start.34) | collective-permute-done | bytes 262176 | tf_op jit(solution)/shard_map/ppermute | solution.py:20
  166.0 1.8 collective-permute-done.55
  170.9 18.0 %collective-permute-start.45 = (bf16[64,2048]{1,0:T(8,128)(2,1)S(1)}, bf16[64,2048]{1,0:T(8,128)(2,1)S(1)}, u32[]{:S(2)}, u32[]{:S(2)}) collective-permute-start(bf16[64,2048]{1,0:T(8,128)(2,1)S(1)} %add_convert_fusion.2), channel_id=1, source_target_pairs={{0,2},{1,3},{2,0},{3,1},{4,6},{5,7},{6,4},{7,5},{8,10},{9,11},{10,... | collective-permute-start | bytes 786440 | tf_op jit(solution)/shard_map/ppermute | solution.py:20
  191.2 3.2 %collective-permute-done.45 = bf16[64,2048]{1,0:T(8,128)(2,1)S(1)} collective-permute-done((bf16[64,2048]{1,0:T(8,128)(2,1)S(1)}, bf16[64,2048]{1,0:T(8,128)(2,1)S(1)}, u32[]{:S(2)}, u32[]{:S(2)}) %collective-permute-start.45) | collective-permute-done | bytes 262176 | tf_op jit(solution)/shard_map/ppermute | solution.py:20
  194.4 1.7 collective-permute-start.36
  196.9 4.5 %collective-permute-done.36 = bf16[64,2048]{1,0:T(8,128)(2,1)S(1)} collective-permute-done((bf16[64,2048]{1,0:T(8,128)(2,1)S(1)}, bf16[64,2048]{1,0:T(8,128)(2,1)S(1)}, u32[]{:S(2)}, u32[]{:S(2)}) %collective-permute-start.36) | collective-permute-done | bytes 262176 | tf_op jit(solution)/shard_map/ppermute | solution.py:20
  204.8 11.8 %convolution_multiply_fusion = f32[4096,1024]{1,0:T(8,128)} fusion(bf16[1024,4096]{1,0:T(8,128)(2,1)S(1)} %constant_dynamic-update-slice_fusion.2, bf16[1024,1024]{1,0:T(8,128)(2,1)S(1)} %constant_dynamic-update-slice_fusion.17), kind=kOutput, calls=%fused_computation | convolution fusion | flops 8594128896 | bytes 27262976 | tf_op jit(solution)/shard_map/dot_general | solution.py:260
  (259 shorter events, 53.5 us)
Async XLA Ops:
  0.6 10.2 %collective-permute-start = (bf16[64,4096]{1,0:T(8,128)(2,1)}, bf16[64,4096]{1,0:T(8,128)(2,1)S(1)}, u32[]{:S(2)}, u32[]{:S(2)}) collective-permute-start(bf16[64,4096]{1,0:T(8,128)(2,1)} %bitcast), channel_id=1, source_target_pairs={{0,1},{1,0},{2,3},{3,2},{4,5},{5,4},{6,7},{7,6},{8,9},{9,8},{10,11... | collective-permute-start | bytes 1572872 | tf_op jit(solution)/shard_map/ppermute | solution.py:15
  2.3 16.3 %collective-permute-start.6 = (bf16[32,4096]{1,0:T(8,128)(2,1)S(1)}, bf16[32,4096]{1,0:T(8,128)(2,1)S(1)}, u32[]{:S(2)}, u32[]{:S(2)}) collective-permute-start(bf16[32,4096]{1,0:T(8,128)(2,1)S(1)} %get-tuple-element.89), channel_id=1, source_target_pairs={{2,4},{3,5},{4,2},{5,3},{10,12},{11,13},{12,10},{13,11},{18,20},{1... | collective-permute-start | bytes 786440 | tf_op jit(solution)/shard_map/ppermute | solution.py:20
  2.9 16.7 %collective-permute-start.2 = (bf16[32,4096]{1,0:T(8,128)(2,1)S(1)}, bf16[32,4096]{1,0:T(8,128)(2,1)S(1)}, u32[]{:S(2)}, u32[]{:S(2)}) collective-permute-start(bf16[32,4096]{1,0:T(8,128)(2,1)S(1)} %get-tuple-element.89), channel_id=1, source_target_pairs={{0,2},{1,3},{2,0},{3,1},{4,6},{5,7},{6,4},{7,5},{8,10},{9,11},{10,... | collective-permute-start | bytes 786440 | tf_op jit(solution)/shard_map/ppermute | solution.py:20
  8.4 10.2 %collective-permute-start.8 = (bf16[32,4096]{1,0:T(8,128)(2,1)S(1)}, bf16[32,4096]{1,0:T(8,128)(2,1)S(1)}, u32[]{:S(2)}, u32[]{:S(2)}) collective-permute-start(bf16[32,4096]{1,0:T(8,128)(2,1)S(1)} %get-tuple-element.90), channel_id=1, source_target_pairs={{2,4},{3,5},{4,2},{5,3},{10,12},{11,13},{12,10},{13,11},{18,20},{1... | collective-permute-start | bytes 786440 | tf_op jit(solution)/shard_map/ppermute | solution.py:20
  9.1 11.7 %collective-permute-start.3 = (bf16[32,4096]{1,0:T(8,128)(2,1)S(1)}, bf16[32,4096]{1,0:T(8,128)(2,1)}, u32[]{:S(2)}, u32[]{:S(2)}) collective-permute-start(bf16[32,4096]{1,0:T(8,128)(2,1)S(1)} %get-tuple-element.90), channel_id=1, source_target_pairs={{0,2},{1,3},{2,0},{3,1},{4,6},{5,7},{6,4},{7,5},{8,10},{9,11},{10,... | collective-permute-start | bytes 786440 | tf_op jit(solution)/shard_map/ppermute | solution.py:20
  17.0 8.1 %collective-permute-start.1 = (bf16[128,1024]{1,0:T(8,128)(2,1)S(1)}, bf16[128,1024]{1,0:T(8,128)(2,1)S(1)}, u32[]{:S(2)}, u32[]{:S(2)}) collective-permute-start(bf16[128,1024]{1,0:T(8,128)(2,1)S(1)} %convolution_convert_fusion.2), channel_id=1, source_target_pairs={{0,8},{8,0},{1,9},{9,1},{2,10},{10,2},{3,11},{11,3},{4,12},{12,4},... | collective-permute-start | bytes 786440 | tf_op jit(solution)/shard_map/ppermute | solution.py:15
  19.6 23.8 %collective-permute-start.12 = (bf16[32,4096]{1,0:T(8,128)(2,1)S(1)}, bf16[32,4096]{1,0:T(8,128)(2,1)S(1)}, u32[]{:S(2)}, u32[]{:S(2)}) collective-permute-start(bf16[32,4096]{1,0:T(8,128)(2,1)S(1)} %collective-permute-done.2), channel_id=1, source_target_pairs={{2,4},{3,5},{4,2},{5,3},{10,12},{11,13},{12,10},{13,11},{18,20},{1... | collective-permute-start | bytes 786440 | tf_op jit(solution)/shard_map/ppermute | solution.py:20
  20.8 24.1 %collective-permute-start.16 = (bf16[32,4096]{1,0:T(8,128)(2,1)}, bf16[32,4096]{1,0:T(8,128)(2,1)S(1)}, u32[]{:S(2)}, u32[]{:S(2)}) collective-permute-start(bf16[32,4096]{1,0:T(8,128)(2,1)} %collective-permute-done.3), channel_id=1, source_target_pairs={{2,4},{3,5},{4,2},{5,3},{10,12},{11,13},{12,10},{13,11},{18,20},{1... | collective-permute-start | bytes 786440 | tf_op jit(solution)/shard_map/ppermute | solution.py:20
  21.5 20.6 %collective-permute-start.7 = (bf16[32,4096]{1,0:T(8,128)(2,1)S(1)}, bf16[32,4096]{1,0:T(8,128)(2,1)S(1)}, u32[]{:S(2)}, u32[]{:S(2)}) collective-permute-start(bf16[32,4096]{1,0:T(8,128)(2,1)S(1)} %collective-permute-done.6), channel_id=1, source_target_pairs={{2,0},{3,1},{4,6},{5,7},{10,8},{11,9},{12,14},{13,15},{18,16},{19,... | collective-permute-start | bytes 786440 | tf_op jit(solution)/shard_map/ppermute | solution.py:20
  22.8 17.8 %collective-permute-start.9 = (bf16[32,4096]{1,0:T(8,128)(2,1)S(1)}, bf16[32,4096]{1,0:T(8,128)(2,1)S(1)}, u32[]{:S(2)}, u32[]{:S(2)}) collective-permute-start(bf16[32,4096]{1,0:T(8,128)(2,1)S(1)} %collective-permute-done.8), channel_id=1, source_target_pairs={{2,0},{3,1},{4,6},{5,7},{10,8},{11,9},{12,14},{13,15},{18,16},{19,... | collective-permute-start | bytes 786440 | tf_op jit(solution)/shard_map/ppermute | solution.py:20
  25.1 2.0 collective-permute-start.4
  27.0 140.8 %collective-permute-start.49 = (bf16[64,4096]{1,0:T(8,128)(2,1)}, bf16[64,4096]{1,0:T(8,128)(2,1)}, u32[]{:S(2)}, u32[]{:S(2)}) collective-permute-start(bf16[64,4096]{1,0:T(8,128)(2,1)} %bitcast), channel_id=1, source_target_pairs={{0,16},{16,0},{1,17},{17,1},{2,18},{18,2},{3,19},{19,3},{4,20},{20... | collective-permute-start | bytes 1572872 | tf_op jit(solution)/shard_map/ppermute | solution.py:15
  40.5 6.9 %collective-permute-start.5 = (bf16[128,1024]{1,0:T(8,128)(2,1)S(1)}, bf16[128,1024]{1,0:T(8,128)(2,1)S(1)}, u32[]{:S(2)}, u32[]{:S(2)}) collective-permute-start(bf16[128,1024]{1,0:T(8,128)(2,1)S(1)} %convolution_convert_fusion.1), channel_id=1, source_target_pairs={{0,8},{8,0},{1,9},{9,1},{2,10},{10,2},{3,11},{11,3},{4,12},{12,4},... | collective-permute-start | bytes 786440 | tf_op jit(solution)/shard_map/ppermute | solution.py:15
  42.2 6.8 %collective-permute-start.10 = (bf16[64,4096]{1,0:T(8,128)(2,1)S(1)}, bf16[64,4096]{1,0:T(8,128)(2,1)S(1)}, u32[]{:S(2)}, u32[]{:S(2)}) collective-permute-start(bf16[64,4096]{1,0:T(8,128)(2,1)S(1)} %pad_maximum_fusion.3), channel_id=1, source_target_pairs={{0,1},{1,0},{2,3},{3,2},{4,5},{5,4},{6,7},{7,6},{8,9},{9,8},{10,11... | collective-permute-start | bytes 1572872 | tf_op jit(solution)/shard_map/ppermute | solution.py:15
  43.4 29.8 %collective-permute-start.20 = (bf16[128,1024]{1,0:T(8,128)(2,1)S(1)}, bf16[128,1024]{1,0:T(8,128)(2,1)S(1)}, u32[]{:S(2)}, u32[]{:S(2)}) collective-permute-start(bf16[128,1024]{1,0:T(8,128)(2,1)S(1)} %get-tuple-element.84), channel_id=1, source_target_pairs={{0,16},{16,0},{1,17},{17,1},{2,18},{18,2},{3,19},{19,3},{4,20},{20... | collective-permute-start | bytes 786440 | tf_op jit(solution)/shard_map/ppermute | solution.py:15
  44.9 11.1 %collective-permute-start.13 = (bf16[32,4096]{1,0:T(8,128)(2,1)S(1)}, bf16[32,4096]{1,0:T(8,128)(2,1)S(1)}, u32[]{:S(2)}, u32[]{:S(2)}) collective-permute-start(bf16[32,4096]{1,0:T(8,128)(2,1)S(1)} %collective-permute-done.12), channel_id=1, source_target_pairs={{2,0},{3,1},{4,6},{5,7},{10,8},{11,9},{12,14},{13,15},{18,16},{19,... | collective-permute-start | bytes 786440 | tf_op jit(solution)/shard_map/ppermute | solution.py:20
  47.4 13.4 %collective-permute-start.17 = (bf16[32,4096]{1,0:T(8,128)(2,1)S(1)}, bf16[32,4096]{1,0:T(8,128)(2,1)S(1)}, u32[]{:S(2)}, u32[]{:S(2)}) collective-permute-start(bf16[32,4096]{1,0:T(8,128)(2,1)S(1)} %collective-permute-done.16), channel_id=1, source_target_pairs={{2,0},{3,1},{4,6},{5,7},{10,8},{11,9},{12,14},{13,15},{18,16},{19,... | collective-permute-start | bytes 786440 | tf_op jit(solution)/shard_map/ppermute | solution.py:20
  49.0 23.6 %collective-permute-start.21 = (bf16[128,1024]{1,0:T(8,128)(2,1)S(1)}, bf16[128,1024]{1,0:T(8,128)(2,1)S(1)}, u32[]{:S(2)}, u32[]{:S(2)}) collective-permute-start(bf16[128,1024]{1,0:T(8,128)(2,1)S(1)} %get-tuple-element.82), channel_id=1, source_target_pairs={{0,16},{16,0},{1,17},{17,1},{2,18},{18,2},{3,19},{19,3},{4,20},{20... | collective-permute-start | bytes 786440 | tf_op jit(solution)/shard_map/ppermute | solution.py:15
  57.6 9.2 %collective-permute-start.11 = (bf16[128,1024]{1,0:T(8,128)(2,1)S(1)}, bf16[128,1024]{1,0:T(8,128)(2,1)S(1)}, u32[]{:S(2)}, u32[]{:S(2)}) collective-permute-start(bf16[128,1024]{1,0:T(8,128)(2,1)S(1)} %convolution_convert_fusion), channel_id=1, source_target_pairs={{0,8},{8,0},{1,9},{9,1},{2,10},{10,2},{3,11},{11,3},{4,12},{12,4},... | collective-permute-start | bytes 786440 | tf_op jit(solution)/shard_map/ppermute | solution.py:15
  60.8 8.0 %collective-permute-start.15 = (bf16[64,1024]{1,0:T(8,128)(2,1)S(1)}, bf16[64,1024]{1,0:T(8,128)(2,1)S(1)}, u32[]{:S(2)}, u32[]{:S(2)}) collective-permute-start(bf16[64,1024]{1,0:T(8,128)(2,1)S(1)} %convolution_convert_fusion.4), channel_id=1, source_target_pairs={{0,8},{8,0},{1,9},{9,1},{2,10},{10,2},{3,11},{11,3},{4,12},{12,4},... | collective-permute-start | bytes 393224 | tf_op jit(solution)/shard_map/ppermute | solution.py:15
  66.9 7.3 %collective-permute-start.22 = (bf16[128,1024]{1,0:T(8,128)(2,1)S(1)}, bf16[128,1024]{1,0:T(8,128)(2,1)S(1)}, u32[]{:S(2)}, u32[]{:S(2)}) collective-permute-start(bf16[128,1024]{1,0:T(8,128)(2,1)S(1)} %get-tuple-element.80), channel_id=1, source_target_pairs={{0,16},{16,0},{1,17},{17,1},{2,18},{18,2},{3,19},{19,3},{4,20},{20... | collective-permute-start | bytes 786440 | tf_op jit(solution)/shard_map/ppermute | solution.py:15
  70.3 6.1 %collective-permute-start.23 = (bf16[64,1024]{1,0:T(8,128)(2,1)S(1)}, bf16[64,1024]{1,0:T(8,128)(2,1)S(1)}, u32[]{:S(2)}, u32[]{:S(2)}) collective-permute-start(bf16[64,1024]{1,0:T(8,128)(2,1)S(1)} %get-tuple-element.98), channel_id=1, source_target_pairs={{0,16},{16,0},{1,17},{17,1},{2,18},{18,2},{3,19},{19,3},{4,20},{20... | collective-permute-start | bytes 393224 | tf_op jit(solution)/shard_map/ppermute | solution.py:15
  72.6 5.3 %collective-permute-start.19 = (bf16[64,1024]{1,0:T(8,128)(2,1)S(1)}, bf16[64,1024]{1,0:T(8,128)(2,1)S(1)}, u32[]{:S(2)}, u32[]{:S(2)}) collective-permute-start(bf16[64,1024]{1,0:T(8,128)(2,1)S(1)} %convolution_convert_fusion.3), channel_id=1, source_target_pairs={{0,8},{8,0},{1,9},{9,1},{2,10},{10,2},{3,11},{11,3},{4,12},{12,4},... | collective-permute-start | bytes 393224 | tf_op jit(solution)/shard_map/ppermute | solution.py:15
  78.0 5.1 %collective-permute-start.24 = (bf16[64,1024]{1,0:T(8,128)(2,1)S(1)}, bf16[64,1024]{1,0:T(8,128)(2,1)}, u32[]{:S(2)}, u32[]{:S(2)}) collective-permute-start(bf16[64,1024]{1,0:T(8,128)(2,1)S(1)} %get-tuple-element.96), channel_id=1, source_target_pairs={{0,16},{16,0},{1,17},{17,1},{2,18},{18,2},{3,19},{19,3},{4,20},{20... | collective-permute-start | bytes 393224 | tf_op jit(solution)/shard_map/ppermute | solution.py:15
  87.9 5.6 %collective-permute-start.26 = (bf16[128,512]{1,0:T(8,128)(2,1)S(1)}, bf16[128,512]{1,0:T(8,128)(2,1)S(1)}, u32[]{:S(2)}, u32[]{:S(2)}) collective-permute-start(bf16[128,512]{1,0:T(8,128)(2,1)S(1)} %add_convert_fusion.10), channel_id=1, source_target_pairs={{0,2},{1,3},{2,0},{3,1},{4,6},{5,7},{6,4},{7,5},{8,10},{9,11},{10,... | collective-permute-start | bytes 393224 | tf_op jit(solution)/shard_map/ppermute | solution.py:15
  93.6 8.5 %collective-permute-start.27 = (bf16[128,512]{1,0:T(8,128)(2,1)S(1)}, bf16[128,512]{1,0:T(8,128)(2,1)S(1)}, u32[]{:S(2)}, u32[]{:S(2)}) collective-permute-start(bf16[128,512]{1,0:T(8,128)(2,1)S(1)} %add_convert_fusion.9), channel_id=1, source_target_pairs={{0,4},{1,5},{2,6},{3,7},{4,0},{5,1},{6,2},{7,3},{8,12},{9,13},{10,... | collective-permute-start | bytes 393224 | tf_op jit(solution)/shard_map/ppermute | solution.py:15
  102.1 5.5 %collective-permute-start.29 = (bf16[128,512]{1,0:T(8,128)(2,1)S(1)}, bf16[128,512]{1,0:T(8,128)(2,1)S(1)}, u32[]{:S(2)}, u32[]{:S(2)}) collective-permute-start(bf16[128,512]{1,0:T(8,128)(2,1)S(1)} %add_convert_fusion.8), channel_id=1, source_target_pairs={{0,8},{8,0},{1,9},{9,1},{2,10},{10,2},{3,11},{11,3},{4,12},{12,4},... | collective-permute-start | bytes 393224 | tf_op jit(solution)/shard_map/ppermute | solution.py:15
  102.7 6.4 %collective-permute-start.28 = (bf16[128,512]{1,0:T(8,128)(2,1)S(1)}, bf16[128,512]{1,0:T(8,128)(2,1)S(1)}, u32[]{:S(2)}, u32[]{:S(2)}) collective-permute-start(bf16[128,512]{1,0:T(8,128)(2,1)S(1)} %add_convert_fusion.8), channel_id=1, source_target_pairs={{0,1},{1,0},{2,3},{3,2},{4,5},{5,4},{6,7},{7,6},{8,9},{9,8},{10,11... | collective-permute-start | bytes 393224 | tf_op jit(solution)/shard_map/ppermute | solution.py:15
  102.7 58.7 %collective-permute-start.57 = (bf16[32,4096]{1,0:T(8,128)(2,1)S(1)}, bf16[32,4096]{1,0:T(8,128)(2,1)S(1)}, u32[]{:S(2)}, u32[]{:S(2)}) collective-permute-start(bf16[32,4096]{1,0:T(8,128)(2,1)S(1)} %copy-done.17), channel_id=1, source_target_pairs={{0,16},{16,0},{1,17},{17,1},{2,18},{18,2},{3,19},{19,3},{4,20},{20... | collective-permute-start | bytes 786440 | tf_op jit(solution)/shard_map/ppermute | solution.py:15
  104.3 64.1 %collective-permute-start.51 = (bf16[64,4096]{1,0:T(8,128)(2,1)S(1)}, bf16[64,4096]{1,0:T(8,128)(2,1)S(1)}, u32[]{:S(2)}, u32[]{:S(2)}) collective-permute-start(bf16[64,4096]{1,0:T(8,128)(2,1)S(1)} %copy-done.13), channel_id=1, source_target_pairs={{0,16},{16,0},{1,17},{17,1},{2,18},{18,2},{3,19},{19,3},{4,20},{20... | collective-permute-start | bytes 1572872 | tf_op jit(solution)/shard_map/ppermute | solution.py:15
  107.6 60.8 %collective-permute-start.53 = (bf16[64,4096]{1,0:T(8,128)(2,1)S(1)}, bf16[64,4096]{1,0:T(8,128)(2,1)S(1)}, u32[]{:S(2)}, u32[]{:S(2)}) collective-permute-start(bf16[64,4096]{1,0:T(8,128)(2,1)S(1)} %copy-done.19), channel_id=1, source_target_pairs={{0,16},{16,0},{1,17},{17,1},{2,18},{18,2},{3,19},{19,3},{4,20},{20... | collective-permute-start | bytes 1572872 | tf_op jit(solution)/shard_map/ppermute | solution.py:15
  131.5 7.4 %collective-permute-start.43 = (bf16[64,2048]{1,0:T(8,128)(2,1)S(1)}, bf16[64,2048]{1,0:T(8,128)(2,1)S(1)}, u32[]{:S(2)}, u32[]{:S(2)}) collective-permute-start(bf16[64,2048]{1,0:T(8,128)(2,1)S(1)} %fusion.62), channel_id=1, source_target_pairs={{0,2},{1,3},{6,4},{7,5},{8,10},{9,11},{14,12},{15,13},{16,18},{17,... | collective-permute-start | bytes 786440 | tf_op jit(solution)/shard_map/ppermute | solution.py:20
  138.9 9.4 %collective-permute-start.47 = (bf16[64,2048]{1,0:T(8,128)(2,1)S(1)}, bf16[64,2048]{1,0:T(8,128)(2,1)S(1)}, u32[]{:S(2)}, u32[]{:S(2)}) collective-permute-start(bf16[64,2048]{1,0:T(8,128)(2,1)S(1)} %fusion.63), channel_id=1, source_target_pairs={{0,2},{1,3},{6,4},{7,5},{8,10},{9,11},{14,12},{15,13},{16,18},{17,... | collective-permute-start | bytes 786440 | tf_op jit(solution)/shard_map/ppermute | solution.py:20
  148.3 8.5 %collective-permute-start.38 = (bf16[64,2048]{1,0:T(8,128)(2,1)S(1)}, bf16[64,2048]{1,0:T(8,128)(2,1)S(1)}, u32[]{:S(2)}, u32[]{:S(2)}) collective-permute-start(bf16[64,2048]{1,0:T(8,128)(2,1)S(1)} %fusion.61), channel_id=1, source_target_pairs={{0,2},{1,3},{6,4},{7,5},{8,10},{9,11},{14,12},{15,13},{16,18},{17,... | collective-permute-start | bytes 786440 | tf_op jit(solution)/shard_map/ppermute | solution.py:20
  156.9 8.3 %collective-permute-start.34 = (bf16[64,2048]{1,0:T(8,128)(2,1)S(1)}, bf16[64,2048]{1,0:T(8,128)(2,1)S(1)}, u32[]{:S(2)}, u32[]{:S(2)}) collective-permute-start(bf16[64,2048]{1,0:T(8,128)(2,1)S(1)} %fusion.60), channel_id=1, source_target_pairs={{0,2},{1,3},{6,4},{7,5},{8,10},{9,11},{14,12},{15,13},{16,18},{17,... | collective-permute-start | bytes 786440 | tf_op jit(solution)/shard_map/ppermute | solution.py:20
  161.4 6.4 %collective-permute-start.55 = (bf16[32,4096]{1,0:T(8,128)(2,1)S(1)}, bf16[32,4096]{1,0:T(8,128)(2,1)S(1)}, u32[]{:S(2)}, u32[]{:S(2)}) collective-permute-start(bf16[32,4096]{1,0:T(8,128)(2,1)S(1)} %copy-done.15), channel_id=1, source_target_pairs={{0,16},{16,0},{1,17},{17,1},{2,18},{18,2},{3,19},{19,3},{4,20},{20... | collective-permute-start | bytes 786440 | tf_op jit(solution)/shard_map/ppermute | solution.py:15
  165.9 24.2 %collective-permute-start.40 = (bf16[64,2048]{1,0:T(8,128)(2,1)S(1)}, bf16[64,2048]{1,0:T(8,128)(2,1)S(1)}, u32[]{:S(2)}, u32[]{:S(2)}) collective-permute-start(bf16[64,2048]{1,0:T(8,128)(2,1)S(1)} %constant_dynamic-slice_fusion.3), channel_id=1, source_target_pairs={{0,1},{1,0},{2,3},{3,2},{4,5},{5,4},{6,7},{7,6},{8,9},{9,8},{10,11... | collective-permute-start | bytes 786440 | tf_op jit(solution)/shard_map/ppermute | solution.py:15
  167.8 2.4 %collective-permute-start.32 = (bf16[64,2048]{1,0:T(8,128)(2,1)S(1)}, bf16[64,2048]{1,0:T(8,128)(2,1)S(1)}, u32[]{:S(2)}, u32[]{:S(2)}) collective-permute-start(bf16[64,2048]{1,0:T(8,128)(2,1)S(1)} %constant_dynamic-slice_fusion.6), channel_id=1, source_target_pairs={{0,1},{1,0},{2,3},{3,2},{4,5},{5,4},{6,7},{7,6},{8,9},{9,8},{10,11... | collective-permute-start | bytes 786440 | tf_op jit(solution)/shard_map/ppermute | solution.py:15
  168.3 28.0 %collective-permute-start.31 = (bf16[64,2048]{1,0:T(8,128)(2,1)S(1)}, bf16[64,2048]{1,0:T(8,128)(2,1)S(1)}, u32[]{:S(2)}, u32[]{:S(2)}) collective-permute-start(bf16[64,2048]{1,0:T(8,128)(2,1)S(1)} %constant_dynamic-slice_fusion.7), channel_id=1, source_target_pairs={{0,1},{1,0},{2,3},{3,2},{4,5},{5,4},{6,7},{7,6},{8,9},{9,8},{10,11... | collective-permute-start | bytes 786440 | tf_op jit(solution)/shard_map/ppermute | solution.py:15
  168.4 36.1 %collective-permute-start.59 = (bf16[512,1024]{1,0:T(8,128)(2,1)S(1)}, bf16[512,1024]{1,0:T(8,128)(2,1)S(1)}, u32[]{:S(2)}, u32[]{:S(2)}) collective-permute-start(bf16[512,1024]{1,0:T(8,128)(2,1)S(1)} %fusion.51), channel_id=1, source_target_pairs={{0,16},{16,0},{1,17},{17,1},{2,18},{18,2},{3,19},{19,3},{4,20},{20... | collective-permute-start | bytes 3145736 | tf_op jit(solution)/shard_map/ppermute | solution.py:15
  170.2 20.9 %collective-permute-start.48 = (bf16[64,2048]{1,0:T(8,128)(2,1)S(1)}, bf16[64,2048]{1,0:T(8,128)(2,1)S(1)}, u32[]{:S(2)}, u32[]{:S(2)}) collective-permute-start(bf16[64,2048]{1,0:T(8,128)(2,1)S(1)} %add_convert_fusion.1), channel_id=1, source_target_pairs={{2,4},{3,5},{4,2},{5,3},{10,12},{11,13},{12,10},{13,11},{18,20},{1... | collective-permute-start | bytes 786440 | tf_op jit(solution)/shard_map/ppermute | solution.py:20
  170.9 23.5 %collective-permute-start.45 = (bf16[64,2048]{1,0:T(8,128)(2,1)S(1)}, bf16[64,2048]{1,0:T(8,128)(2,1)S(1)}, u32[]{:S(2)}, u32[]{:S(2)}) collective-permute-start(bf16[64,2048]{1,0:T(8,128)(2,1)S(1)} %add_convert_fusion.2), channel_id=1, source_target_pairs={{0,2},{1,3},{2,0},{3,1},{4,6},{5,7},{6,4},{7,5},{8,10},{9,11},{10,... | collective-permute-start | bytes 786440 | tf_op jit(solution)/shard_map/ppermute | solution.py:20
  190.1 6.3 %collective-permute-start.39 = (bf16[64,2048]{1,0:T(8,128)(2,1)S(1)}, bf16[64,2048]{1,0:T(8,128)(2,1)S(1)}, u32[]{:S(2)}, u32[]{:S(2)}) collective-permute-start(bf16[64,2048]{1,0:T(8,128)(2,1)S(1)} %add_convert_fusion.5), channel_id=1, source_target_pairs={{2,4},{3,5},{4,2},{5,3},{10,12},{11,13},{12,10},{13,11},{18,20},{1... | collective-permute-start | bytes 786440 | tf_op jit(solution)/shard_map/ppermute | solution.py:20
  191.1 11.3 %collective-permute-start.50 = (bf16[64,4096]{1,0:T(8,128)(2,1)}, bf16[64,4096]{1,0:T(8,128)(2,1)S(1)}, u32[]{:S(2)}, u32[]{:S(2)}) collective-permute-start(bf16[64,4096]{1,0:T(8,128)(2,1)} %collective-permute-done.49), channel_id=1, source_target_pairs={{0,1},{1,0},{2,3},{3,2},{4,5},{5,4},{6,7},{7,6},{8,9},{9,8},{10,11... | collective-permute-start | bytes 1572872 | tf_op jit(solution)/shard_map/ppermute | solution.py:15
  194.4 7.0 %collective-permute-start.36 = (bf16[64,2048]{1,0:T(8,128)(2,1)S(1)}, bf16[64,2048]{1,0:T(8,128)(2,1)S(1)}, u32[]{:S(2)}, u32[]{:S(2)}) collective-permute-start(bf16[64,2048]{1,0:T(8,128)(2,1)S(1)} %add_convert_fusion.6), channel_id=1, source_target_pairs={{0,2},{1,3},{2,0},{3,1},{4,6},{5,7},{6,4},{7,5},{8,10},{9,11},{10,... | collective-permute-start | bytes 786440 | tf_op jit(solution)/shard_map/ppermute | solution.py:20
  196.3 8.2 %collective-permute-start.56 = (bf16[32,4096]{1,0:T(8,128)(2,1)S(1)}, bf16[32,4096]{1,0:T(8,128)(2,1)S(1)}, u32[]{:S(2)}, u32[]{:S(2)}) collective-permute-start(bf16[32,4096]{1,0:T(8,128)(2,1)S(1)} %collective-permute-done.55), channel_id=1, source_target_pairs={{0,1},{1,0},{2,3},{3,2},{4,5},{5,4},{6,7},{7,6},{8,9},{9,8},{10,11... | collective-permute-start | bytes 786440 | tf_op jit(solution)/shard_map/ppermute | solution.py:15
  196.4 8.4 %collective-permute-start.58 = (bf16[32,4096]{1,0:T(8,128)(2,1)S(1)}, bf16[32,4096]{1,0:T(8,128)(2,1)S(1)}, u32[]{:S(2)}, u32[]{:S(2)}) collective-permute-start(bf16[32,4096]{1,0:T(8,128)(2,1)S(1)} %collective-permute-done.57), channel_id=1, source_target_pairs={{0,1},{1,0},{2,3},{3,2},{4,5},{5,4},{6,7},{7,6},{8,9},{9,8},{10,11... | collective-permute-start | bytes 786440 | tf_op jit(solution)/shard_map/ppermute | solution.py:15
  202.4 2.0 collective-permute-start.54
  (36 other events, 257.5 us)

commit v2 on v1

--- a/solution.py
+++ b/solution.py
@@ -36,10 +36,12 @@
     return narrow(wide(first) + wide(second))
 
 
-def in_order(own, other, core):
-    first = jnp.where(core == 0, own, other)
-    second = jnp.where(core == 0, other, own)
-    return jnp.concatenate([first, second], axis=0)
+def ordered(own, other, side):
+    return [jnp.where(side == 0, own, other), jnp.where(side == 0, other, own)]
+
+
+def in_order(own, other, side):
+    return jnp.concatenate(ordered(own, other, side), axis=0)
 
 
 OUTER_PAIRS = [(0, 1), (1, 0), (2, 3), (3, 2)]
@@ -60,17 +62,31 @@
     width = weight.shape[1]
     line = columns == 8
 
+    def product(pieces):
+        return narrow(
+            jnp.dot(
+                jnp.concatenate(pieces, axis=0),
+                weight,
+                preferred_element_type=jnp.float32,
+            )
+        )
+
     if line:
-        own = in_order(local, swap(local, "col", 1), core)
-        own_part = narrow(
-            jnp.dot(own, weight, preferred_element_type=jnp.float32)
-        )
+        own = ordered(local, swap(local, "col", 1), core)
+        own_part = product(own)
         halves = jnp.split(local, 2, axis=0)
-        middle = [chip_moves(part, MIDDLE) for part in halves]
-        near = [chip_moves(part, OUTER_PAIRS) for part in halves]
-        across = [chip_moves(after(part, own_part), MIDDLE) for part in near]
-        outward = [chip_moves(after(part, own_part), OUTWARD) for part in middle]
-        last = [chip_moves(part, OUTWARD) for part in across]
+        middle, near, outward, across, last = [], [], [], [], []
+        for part in halves:
+            middle.append(chip_moves(part, MIDDLE))
+            near.append(chip_moves(part, OUTER_PAIRS))
+        for at in range(2):
+            held = after(middle[at], own_part)
+            outward.append(chip_moves(held, OUTWARD))
+        for at in range(2):
+            held = after(near[at], own_part)
+            across.append(chip_moves(held, MIDDLE))
+        for at in range(2):
+            last.append(chip_moves(across[at], OUTWARD))
         low = chip < 2
         chips = [
             chip,
@@ -106,16 +122,18 @@
             if at >= 1:
                 newest = after(newest, parts[at - 1])
             if at >= 2:
-                newest = after(newest, sent[at - 2])
+                newest = after(newest, sent[min(at - 2, 1)])
             merged.append(piece[0] + newest if len(piece) == 2 else newest)
         stream = jnp.concatenate(merged, axis=0) if len(merged) > 1 else merged[0]
         streams.append(stream)
         if line and at == 0:
             block, part = own, own_part
         else:
-            block = in_order(stream, swap(stream, "col", 1), core) if line else stream
-            part = narrow(jnp.dot(block, weight, preferred_element_type=jnp.float32))
-        own_blocks.append(block)
+            block = [stream]
+            if line:
+                block = ordered(stream, swap(stream, "col", 1), core)
+            part = product(block)
+        own_blocks += block
         parts.append(part)
         total = wide(parts[at])
         distance = 1
@@ -212,7 +230,7 @@
             slope = lax.dynamic_slice(dpre, (starts[at], 0), (2 * share, width))
             for side in range(sides):
                 sums[at][side] = chip_sum(slope, side)
-        results = []
+        results, late = [], []
         first_out = narrow(sums[3][0])
         for side in range(sides):
             far = sums[3][side]
@@ -223,26 +241,26 @@
             mid_across = chip_moves(narrow(mid + wide(mid_in)), MIDDLE)
             close = sums[1][side] + wide(far_across)
             closed = chip_moves(narrow(close), OUTER_PAIRS)
-            late = far_across
+            late.append(far_across)
             results.append(narrow(sums[0][side] + wide(closed) + wide(mid_across)))
         grad_hidden = jnp.concatenate(results, axis=1)
     else:
         grad_hidden = lax.psum_scatter(
             back(dpre, 0, 1), "col", scatter_dimension=0, tiled=True
         )
-        first_out = late = grad_hidden
+        first_out, late = grad_hidden, [grad_hidden] * 2
 
     dpre_other = swap(after(dpre, first_out), "view", 1)
-    clips = [after(block, late) for block in own_blocks]
+    clips = [after(block, late[0]) for block in own_blocks]
     slopes = [
         lax.dynamic_slice(dpre, (start, 0), (size, width))
         for place in places
         for start, size in place
     ]
     for at, stream in enumerate(streams):
-        stream = after(stream, parts[0] if at == 0 else begun)
+        if at >= 2:
+            stream = after(stream, begun)
         got = swap(stream, "view", 1)
-        got = after(got, late)
         if line:
             clips += [got, swap(got, "col", 1)]
             (first, size), (second, _) = places[at]

time: 217 us -> 237 us (1.092)
  the two profiles are of different devices: /device:TPU:0 before, /device:TPU:16 now
where the time goes in v2:
time: 237 us; the launch traced here: 236 us
  waiting for transfers between devices  108 us (46%)
  starting transfers between devices  62.8 us (26%)
  matrix products  43 us (18%)
  other arithmetic  10.9 us (5%)
  local copies, waits for them, and re-layouts  9.08 us (4%)
    ppermute x20, waiting for transfers between devices, chip_moves(): return lax.ppermute(block, 'col', route)  69.8 us
    ppermute x40, waiting for transfers between devices, swap(): lax.ppermute(block, axis, [(at, at ^ distance) for at in range(count)])  38.4 us
    ppermute x20, starting transfers between devices, chip_moves(): return lax.ppermute(block, 'col', route)  36.2 us
    ppermute x40, starting transfers between devices, swap(): lax.ppermute(block, axis, [(at, at ^ distance) for at in range(count)])  26.5 us
    dot_general x8, matrix products, back(): lax.dot_general(slope, weight[side * tall:(side + 1) * tall], (((1,), (1,...  14.8 us
    dot_general x5, matrix products, product(): jnp.dot(jnp.concatenate(pieces, axis=0), weight, preferred_element_type=j...  14.8 us
    dot_general x1, matrix products, shards(): lax.dot_general(clips, slopes, (((0,), (0,)), ((), ())), preferred_elemen...  11.8 us
  transfers between devices with their start and end apart: 60, of which 32 were waited for; matrix products, arithmetic and copies ran while one was open for 18% of the time, Pallas kernels for 0%

profile of v2, /device:TPU:16, one launch (start us, length us, event | category | flops | bytes accessed | tf_op | source)
XLA Modules:
  0.0 236.2 jit_solution(4954399609145214146)
XLA Ops:
  1.8 1.6 collective-permute-start.2
  5.0 5.1 %convolution_convert_fusion.2 = bf16[128,1024]{1,0:T(8,128)(2,1)S(1)} fusion(bf16[4096,1024]{1,0:T(8,128)(2,1)} %param.3, bf16[64,4096]{1,0:T(8,128)(2,1)S(1)} %get-tuple-element.49, bf16[64,4096]{1,0:T(8,128)(2,1)S(1)} %get-tuple-element.48), kind=kOutput, calls=%fused_computation.48 | convolution fusion | flops 1075970048 | bytes 9699328 | tf_op jit(solution)/shard_map/dot_general | solution.py:67
  10.1 6.0 %collective-permute-done.3 = bf16[32,4096]{1,0:T(8,128)(2,1)S(1)} collective-permute-done((bf16[32,4096]{1,0:T(8,128)(2,1)S(1)}, bf16[32,4096]{1,0:T(8,128)(2,1)S(1)}, u32[]{:S(2)}, u32[]{:S(2)}) %collective-permute-start.3) | collective-permute-done | bytes 262176 | tf_op jit(solution)/shard_map/ppermute | solution.py:20
  17.6 2.3 collective-permute-start.8
  20.0 3.5 %collective-permute-start.6 = (bf16[32,4096]{1,0:T(8,128)(2,1)S(1)}, bf16[32,4096]{1,0:T(8,128)(2,1)S(1)}, u32[]{:S(2)}, u32[]{:S(2)}) collective-permute-start(bf16[32,4096]{1,0:T(8,128)(2,1)S(1)} %get-tuple-element.85), channel_id=1, source_target_pairs={{2,4},{3,5},{4,2},{5,3},{10,12},{11,13},{12,10},{13,11},{18,20},{1... | collective-permute-start | bytes 786440 | tf_op jit(solution)/shard_map/ppermute | solution.py:20
  23.5 1.6 collective-permute-start.1
  25.0 2.3 collective-permute-start.12
  28.7 2.3 collective-permute-start.16
  31.0 3.3 %collective-permute-done.6 = bf16[32,4096]{1,0:T(8,128)(2,1)S(1)} collective-permute-done((bf16[32,4096]{1,0:T(8,128)(2,1)S(1)}, bf16[32,4096]{1,0:T(8,128)(2,1)S(1)}, u32[]{:S(2)}, u32[]{:S(2)}) %collective-permute-start.6) | collective-permute-done | bytes 262176 | tf_op jit(solution)/shard_map/ppermute | solution.py:20
  37.0 1.6 collective-permute-start.20
  39.9 5.2 %convolution_convert_fusion.1 = bf16[128,1024]{1,0:T(8,128)(2,1)S(1)} fusion(bf16[4096,1024]{1,0:T(8,128)(2,1)} %param.3, bf16[64,4096]{1,0:T(8,128)(2,1)S(1)} %get-tuple-element.51, bf16[64,4096]{1,0:T(8,128)(2,1)S(1)} %get-tuple-element.50), kind=kOutput, calls=%fused_computation.47 | convolution fusion | flops 1075970048 | bytes 9699328 | tf_op jit(solution)/shard_map/dot_general | solution.py:67
  49.1 4.4 %collective-permute-start.13 = (bf16[32,4096]{1,0:T(8,128)(2,1)S(1)}, bf16[32,4096]{1,0:T(8,128)(2,1)S(1)}, u32[]{:S(2)}, u32[]{:S(2)}) collective-permute-start(bf16[32,4096]{1,0:T(8,128)(2,1)S(1)} %collective-permute-done.12), channel_id=1, source_target_pairs={{2,0},{3,1},{4,6},{5,7},{10,8},{11,9},{12,14},{13,15},{18,16},{19,... | collective-permute-start | bytes 786440 | tf_op jit(solution)/shard_map/ppermute | solution.py:20
  55.2 1.6 collective-permute-start.21
  58.3 1.9 collective-permute-done.13
  63.7 1.6 convolution_convert_fusion.4
  66.1 4.1 %collective-permute-done.11 = bf16[128,1024]{1,0:T(8,128)(2,1)S(1)} collective-permute-done((bf16[128,1024]{1,0:T(8,128)(2,1)S(1)}, bf16[128,1024]{1,0:T(8,128)(2,1)S(1)}, u32[]{:S(2)}, u32[]{:S(2)}) %collective-permute-start.11) | collective-permute-done | bytes 262176 | tf_op jit(solution)/shard_map/ppermute | solution.py:15
  70.4 1.6 collective-permute-start.22
  72.7 1.6 collective-permute-start.23
  74.4 1.6 convolution_convert_fusion.3
  76.6 2.6 %collective-permute-done.22 = bf16[128,1024]{1,0:T(8,128)(2,1)S(1)} collective-permute-done((bf16[128,1024]{1,0:T(8,128)(2,1)S(1)}, bf16[128,1024]{1,0:T(8,128)(2,1)S(1)}, u32[]{:S(2)}, u32[]{:S(2)}) %collective-permute-start.22) | collective-permute-done | bytes 262176 | tf_op jit(solution)/shard_map/ppermute | solution.py:15
  82.8 3.4 %collective-permute-done.24 = bf16[64,1024]{1,0:T(8,128)(2,1)} collective-permute-done((bf16[64,1024]{1,0:T(8,128)(2,1)S(1)}, bf16[64,1024]{1,0:T(8,128)(2,1)}, u32[]{:S(2)}, u32[]{:S(2)}) %collective-permute-start.24) | collective-permute-done | bytes 131104 | tf_op jit(solution)/shard_map/ppermute | solution.py:15
  88.4 1.5 fusion.47
  92.9 2.6 %collective-permute-start.26 = (bf16[128,512]{1,0:T(8,128)(2,1)S(1)}, bf16[128,512]{1,0:T(8,128)(2,1)S(1)}, u32[]{:S(2)}, u32[]{:S(2)}) collective-permute-start(bf16[128,512]{1,0:T(8,128)(2,1)S(1)} %add_convert_fusion.10), channel_id=1, source_target_pairs={{0,2},{1,3},{2,0},{3,1},{4,6},{5,7},{6,4},{7,5},{8,10},{9,11},{10,... | collective-permute-start | bytes 393224 | tf_op jit(solution)/shard_map/ppermute | solution.py:15
  95.5 3.8 %collective-permute-done.26 = bf16[128,512]{1,0:T(8,128)(2,1)S(1)} collective-permute-done((bf16[128,512]{1,0:T(8,128)(2,1)S(1)}, bf16[128,512]{1,0:T(8,128)(2,1)S(1)}, u32[]{:S(2)}, u32[]{:S(2)}) %collective-permute-start.26) | collective-permute-done | bytes 131104 | tf_op jit(solution)/shard_map/ppermute | solution.py:15
  99.3 1.7 collective-permute-start.27
  103.0 3.0 %collective-permute-done.27 = bf16[128,512]{1,0:T(8,128)(2,1)S(1)} collective-permute-done((bf16[128,512]{1,0:T(8,128)(2,1)S(1)}, bf16[128,512]{1,0:T(8,128)(2,1)S(1)}, u32[]{:S(2)}, u32[]{:S(2)}) %collective-permute-start.27) | collective-permute-done | bytes 131104 | tf_op jit(solution)/shard_map/ppermute | solution.py:15
  107.8 3.7 %collective-permute-done.29 = bf16[128,512]{1,0:T(8,128)(2,1)S(1)} collective-permute-done((bf16[128,512]{1,0:T(8,128)(2,1)S(1)}, bf16[128,512]{1,0:T(8,128)(2,1)S(1)}, u32[]{:S(2)}, u32[]{:S(2)}) %collective-permute-start.29) | collective-permute-done | bytes 131104 | tf_op jit(solution)/shard_map/ppermute | solution.py:15
  115.8 4.0 %fusion.36 = bf16[128,2048]{1,0:T(8,128)(2,1)S(1)} fusion(bf16[4096,1024]{1,0:T(8,128)(2,1)} %param.3, bf16[512,1024]{1,0:T(8,128)(2,1)S(1)} %fusion.51, s32[]{:T(128)S(6)} %select_n.266), kind=kOutput, calls=%fused_computation.32 | convolution fusion | flops 537133056 | bytes 4980740 | tf_op jit(solution)/shard_map/dot_general | solution.py:209
  121.3 1.7 fusion.27
  123.1 1.5 fusion.24
  124.6 1.5 fusion.30
  126.1 1.5 fusion.33
  129.2 1.5 fusion.18
  138.4 10.0 %collective-permute-done.43 = bf16[64,2048]{1,0:T(8,128)(2,1)S(1)} collective-permute-done((bf16[64,2048]{1,0:T(8,128)(2,1)S(1)}, bf16[64,2048]{1,0:T(8,128)(2,1)S(1)}, u32[]{:S(2)}, u32[]{:S(2)}) %collective-permute-start.43) | collective-permute-done | bytes 262176 | tf_op jit(solution)/shard_map/ppermute | solution.py:20
  149.9 8.3 %collective-permute-done.47 = bf16[64,2048]{1,0:T(8,128)(2,1)S(1)} collective-permute-done((bf16[64,2048]{1,0:T(8,128)(2,1)S(1)}, bf16[64,2048]{1,0:T(8,128)(2,1)S(1)}, u32[]{:S(2)}, u32[]{:S(2)}) %collective-permute-start.47) | collective-permute-done | bytes 262176 | tf_op jit(solution)/shard_map/ppermute | solution.py:20
  159.5 7.4 %collective-permute-done.34 = bf16[64,2048]{1,0:T(8,128)(2,1)S(1)} collective-permute-done((bf16[64,2048]{1,0:T(8,128)(2,1)S(1)}, bf16[64,2048]{1,0:T(8,128)(2,1)S(1)}, u32[]{:S(2)}, u32[]{:S(2)}) %collective-permute-start.34) | collective-permute-done | bytes 262176 | tf_op jit(solution)/shard_map/ppermute | solution.py:20
  169.3 5.9 %collective-permute-done.38 = bf16[64,2048]{1,0:T(8,128)(2,1)S(1)} collective-permute-done((bf16[64,2048]{1,0:T(8,128)(2,1)S(1)}, bf16[64,2048]{1,0:T(8,128)(2,1)S(1)}, u32[]{:S(2)}, u32[]{:S(2)}) %collective-permute-start.38) | collective-permute-done | bytes 262176 | tf_op jit(solution)/shard_map/ppermute | solution.py:20
  175.2 1.9 collective-permute-start.35
  178.3 5.1 %collective-permute-done.35 = bf16[64,2048]{1,0:T(8,128)(2,1)S(1)} collective-permute-done((bf16[64,2048]{1,0:T(8,128)(2,1)S(1)}, bf16[64,2048]{1,0:T(8,128)(2,1)S(1)}, u32[]{:S(2)}, u32[]{:S(2)}) %collective-permute-start.35) | collective-permute-done | bytes 262176 | tf_op jit(solution)/shard_map/ppermute | solution.py:20
  188.1 1.9 collective-permute-start.44
  190.4 8.0 %collective-permute-done.44 = bf16[64,2048]{1,0:T(8,128)(2,1)S(1)} collective-permute-done((bf16[64,2048]{1,0:T(8,128)(2,1)S(1)}, bf16[64,2048]{1,0:T(8,128)(2,1)S(1)}, u32[]{:S(2)}, u32[]{:S(2)}) %collective-permute-start.44) | collective-permute-done | bytes 262176 | tf_op jit(solution)/shard_map/ppermute | solution.py:20
  199.5 2.2 collective-permute-start.48
  201.9 3.9 %collective-permute-start.39 = (bf16[64,2048]{1,0:T(8,128)(2,1)S(1)}, bf16[64,2048]{1,0:T(8,128)(2,1)S(1)}, u32[]{:S(2)}, u32[]{:S(2)}) collective-permute-start(bf16[64,2048]{1,0:T(8,128)(2,1)S(1)} %add_convert_fusion.5), channel_id=1, source_target_pairs={{2,4},{3,5},{4,2},{5,3},{10,12},{11,13},{12,10},{13,11},{18,20},{1... | collective-permute-start | bytes 786440 | tf_op jit(solution)/shard_map/ppermute | solution.py:20
  205.8 4.8 %collective-permute-done.48 = bf16[64,2048]{1,0:T(8,128)(2,1)S(1)} collective-permute-done((bf16[64,2048]{1,0:T(8,128)(2,1)S(1)}, bf16[64,2048]{1,0:T(8,128)(2,1)S(1)}, u32[]{:S(2)}, u32[]{:S(2)}) %collective-permute-start.48) | collective-permute-done | bytes 262176 | tf_op jit(solution)/shard_map/ppermute | solution.py:20
  210.8 4.7 %collective-permute-done.39 = bf16[64,2048]{1,0:T(8,128)(2,1)S(1)} collective-permute-done((bf16[64,2048]{1,0:T(8,128)(2,1)S(1)}, bf16[64,2048]{1,0:T(8,128)(2,1)S(1)}, u32[]{:S(2)}, u32[]{:S(2)}) %collective-permute-start.39) | collective-permute-done | bytes 262176 | tf_op jit(solution)/shard_map/ppermute | solution.py:20
  215.5 2.0 collective-permute-done.36
  218.4 5.7 %collective-permute-done.59 = bf16[512,1024]{1,0:T(8,128)(2,1)S(1)} collective-permute-done((bf16[512,1024]{1,0:T(8,128)(2,1)S(1)}, bf16[512,1024]{1,0:T(8,128)(2,1)S(1)}, u32[]{:S(2)}, u32[]{:S(2)}) %collective-permute-start.59) | collective-permute-done | bytes 1048608 | tf_op jit(solution)/shard_map/ppermute | solution.py:15
  224.4 11.8 %convolution_multiply_fusion = f32[4096,1024]{1,0:T(8,128)} fusion(bf16[1024,4096]{1,0:T(8,128)(2,1)S(1)} %constant_dynamic-update-slice_fusion.2, bf16[1024,1024]{1,0:T(8,128)(2,1)S(1)} %constant_dynamic-update-slice_fusion.22), kind=kOutput, calls=%fused_computation | convolution fusion | flops 8594128896 | bytes 27262976 | tf_op jit(solution)/shard_map/dot_general | solution.py:278
  (265 shorter events, 63.1 us)
Async XLA Ops:
  1.8 14.4 %collective-permute-start.2 = (bf16[32,4096]{1,0:T(8,128)(2,1)S(1)}, bf16[32,4096]{1,0:T(8,128)(2,1)S(1)}, u32[]{:S(2)}, u32[]{:S(2)}) collective-permute-start(bf16[32,4096]{1,0:T(8,128)(2,1)S(1)} %get-tuple-element.85), channel_id=1, source_target_pairs={{0,2},{1,3},{2,0},{3,1},{4,6},{5,7},{6,4},{7,5},{8,10},{9,11},{10,... | collective-permute-start | bytes 786440 | tf_op jit(solution)/shard_map/ppermute | solution.py:20
  3.4 12.7 %collective-permute-start.3 = (bf16[32,4096]{1,0:T(8,128)(2,1)S(1)}, bf16[32,4096]{1,0:T(8,128)(2,1)S(1)}, u32[]{:S(2)}, u32[]{:S(2)}) collective-permute-start(bf16[32,4096]{1,0:T(8,128)(2,1)S(1)} %get-tuple-element.86), channel_id=1, source_target_pairs={{0,2},{1,3},{2,0},{3,1},{4,6},{5,7},{6,4},{7,5},{8,10},{9,11},{10,... | collective-permute-start | bytes 786440 | tf_op jit(solution)/shard_map/ppermute | solution.py:20
  17.6 19.4 %collective-permute-start.4 = (bf16[64,4096]{1,0:T(8,128)(2,1)}, bf16[64,4096]{1,0:T(8,128)(2,1)S(1)}, u32[]{:S(2)}, u32[]{:S(2)}) collective-permute-start(bf16[64,4096]{1,0:T(8,128)(2,1)} %constant_dynamic-update-slice_fusion), channel_id=1, source_target_pairs={{0,1},{1,0},{2,3},{3,2},{4,5},{5,4},{6,7},{7,6},{8,9},{9,8},{10,11... | collective-permute-start | bytes 1572872 | tf_op jit(solution)/shard_map/ppermute | solution.py:15
  17.6 11.1 %collective-permute-start.8 = (bf16[32,4096]{1,0:T(8,128)(2,1)S(1)}, bf16[32,4096]{1,0:T(8,128)(2,1)S(1)}, u32[]{:S(2)}, u32[]{:S(2)}) collective-permute-start(bf16[32,4096]{1,0:T(8,128)(2,1)S(1)} %get-tuple-element.86), channel_id=1, source_target_pairs={{2,4},{3,5},{4,2},{5,3},{10,12},{11,13},{12,10},{13,11},{18,20},{1... | collective-permute-start | bytes 786440 | tf_op jit(solution)/shard_map/ppermute | solution.py:20
  20.0 14.3 %collective-permute-start.6 = (bf16[32,4096]{1,0:T(8,128)(2,1)S(1)}, bf16[32,4096]{1,0:T(8,128)(2,1)S(1)}, u32[]{:S(2)}, u32[]{:S(2)}) collective-permute-start(bf16[32,4096]{1,0:T(8,128)(2,1)S(1)} %get-tuple-element.85), channel_id=1, source_target_pairs={{2,4},{3,5},{4,2},{5,3},{10,12},{11,13},{12,10},{13,11},{18,20},{1... | collective-permute-start | bytes 786440 | tf_op jit(solution)/shard_map/ppermute | solution.py:20
  23.5 12.1 %collective-permute-start.1 = (bf16[128,1024]{1,0:T(8,128)(2,1)S(1)}, bf16[128,1024]{1,0:T(8,128)(2,1)S(1)}, u32[]{:S(2)}, u32[]{:S(2)}) collective-permute-start(bf16[128,1024]{1,0:T(8,128)(2,1)S(1)} %convolution_convert_fusion.2), channel_id=1, source_target_pairs={{0,8},{8,0},{1,9},{9,1},{2,10},{10,2},{3,11},{11,3},{4,12},{12,4},... | collective-permute-start | bytes 786440 | tf_op jit(solution)/shard_map/ppermute | solution.py:15
  25.0 24.1 %collective-permute-start.12 = (bf16[32,4096]{1,0:T(8,128)(2,1)S(1)}, bf16[32,4096]{1,0:T(8,128)(2,1)S(1)}, u32[]{:S(2)}, u32[]{:S(2)}) collective-permute-start(bf16[32,4096]{1,0:T(8,128)(2,1)S(1)} %collective-permute-done.2), channel_id=1, source_target_pairs={{2,4},{3,5},{4,2},{5,3},{10,12},{11,13},{12,10},{13,11},{18,20},{1... | collective-permute-start | bytes 786440 | tf_op jit(solution)/shard_map/ppermute | solution.py:20
  28.7 24.9 %collective-permute-start.16 = (bf16[32,4096]{1,0:T(8,128)(2,1)S(1)}, bf16[32,4096]{1,0:T(8,128)(2,1)S(1)}, u32[]{:S(2)}, u32[]{:S(2)}) collective-permute-start(bf16[32,4096]{1,0:T(8,128)(2,1)S(1)} %collective-permute-done.3), channel_id=1, source_target_pairs={{2,4},{3,5},{4,2},{5,3},{10,12},{11,13},{12,10},{13,11},{18,20},{1... | collective-permute-start | bytes 786440 | tf_op jit(solution)/shard_map/ppermute | solution.py:20
  34.3 13.6 %collective-permute-start.7 = (bf16[32,4096]{1,0:T(8,128)(2,1)S(1)}, bf16[32,4096]{1,0:T(8,128)(2,1)S(1)}, u32[]{:S(2)}, u32[]{:S(2)}) collective-permute-start(bf16[32,4096]{1,0:T(8,128)(2,1)S(1)} %collective-permute-done.6), channel_id=1, source_target_pairs={{2,0},{3,1},{4,6},{5,7},{10,8},{11,9},{12,14},{13,15},{18,16},{19,... | collective-permute-start | bytes 786440 | tf_op jit(solution)/shard_map/ppermute | solution.py:20
  35.6 10.8 %collective-permute-start.9 = (bf16[32,4096]{1,0:T(8,128)(2,1)S(1)}, bf16[32,4096]{1,0:T(8,128)(2,1)S(1)}, u32[]{:S(2)}, u32[]{:S(2)}) collective-permute-start(bf16[32,4096]{1,0:T(8,128)(2,1)S(1)} %collective-permute-done.8), channel_id=1, source_target_pairs={{2,0},{3,1},{4,6},{5,7},{10,8},{11,9},{12,14},{13,15},{18,16},{19,... | collective-permute-start | bytes 786440 | tf_op jit(solution)/shard_map/ppermute | solution.py:20
  37.0 39.6 %collective-permute-start.20 = (bf16[128,1024]{1,0:T(8,128)(2,1)S(1)}, bf16[128,1024]{1,0:T(8,128)(2,1)S(1)}, u32[]{:S(2)}, u32[]{:S(2)}) collective-permute-start(bf16[128,1024]{1,0:T(8,128)(2,1)S(1)} %get-tuple-element.80), channel_id=1, source_target_pairs={{0,16},{16,0},{1,17},{17,1},{2,18},{18,2},{3,19},{19,3},{4,20},{20... | collective-permute-start | bytes 786440 | tf_op jit(solution)/shard_map/ppermute | solution.py:15
  46.4 8.7 %collective-permute-start.5 = (bf16[128,1024]{1,0:T(8,128)(2,1)S(1)}, bf16[128,1024]{1,0:T(8,128)(2,1)S(1)}, u32[]{:S(2)}, u32[]{:S(2)}) collective-permute-start(bf16[128,1024]{1,0:T(8,128)(2,1)S(1)} %convolution_convert_fusion.1), channel_id=1, source_target_pairs={{0,8},{8,0},{1,9},{9,1},{2,10},{10,2},{3,11},{11,3},{4,12},{12,4},... | collective-permute-start | bytes 786440 | tf_op jit(solution)/shard_map/ppermute | solution.py:15
  48.8 7.9 %collective-permute-start.10 = (bf16[64,4096]{1,0:T(8,128)(2,1)}, bf16[64,4096]{1,0:T(8,128)(2,1)S(1)}, u32[]{:S(2)}, u32[]{:S(2)}) collective-permute-start(bf16[64,4096]{1,0:T(8,128)(2,1)} %pad_maximum_fusion), channel_id=1, source_target_pairs={{0,1},{1,0},{2,3},{3,2},{4,5},{5,4},{6,7},{7,6},{8,9},{9,8},{10,11... | collective-permute-start | bytes 1572872 | tf_op jit(solution)/shard_map/ppermute | solution.py:15
  49.1 11.1 %collective-permute-start.13 = (bf16[32,4096]{1,0:T(8,128)(2,1)S(1)}, bf16[32,4096]{1,0:T(8,128)(2,1)S(1)}, u32[]{:S(2)}, u32[]{:S(2)}) collective-permute-start(bf16[32,4096]{1,0:T(8,128)(2,1)S(1)} %collective-permute-done.12), channel_id=1, source_target_pairs={{2,0},{3,1},{4,6},{5,7},{10,8},{11,9},{12,14},{13,15},{18,16},{19,... | collective-permute-start | bytes 786440 | tf_op jit(solution)/shard_map/ppermute | solution.py:20
  53.6 12.4 %collective-permute-start.17 = (bf16[32,4096]{1,0:T(8,128)(2,1)S(1)}, bf16[32,4096]{1,0:T(8,128)(2,1)S(1)}, u32[]{:S(2)}, u32[]{:S(2)}) collective-permute-start(bf16[32,4096]{1,0:T(8,128)(2,1)S(1)} %collective-permute-done.16), channel_id=1, source_target_pairs={{2,0},{3,1},{4,6},{5,7},{10,8},{11,9},{12,14},{13,15},{18,16},{19,... | collective-permute-start | bytes 786440 | tf_op jit(solution)/shard_map/ppermute | solution.py:20
  55.2 21.5 %collective-permute-start.21 = (bf16[128,1024]{1,0:T(8,128)(2,1)S(1)}, bf16[128,1024]{1,0:T(8,128)(2,1)S(1)}, u32[]{:S(2)}, u32[]{:S(2)}) collective-permute-start(bf16[128,1024]{1,0:T(8,128)(2,1)S(1)} %get-tuple-element.78), channel_id=1, source_target_pairs={{0,16},{16,0},{1,17},{17,1},{2,18},{18,2},{3,19},{19,3},{4,20},{20... | collective-permute-start | bytes 786440 | tf_op jit(solution)/shard_map/ppermute | solution.py:15
  61.0 9.2 %collective-permute-start.11 = (bf16[128,1024]{1,0:T(8,128)(2,1)S(1)}, bf16[128,1024]{1,0:T(8,128)(2,1)S(1)}, u32[]{:S(2)}, u32[]{:S(2)}) collective-permute-start(bf16[128,1024]{1,0:T(8,128)(2,1)S(1)} %convolution_convert_fusion), channel_id=1, source_target_pairs={{0,8},{8,0},{1,9},{9,1},{2,10},{10,2},{3,11},{11,3},{4,12},{12,4},... | collective-permute-start | bytes 786440 | tf_op jit(solution)/shard_map/ppermute | solution.py:15
  65.4 7.3 %collective-permute-start.15 = (bf16[64,1024]{1,0:T(8,128)(2,1)S(1)}, bf16[64,1024]{1,0:T(8,128)(2,1)S(1)}, u32[]{:S(2)}, u32[]{:S(2)}) collective-permute-start(bf16[64,1024]{1,0:T(8,128)(2,1)S(1)} %convolution_convert_fusion.4), channel_id=1, source_target_pairs={{0,8},{8,0},{1,9},{9,1},{2,10},{10,2},{3,11},{11,3},{4,12},{12,4},... | collective-permute-start | bytes 393224 | tf_op jit(solution)/shard_map/ppermute | solution.py:15
  66.0 8.2 %collective-permute-start.18 = (bf16[32,4096]{1,0:T(8,128)(2,1)S(1)}, bf16[32,4096]{1,0:T(8,128)(2,1)S(1)}, u32[]{:S(2)}, u32[]{:S(2)}) collective-permute-start(bf16[32,4096]{1,0:T(8,128)(2,1)S(1)} %add.297), channel_id=1, source_target_pairs={{0,1},{1,0},{2,3},{3,2},{4,5},{5,4},{6,7},{7,6},{8,9},{9,8},{10,11... | collective-permute-start | bytes 786440 | tf_op jit(solution)/shard_map/ppermute | solution.py:15
  70.4 8.9 %collective-permute-start.22 = (bf16[128,1024]{1,0:T(8,128)(2,1)S(1)}, bf16[128,1024]{1,0:T(8,128)(2,1)S(1)}, u32[]{:S(2)}, u32[]{:S(2)}) collective-permute-start(bf16[128,1024]{1,0:T(8,128)(2,1)S(1)} %get-tuple-element.76), channel_id=1, source_target_pairs={{0,16},{16,0},{1,17},{17,1},{2,18},{18,2},{3,19},{19,3},{4,20},{20... | collective-permute-start | bytes 786440 | tf_op jit(solution)/shard_map/ppermute | solution.py:15
  72.7 8.0 %collective-permute-start.23 = (bf16[64,1024]{1,0:T(8,128)(2,1)S(1)}, bf16[64,1024]{1,0:T(8,128)(2,1)S(1)}, u32[]{:S(2)}, u32[]{:S(2)}) collective-permute-start(bf16[64,1024]{1,0:T(8,128)(2,1)S(1)} %get-tuple-element.94), channel_id=1, source_target_pairs={{0,16},{16,0},{1,17},{17,1},{2,18},{18,2},{3,19},{19,3},{4,20},{20... | collective-permute-start | bytes 393224 | tf_op jit(solution)/shard_map/ppermute | solution.py:15
  92.9 6.4 %collective-permute-start.26 = (bf16[128,512]{1,0:T(8,128)(2,1)S(1)}, bf16[128,512]{1,0:T(8,128)(2,1)S(1)}, u32[]{:S(2)}, u32[]{:S(2)}) collective-permute-start(bf16[128,512]{1,0:T(8,128)(2,1)S(1)} %add_convert_fusion.10), channel_id=1, source_target_pairs={{0,2},{1,3},{2,0},{3,1},{4,6},{5,7},{6,4},{7,5},{8,10},{9,11},{10,... | collective-permute-start | bytes 393224 | tf_op jit(solution)/shard_map/ppermute | solution.py:15
  99.3 6.7 %collective-permute-start.27 = (bf16[128,512]{1,0:T(8,128)(2,1)S(1)}, bf16[128,512]{1,0:T(8,128)(2,1)S(1)}, u32[]{:S(2)}, u32[]{:S(2)}) collective-permute-start(bf16[128,512]{1,0:T(8,128)(2,1)S(1)} %add_convert_fusion.9), channel_id=1, source_target_pairs={{0,4},{1,5},{2,6},{3,7},{4,0},{5,1},{6,2},{7,3},{8,12},{9,13},{10,... | collective-permute-start | bytes 393224 | tf_op jit(solution)/shard_map/ppermute | solution.py:15
  101.0 67.3 %collective-permute-start.49 = (bf16[64,4096]{1,0:T(8,128)(2,1)}, bf16[64,4096]{1,0:T(8,128)(2,1)}, u32[]{:S(2)}, u32[]{:S(2)}) collective-permute-start(bf16[64,4096]{1,0:T(8,128)(2,1)} %bitcast), channel_id=1, source_target_pairs={{0,16},{16,0},{1,17},{17,1},{2,18},{18,2},{3,19},{19,3},{4,20},{20... | collective-permute-start | bytes 1572872 | tf_op jit(solution)/shard_map/ppermute | solution.py:15
  102.1 75.1 %collective-permute-start.51 = (bf16[64,4096]{1,0:T(8,128)(2,1)}, bf16[64,4096]{1,0:T(8,128)(2,1)S(1)}, u32[]{:S(2)}, u32[]{:S(2)}) collective-permute-start(bf16[64,4096]{1,0:T(8,128)(2,1)} %constant_dynamic-update-slice_fusion), channel_id=1, source_target_pairs={{0,16},{16,0},{1,17},{17,1},{2,18},{18,2},{3,19},{19,3},{4,20},{20... | collective-permute-start | bytes 1572872 | tf_op jit(solution)/shard_map/ppermute | solution.py:15
  106.1 5.5 %collective-permute-start.29 = (bf16[128,512]{1,0:T(8,128)(2,1)S(1)}, bf16[128,512]{1,0:T(8,128)(2,1)S(1)}, u32[]{:S(2)}, u32[]{:S(2)}) collective-permute-start(bf16[128,512]{1,0:T(8,128)(2,1)S(1)} %add_convert_fusion.8), channel_id=1, source_target_pairs={{0,8},{8,0},{1,9},{9,1},{2,10},{10,2},{3,11},{11,3},{4,12},{12,4},... | collective-permute-start | bytes 393224 | tf_op jit(solution)/shard_map/ppermute | solution.py:15
  106.7 6.0 %collective-permute-start.28 = (bf16[128,512]{1,0:T(8,128)(2,1)S(1)}, bf16[128,512]{1,0:T(8,128)(2,1)S(1)}, u32[]{:S(2)}, u32[]{:S(2)}) collective-permute-start(bf16[128,512]{1,0:T(8,128)(2,1)S(1)} %add_convert_fusion.8), channel_id=1, source_target_pairs={{0,1},{1,0},{2,3},{3,2},{4,5},{5,4},{6,7},{7,6},{8,9},{9,8},{10,11... | collective-permute-start | bytes 393224 | tf_op jit(solution)/shard_map/ppermute | solution.py:15
  106.7 70.6 %collective-permute-start.55 = (bf16[32,4096]{1,0:T(8,128)(2,1)}, bf16[32,4096]{1,0:T(8,128)(2,1)S(1)}, u32[]{:S(2)}, u32[]{:S(2)}) collective-permute-start(bf16[32,4096]{1,0:T(8,128)(2,1)} %add.292), channel_id=1, source_target_pairs={{0,16},{16,0},{1,17},{17,1},{2,18},{18,2},{3,19},{19,3},{4,20},{20... | collective-permute-start | bytes 786440 | tf_op jit(solution)/shard_map/ppermute | solution.py:15
  111.6 66.3 %collective-permute-start.53 = (bf16[64,4096]{1,0:T(8,128)(2,1)}, bf16[64,4096]{1,0:T(8,128)(2,1)S(1)}, u32[]{:S(2)}, u32[]{:S(2)}) collective-permute-start(bf16[64,4096]{1,0:T(8,128)(2,1)} %pad_maximum_fusion), channel_id=1, source_target_pairs={{0,16},{16,0},{1,17},{17,1},{2,18},{18,2},{3,19},{19,3},{4,20},{20... | collective-permute-start | bytes 1572872 | tf_op jit(solution)/shard_map/ppermute | solution.py:15
  137.1 11.4 %collective-permute-start.43 = (bf16[64,2048]{1,0:T(8,128)(2,1)S(1)}, bf16[64,2048]{1,0:T(8,128)(2,1)S(1)}, u32[]{:S(2)}, u32[]{:S(2)}) collective-permute-start(bf16[64,2048]{1,0:T(8,128)(2,1)S(1)} %fusion.77), channel_id=1, source_target_pairs={{0,2},{1,3},{6,4},{7,5},{8,10},{9,11},{14,12},{15,13},{16,18},{17,... | collective-permute-start | bytes 786440 | tf_op jit(solution)/shard_map/ppermute | solution.py:20
  148.4 9.7 %collective-permute-start.47 = (bf16[64,2048]{1,0:T(8,128)(2,1)S(1)}, bf16[64,2048]{1,0:T(8,128)(2,1)S(1)}, u32[]{:S(2)}, u32[]{:S(2)}) collective-permute-start(bf16[64,2048]{1,0:T(8,128)(2,1)S(1)} %fusion.78), channel_id=1, source_target_pairs={{0,2},{1,3},{6,4},{7,5},{8,10},{9,11},{14,12},{15,13},{16,18},{17,... | collective-permute-start | bytes 786440 | tf_op jit(solution)/shard_map/ppermute | solution.py:20
  158.1 8.8 %collective-permute-start.34 = (bf16[64,2048]{1,0:T(8,128)(2,1)S(1)}, bf16[64,2048]{1,0:T(8,128)(2,1)S(1)}, u32[]{:S(2)}, u32[]{:S(2)}) collective-permute-start(bf16[64,2048]{1,0:T(8,128)(2,1)S(1)} %fusion.75), channel_id=1, source_target_pairs={{0,2},{1,3},{6,4},{7,5},{8,10},{9,11},{14,12},{15,13},{16,18},{17,... | collective-permute-start | bytes 786440 | tf_op jit(solution)/shard_map/ppermute | solution.py:20
  166.9 8.3 %collective-permute-start.38 = (bf16[64,2048]{1,0:T(8,128)(2,1)S(1)}, bf16[64,2048]{1,0:T(8,128)(2,1)S(1)}, u32[]{:S(2)}, u32[]{:S(2)}) collective-permute-start(bf16[64,2048]{1,0:T(8,128)(2,1)S(1)} %fusion.76), channel_id=1, source_target_pairs={{0,2},{1,3},{6,4},{7,5},{8,10},{9,11},{14,12},{15,13},{16,18},{17,... | collective-permute-start | bytes 786440 | tf_op jit(solution)/shard_map/ppermute | solution.py:20
  168.4 9.5 %collective-permute-start.57 = (bf16[32,4096]{1,0:T(8,128)(2,1)S(1)}, bf16[32,4096]{1,0:T(8,128)(2,1)S(1)}, u32[]{:S(2)}, u32[]{:S(2)}) collective-permute-start(bf16[32,4096]{1,0:T(8,128)(2,1)S(1)} %copy-done.20), channel_id=1, source_target_pairs={{0,16},{16,0},{1,17},{17,1},{2,18},{18,2},{3,19},{19,3},{4,20},{20... | collective-permute-start | bytes 786440 | tf_op jit(solution)/shard_map/ppermute | solution.py:15
  175.2 8.3 %collective-permute-start.35 = (bf16[64,2048]{1,0:T(8,128)(2,1)S(1)}, bf16[64,2048]{1,0:T(8,128)(2,1)S(1)}, u32[]{:S(2)}, u32[]{:S(2)}) collective-permute-start(bf16[64,2048]{1,0:T(8,128)(2,1)S(1)} %add_convert_fusion.7), channel_id=1, source_target_pairs={{2,4},{3,5},{4,2},{5,3},{10,12},{11,13},{12,10},{13,11},{18,20},{1... | collective-permute-start | bytes 786440 | tf_op jit(solution)/shard_map/ppermute | solution.py:20
  177.2 8.7 %collective-permute-start.50 = (bf16[64,4096]{1,0:T(8,128)(2,1)}, bf16[64,4096]{1,0:T(8,128)(2,1)S(1)}, u32[]{:S(2)}, u32[]{:S(2)}) collective-permute-start(bf16[64,4096]{1,0:T(8,128)(2,1)} %collective-permute-done.49), channel_id=1, source_target_pairs={{0,1},{1,0},{2,3},{3,2},{4,5},{5,4},{6,7},{7,6},{8,9},{9,8},{10,11... | collective-permute-start | bytes 1572872 | tf_op jit(solution)/shard_map/ppermute | solution.py:15
  177.3 10.8 %collective-permute-start.52 = (bf16[64,4096]{1,0:T(8,128)(2,1)S(1)}, bf16[64,4096]{1,0:T(8,128)(2,1)S(1)}, u32[]{:S(2)}, u32[]{:S(2)}) collective-permute-start(bf16[64,4096]{1,0:T(8,128)(2,1)S(1)} %collective-permute-done.51), channel_id=1, source_target_pairs={{0,1},{1,0},{2,3},{3,2},{4,5},{5,4},{6,7},{7,6},{8,9},{9,8},{10,11... | collective-permute-start | bytes 1572872 | tf_op jit(solution)/shard_map/ppermute | solution.py:15
  177.8 21.7 %collective-permute-start.56 = (bf16[32,4096]{1,0:T(8,128)(2,1)S(1)}, bf16[32,4096]{1,0:T(8,128)(2,1)S(1)}, u32[]{:S(2)}, u32[]{:S(2)}) collective-permute-start(bf16[32,4096]{1,0:T(8,128)(2,1)S(1)} %collective-permute-done.55), channel_id=1, source_target_pairs={{0,1},{1,0},{2,3},{3,2},{4,5},{5,4},{6,7},{7,6},{8,9},{9,8},{10,11... | collective-permute-start | bytes 786440 | tf_op jit(solution)/shard_map/ppermute | solution.py:15
  177.9 23.9 %collective-permute-start.58 = (bf16[32,4096]{1,0:T(8,128)(2,1)S(1)}, bf16[32,4096]{1,0:T(8,128)(2,1)S(1)}, u32[]{:S(2)}, u32[]{:S(2)}) collective-permute-start(bf16[32,4096]{1,0:T(8,128)(2,1)S(1)} %collective-permute-done.57), channel_id=1, source_target_pairs={{0,1},{1,0},{2,3},{3,2},{4,5},{5,4},{6,7},{7,6},{8,9},{9,8},{10,11... | collective-permute-start | bytes 786440 | tf_op jit(solution)/shard_map/ppermute | solution.py:15
  183.4 15.1 %collective-permute-start.54 = (bf16[64,4096]{1,0:T(8,128)(2,1)S(1)}, bf16[64,4096]{1,0:T(8,128)(2,1)S(1)}, u32[]{:S(2)}, u32[]{:S(2)}) collective-permute-start(bf16[64,4096]{1,0:T(8,128)(2,1)S(1)} %collective-permute-done.53), channel_id=1, source_target_pairs={{0,1},{1,0},{2,3},{3,2},{4,5},{5,4},{6,7},{7,6},{8,9},{9,8},{10,11... | collective-permute-start | bytes 1572872 | tf_op jit(solution)/shard_map/ppermute | solution.py:15
  188.1 10.2 %collective-permute-start.44 = (bf16[64,2048]{1,0:T(8,128)(2,1)S(1)}, bf16[64,2048]{1,0:T(8,128)(2,1)S(1)}, u32[]{:S(2)}, u32[]{:S(2)}) collective-permute-start(bf16[64,2048]{1,0:T(8,128)(2,1)S(1)} %add_convert_fusion.3), channel_id=1, source_target_pairs={{2,4},{3,5},{4,2},{5,3},{10,12},{11,13},{12,10},{13,11},{18,20},{1... | collective-permute-start | bytes 786440 | tf_op jit(solution)/shard_map/ppermute | solution.py:20
  190.2 11.8 %collective-permute-start.40 = (bf16[64,2048]{1,0:T(8,128)(2,1)S(1)}, bf16[64,2048]{1,0:T(8,128)(2,1)S(1)}, u32[]{:S(2)}, u32[]{:S(2)}) collective-permute-start(bf16[64,2048]{1,0:T(8,128)(2,1)S(1)} %constant_dynamic-slice_fusion.3), channel_id=1, source_target_pairs={{0,1},{1,0},{2,3},{3,2},{4,5},{5,4},{6,7},{7,6},{8,9},{9,8},{10,11... | collective-permute-start | bytes 786440 | tf_op jit(solution)/shard_map/ppermute | solution.py:15
  198.4 12.4 %collective-permute-start.31 = (bf16[64,2048]{1,0:T(8,128)(2,1)S(1)}, bf16[64,2048]{1,0:T(8,128)(2,1)S(1)}, u32[]{:S(2)}, u32[]{:S(2)}) collective-permute-start(bf16[64,2048]{1,0:T(8,128)(2,1)S(1)} %constant_dynamic-slice_fusion.7), channel_id=1, source_target_pairs={{0,1},{1,0},{2,3},{3,2},{4,5},{5,4},{6,7},{7,6},{8,9},{9,8},{10,11... | collective-permute-start | bytes 786440 | tf_op jit(solution)/shard_map/ppermute | solution.py:15
  198.5 25.6 %collective-permute-start.59 = (bf16[512,1024]{1,0:T(8,128)(2,1)S(1)}, bf16[512,1024]{1,0:T(8,128)(2,1)S(1)}, u32[]{:S(2)}, u32[]{:S(2)}) collective-permute-start(bf16[512,1024]{1,0:T(8,128)(2,1)S(1)} %fusion.51), channel_id=1, source_target_pairs={{0,16},{16,0},{1,17},{17,1},{2,18},{18,2},{3,19},{19,3},{4,20},{20... | collective-permute-start | bytes 3145736 | tf_op jit(solution)/shard_map/ppermute | solution.py:15
  199.5 11.1 %collective-permute-start.48 = (bf16[64,2048]{1,0:T(8,128)(2,1)S(1)}, bf16[64,2048]{1,0:T(8,128)(2,1)S(1)}, u32[]{:S(2)}, u32[]{:S(2)}) collective-permute-start(bf16[64,2048]{1,0:T(8,128)(2,1)S(1)} %add_convert_fusion.1), channel_id=1, source_target_pairs={{2,4},{3,5},{4,2},{5,3},{10,12},{11,13},{12,10},{13,11},{18,20},{1... | collective-permute-start | bytes 786440 | tf_op jit(solution)/shard_map/ppermute | solution.py:20
  201.8 8.8 %collective-permute-start.45 = (bf16[64,2048]{1,0:T(8,128)(2,1)S(1)}, bf16[64,2048]{1,0:T(8,128)(2,1)S(1)}, u32[]{:S(2)}, u32[]{:S(2)}) collective-permute-start(bf16[64,2048]{1,0:T(8,128)(2,1)S(1)} %add_convert_fusion.2), channel_id=1, source_target_pairs={{0,2},{1,3},{2,0},{3,1},{4,6},{5,7},{6,4},{7,5},{8,10},{9,11},{10,... | collective-permute-start | bytes 786440 | tf_op jit(solution)/shard_map/ppermute | solution.py:20
  201.9 13.6 %collective-permute-start.39 = (bf16[64,2048]{1,0:T(8,128)(2,1)S(1)}, bf16[64,2048]{1,0:T(8,128)(2,1)S(1)}, u32[]{:S(2)}, u32[]{:S(2)}) collective-permute-start(bf16[64,2048]{1,0:T(8,128)(2,1)S(1)} %add_convert_fusion.5), channel_id=1, source_target_pairs={{2,4},{3,5},{4,2},{5,3},{10,12},{11,13},{12,10},{13,11},{18,20},{1... | collective-permute-start | bytes 786440 | tf_op jit(solution)/shard_map/ppermute | solution.py:20
  210.6 6.8 %collective-permute-start.36 = (bf16[64,2048]{1,0:T(8,128)(2,1)S(1)}, bf16[64,2048]{1,0:T(8,128)(2,1)S(1)}, u32[]{:S(2)}, u32[]{:S(2)}) collective-permute-start(bf16[64,2048]{1,0:T(8,128)(2,1)S(1)} %add_convert_fusion.6), channel_id=1, source_target_pairs={{0,2},{1,3},{2,0},{3,1},{4,6},{5,7},{6,4},{7,5},{8,10},{9,11},{10,... | collective-permute-start | bytes 786440 | tf_op jit(solution)/shard_map/ppermute | solution.py:20
  (39 other events, 307.6 us)

commit v3 on v2

--- a/solution.py
+++ b/solution.py
@@ -36,12 +36,10 @@
     return narrow(wide(first) + wide(second))
 
 
-def ordered(own, other, side):
-    return [jnp.where(side == 0, own, other), jnp.where(side == 0, other, own)]
-
-
 def in_order(own, other, side):
-    return jnp.concatenate(ordered(own, other, side), axis=0)
+    first = jnp.where(side == 0, own, other)
+    second = jnp.where(side == 0, other, own)
+    return jnp.concatenate([first, second], axis=0)
 
 
 OUTER_PAIRS = [(0, 1), (1, 0), (2, 3), (3, 2)]
@@ -62,17 +60,11 @@
     width = weight.shape[1]
     line = columns == 8
 
-    def product(pieces):
-        return narrow(
-            jnp.dot(
-                jnp.concatenate(pieces, axis=0),
-                weight,
-                preferred_element_type=jnp.float32,
-            )
-        )
+    def product(block):
+        return narrow(jnp.dot(block, weight, preferred_element_type=jnp.float32))
 
     if line:
-        own = ordered(local, swap(local, "col", 1), core)
+        own = in_order(local, swap(local, "col", 1), core)
         own_part = product(own)
         halves = jnp.split(local, 2, axis=0)
         middle, near, outward, across, last = [], [], [], [], []
@@ -129,11 +121,11 @@
         if line and at == 0:
             block, part = own, own_part
         else:
-            block = [stream]
+            block = stream
             if line:
-                block = ordered(stream, swap(stream, "col", 1), core)
+                block = in_order(stream, swap(stream, "col", 1), core)
             part = product(block)
-        own_blocks += block
+        own_blocks.append(block)
         parts.append(part)
         total = wide(parts[at])
         distance = 1
@@ -231,26 +223,26 @@
             for side in range(sides):
                 sums[at][side] = chip_sum(slope, side)
         results, late = [], []
-        first_out = narrow(sums[3][0])
         for side in range(sides):
             far = sums[3][side]
             far_in = chip_moves(narrow(far), INWARD)
+            mid = sums[2][side]
+            far_in = after(far_in, narrow(mid))
             far_across = chip_moves(narrow(far + wide(far_in)), MIDDLE)
-            mid = sums[2][side]
+            late.append(far_across)
             mid_in = chip_moves(narrow(mid), INWARD)
             mid_across = chip_moves(narrow(mid + wide(mid_in)), MIDDLE)
             close = sums[1][side] + wide(far_across)
             closed = chip_moves(narrow(close), OUTER_PAIRS)
-            late.append(far_across)
             results.append(narrow(sums[0][side] + wide(closed) + wide(mid_across)))
         grad_hidden = jnp.concatenate(results, axis=1)
     else:
         grad_hidden = lax.psum_scatter(
             back(dpre, 0, 1), "col", scatter_dimension=0, tiled=True
         )
-        first_out, late = grad_hidden, [grad_hidden] * 2
-
-    dpre_other = swap(after(dpre, first_out), "view", 1)
+        late = [grad_hidden] * 2
+
+    dpre_other = after(swap(dpre, "view", 1), late[1])
     clips = [after(block, late[0]) for block in own_blocks]
     slopes = [
         lax.dynamic_slice(dpre, (start, 0), (size, width))

time: 237 us -> 238 us (level)
  the two profiles are of different devices: /device:TPU:16 before, /device:TPU:0 now
where the time goes in v3:
time: 238 us; the launch traced here: 237 us
  waiting for transfers between devices  116 us (49%)
  starting transfers between devices  63 us (26%)
  matrix products  36.2 us (15%)
  local copies, waits for them, and re-layouts  10.2 us (4%)
  other arithmetic  9.86 us (4%)
    ppermute x40, waiting for transfers between devices, swap(): lax.ppermute(block, axis, [(at, at ^ distance) for at in range(count)])  72.9 us
    ppermute x20, waiting for transfers between devices, chip_moves(): return lax.ppermute(block, 'col', route)  43.1 us
    ppermute x20, starting transfers between devices, chip_moves(): return lax.ppermute(block, 'col', route)  40.5 us
    ppermute x40, starting transfers between devices, swap(): lax.ppermute(block, axis, [(at, at ^ distance) for at in range(count)])  22.5 us
    dot_general x8, matrix products, back(): lax.dot_general(slope, weight[side * tall:(side + 1) * tall], (((1,), (1,...  12.3 us
    dot_general x1, matrix products, shards(): lax.dot_general(clips, slopes, (((0,), (0,)), ((), ())), preferred_elemen...  11.6 us
    dot_general x5, matrix products, product(): return narrow(jnp.dot(block, weight, preferred_element_type=jnp.float32))  10.6 us
    unnamed x78, local copies, waits for them, and re-layouts  4.87 us
  transfers between devices with their start and end apart: 60, of which 29 were waited for; matrix products, arithmetic and copies ran while one was open for 23% of the time, Pallas kernels for 0%

profile of v3, /device:TPU:0, one launch (start us, length us, event | category | flops | bytes accessed | tf_op | source)
XLA Modules:
  0.0 237.3 jit_solution(15739367523361011221)
XLA Ops:
  2.9 5.4 %collective-permute-start.2 = (bf16[32,4096]{1,0:T(8,128)(2,1)S(1)}, bf16[32,4096]{1,0:T(8,128)(2,1)S(1)}, u32[]{:S(2)}, u32[]{:S(2)}) collective-permute-start(bf16[32,4096]{1,0:T(8,128)(2,1)S(1)} %get-tuple-element.79), channel_id=1, source_target_pairs={{0,2},{1,3},{2,0},{3,1},{4,6},{5,7},{6,4},{7,5},{8,10},{9,11},{10,... | collective-permute-start | bytes 786440 | tf_op jit(solution)/shard_map/ppermute | solution.py:20
  9.1 1.8 collective-permute-start.3
  10.8 1.5 collective-permute-start.49
  13.6 4.9 %convolution_convert_fusion.2 = bf16[128,1024]{1,0:T(8,128)(2,1)S(1)} fusion(bf16[4096,1024]{1,0:T(8,128)(2,1)} %param.3, bf16[64,4096]{1,0:T(8,128)(2,1)S(1)} %get-tuple-element.66, bf16[64,4096]{1,0:T(8,128)(2,1)S(1)} %get-tuple-element.65), kind=kOutput, calls=%fused_computation.48 | convolution fusion | flops 1075970048 | bytes 9699328 | tf_op jit(solution)/shard_map/dot_general | solution.py:64
  18.5 1.6 collective-permute-start.1
  24.5 1.7 constant_dynamic-update-slice_fusion
  26.6 1.7 collective-permute-done.4
  32.0 11.1 %collective-permute-done.9 = bf16[32,4096]{1,0:T(8,128)(2,1)S(1)} collective-permute-done((bf16[32,4096]{1,0:T(8,128)(2,1)S(1)}, bf16[32,4096]{1,0:T(8,128)(2,1)S(1)}, u32[]{:S(2)}, u32[]{:S(2)}) %collective-permute-start.9) | collective-permute-done | bytes 262176 | tf_op jit(solution)/shard_map/ppermute | solution.py:20
  45.0 5.9 %collective-permute-done.5 = bf16[128,1024]{1,0:T(8,128)(2,1)S(1)} collective-permute-done((bf16[128,1024]{1,0:T(8,128)(2,1)S(1)}, bf16[128,1024]{1,0:T(8,128)(2,1)S(1)}, u32[]{:S(2)}, u32[]{:S(2)}) %collective-permute-start.5) | collective-permute-done | bytes 262176 | tf_op jit(solution)/shard_map/ppermute | solution.py:15
  50.9 1.5 collective-permute-start.51
  54.4 1.5 collective-permute-start.17
  57.4 6.7 %collective-permute-done.13 = bf16[32,4096]{1,0:T(8,128)(2,1)S(1)} collective-permute-done((bf16[32,4096]{1,0:T(8,128)(2,1)S(1)}, bf16[32,4096]{1,0:T(8,128)(2,1)S(1)}, u32[]{:S(2)}, u32[]{:S(2)}) %collective-permute-start.13) | collective-permute-done | bytes 262176 | tf_op jit(solution)/shard_map/ppermute | solution.py:20
  64.4 1.5 collective-permute-done.14
  66.4 1.6 convolution_convert_fusion.4
  68.1 1.6 collective-permute-start.21
  69.7 4.5 %collective-permute-done.11 = bf16[128,1024]{1,0:T(8,128)(2,1)S(1)} collective-permute-done((bf16[128,1024]{1,0:T(8,128)(2,1)S(1)}, bf16[128,1024]{1,0:T(8,128)(2,1)S(1)}, u32[]{:S(2)}, u32[]{:S(2)}) %collective-permute-start.11) | collective-permute-done | bytes 262176 | tf_op jit(solution)/shard_map/ppermute | solution.py:15
  74.9 4.2 %collective-permute-done.15 = bf16[64,1024]{1,0:T(8,128)(2,1)S(1)} collective-permute-done((bf16[64,1024]{1,0:T(8,128)(2,1)S(1)}, bf16[64,1024]{1,0:T(8,128)(2,1)S(1)}, u32[]{:S(2)}, u32[]{:S(2)}) %collective-permute-start.15) | collective-permute-done | bytes 131104 | tf_op jit(solution)/shard_map/ppermute | solution.py:15
  80.7 1.5 collective-permute-start.22
  82.3 1.6 convolution_convert_fusion.3
  85.0 4.8 %collective-permute-done.22 = bf16[128,1024]{1,0:T(8,128)(2,1)S(1)} collective-permute-done((bf16[128,1024]{1,0:T(8,128)(2,1)S(1)}, bf16[128,1024]{1,0:T(8,128)(2,1)S(1)}, u32[]{:S(2)}, u32[]{:S(2)}) %collective-permute-start.22) | collective-permute-done | bytes 262176 | tf_op jit(solution)/shard_map/ppermute | solution.py:15
  90.1 1.7 collective-permute-done.23
  91.9 1.6 collective-permute-start.24
  94.0 3.0 %collective-permute-done.24 = bf16[64,1024]{1,0:T(8,128)(2,1)} collective-permute-done((bf16[64,1024]{1,0:T(8,128)(2,1)S(1)}, bf16[64,1024]{1,0:T(8,128)(2,1)}, u32[]{:S(2)}, u32[]{:S(2)}) %collective-permute-start.24) | collective-permute-done | bytes 131104 | tf_op jit(solution)/shard_map/ppermute | solution.py:15
  102.0 5.5 %collective-permute-done.26 = bf16[128,512]{1,0:T(8,128)(2,1)S(1)} collective-permute-done((bf16[128,512]{1,0:T(8,128)(2,1)S(1)}, bf16[128,512]{1,0:T(8,128)(2,1)S(1)}, u32[]{:S(2)}, u32[]{:S(2)}) %collective-permute-start.26) | collective-permute-done | bytes 131104 | tf_op jit(solution)/shard_map/ppermute | solution.py:15
  108.9 7.1 %collective-permute-done.27 = bf16[128,512]{1,0:T(8,128)(2,1)S(1)} collective-permute-done((bf16[128,512]{1,0:T(8,128)(2,1)S(1)}, bf16[128,512]{1,0:T(8,128)(2,1)S(1)}, u32[]{:S(2)}, u32[]{:S(2)}) %collective-permute-start.27) | collective-permute-done | bytes 131104 | tf_op jit(solution)/shard_map/ppermute | solution.py:15
  116.7 1.6 collective-permute-start.55
  118.2 3.3 %collective-permute-done.29 = bf16[128,512]{1,0:T(8,128)(2,1)S(1)} collective-permute-done((bf16[128,512]{1,0:T(8,128)(2,1)S(1)}, bf16[128,512]{1,0:T(8,128)(2,1)S(1)}, u32[]{:S(2)}, u32[]{:S(2)}) %collective-permute-start.29) | collective-permute-done | bytes 131104 | tf_op jit(solution)/shard_map/ppermute | solution.py:15
  121.5 1.5 collective-permute-start.53
  126.7 1.5 fusion.36
  128.2 1.5 fusion.39
  129.8 1.7 fusion.27
  131.5 1.5 fusion.24
  133.0 1.5 fusion.30
  134.5 1.5 fusion.33
  136.1 1.5 fusion.21
  137.6 1.5 fusion.18
  145.4 1.6 collective-permute-start.43
  147.0 5.8 %collective-permute-done.43 = bf16[64,2048]{1,0:T(8,128)(2,1)S(1)} collective-permute-done((bf16[64,2048]{1,0:T(8,128)(2,1)S(1)}, bf16[64,2048]{1,0:T(8,128)(2,1)S(1)}, u32[]{:S(2)}, u32[]{:S(2)}) %collective-permute-start.43) | collective-permute-done | bytes 262176 | tf_op jit(solution)/shard_map/ppermute | solution.py:20
  152.8 4.4 %collective-permute-start.47 = (bf16[64,2048]{1,0:T(8,128)(2,1)S(1)}, bf16[64,2048]{1,0:T(8,128)(2,1)S(1)}, u32[]{:S(2)}, u32[]{:S(2)}) collective-permute-start(bf16[64,2048]{1,0:T(8,128)(2,1)S(1)} %fusion.63), channel_id=1, source_target_pairs={{0,2},{1,3},{6,4},{7,5},{8,10},{9,11},{14,12},{15,13},{16,18},{17,... | collective-permute-start | bytes 786440 | tf_op jit(solution)/shard_map/ppermute | solution.py:20
  157.3 4.9 %collective-permute-done.47 = bf16[64,2048]{1,0:T(8,128)(2,1)S(1)} collective-permute-done((bf16[64,2048]{1,0:T(8,128)(2,1)S(1)}, bf16[64,2048]{1,0:T(8,128)(2,1)S(1)}, u32[]{:S(2)}, u32[]{:S(2)}) %collective-permute-start.47) | collective-permute-done | bytes 262176 | tf_op jit(solution)/shard_map/ppermute | solution.py:20
  162.2 4.4 %collective-permute-start.34 = (bf16[64,2048]{1,0:T(8,128)(2,1)S(1)}, bf16[64,2048]{1,0:T(8,128)(2,1)S(1)}, u32[]{:S(2)}, u32[]{:S(2)}) collective-permute-start(bf16[64,2048]{1,0:T(8,128)(2,1)S(1)} %fusion.60), channel_id=1, source_target_pairs={{0,2},{1,3},{6,4},{7,5},{8,10},{9,11},{14,12},{15,13},{16,18},{17,... | collective-permute-start | bytes 786440 | tf_op jit(solution)/shard_map/ppermute | solution.py:20
  166.7 4.0 %collective-permute-done.34 = bf16[64,2048]{1,0:T(8,128)(2,1)S(1)} collective-permute-done((bf16[64,2048]{1,0:T(8,128)(2,1)S(1)}, bf16[64,2048]{1,0:T(8,128)(2,1)S(1)}, u32[]{:S(2)}, u32[]{:S(2)}) %collective-permute-start.34) | collective-permute-done | bytes 262176 | tf_op jit(solution)/shard_map/ppermute | solution.py:20
  170.7 4.4 %collective-permute-start.38 = (bf16[64,2048]{1,0:T(8,128)(2,1)S(1)}, bf16[64,2048]{1,0:T(8,128)(2,1)S(1)}, u32[]{:S(2)}, u32[]{:S(2)}) collective-permute-start(bf16[64,2048]{1,0:T(8,128)(2,1)S(1)} %fusion.61), channel_id=1, source_target_pairs={{0,2},{1,3},{6,4},{7,5},{8,10},{9,11},{14,12},{15,13},{16,18},{17,... | collective-permute-start | bytes 786440 | tf_op jit(solution)/shard_map/ppermute | solution.py:20
  175.8 3.1 %collective-permute-done.38 = bf16[64,2048]{1,0:T(8,128)(2,1)S(1)} collective-permute-done((bf16[64,2048]{1,0:T(8,128)(2,1)S(1)}, bf16[64,2048]{1,0:T(8,128)(2,1)S(1)}, u32[]{:S(2)}, u32[]{:S(2)}) %collective-permute-start.38) | collective-permute-done | bytes 262176 | tf_op jit(solution)/shard_map/ppermute | solution.py:20
  190.7 18.6 %collective-permute-done.59 = bf16[512,1024]{1,0:T(8,128)(2,1)S(1)} collective-permute-done((bf16[512,1024]{1,0:T(8,128)(2,1)S(1)}, bf16[512,1024]{1,0:T(8,128)(2,1)S(1)}, u32[]{:S(2)}, u32[]{:S(2)}) %collective-permute-start.59) | collective-permute-done | bytes 1048608 | tf_op jit(solution)/shard_map/ppermute | solution.py:15
  209.3 7.6 %collective-permute-start.46 = (bf16[64,2048]{1,0:T(8,128)(2,1)S(1)}, bf16[64,2048]{1,0:T(8,128)(2,1)S(1)}, u32[]{:S(2)}, u32[]{:S(2)}) collective-permute-start(bf16[64,2048]{1,0:T(8,128)(2,1)S(1)} %add_convert_fusion.2), channel_id=1, source_target_pairs={{0,2},{1,3},{2,0},{3,1},{4,6},{5,7},{6,4},{7,5},{8,10},{9,11},{10,... | collective-permute-start | bytes 786440 | tf_op jit(solution)/shard_map/ppermute | solution.py:20
  217.1 11.6 %convolution_multiply_fusion = f32[4096,1024]{1,0:T(8,128)} fusion(bf16[1024,4096]{1,0:T(8,128)(2,1)S(1)} %constant_dynamic-update-slice_fusion.2, bf16[1024,1024]{1,0:T(8,128)(2,1)S(1)} %constant_dynamic-update-slice_fusion.17), kind=kOutput, calls=%fused_computation | convolution fusion | flops 8594128896 | bytes 27262976 | tf_op jit(solution)/shard_map/dot_general | solution.py:270
  229.0 7.4 %collective-permute-done.37 = bf16[64,2048]{1,0:T(8,128)(2,1)S(1)} collective-permute-done((bf16[64,2048]{1,0:T(8,128)(2,1)S(1)}, bf16[64,2048]{1,0:T(8,128)(2,1)S(1)}, u32[]{:S(2)}, u32[]{:S(2)}) %collective-permute-start.37) | collective-permute-done | bytes 262176 | tf_op jit(solution)/shard_map/ppermute | solution.py:20
  (255 shorter events, 53.3 us)
Async XLA Ops:
  0.6 10.2 %collective-permute-start = (bf16[64,4096]{1,0:T(8,128)(2,1)}, bf16[64,4096]{1,0:T(8,128)(2,1)S(1)}, u32[]{:S(2)}, u32[]{:S(2)}) collective-permute-start(bf16[64,4096]{1,0:T(8,128)(2,1)} %bitcast.22), channel_id=1, source_target_pairs={{0,1},{1,0},{2,3},{3,2},{4,5},{5,4},{6,7},{7,6},{8,9},{9,8},{10,11... | collective-permute-start | bytes 1572872 | tf_op jit(solution)/shard_map/ppermute | solution.py:15
  2.3 17.8 %collective-permute-start.6 = (bf16[32,4096]{1,0:T(8,128)(2,1)S(1)}, bf16[32,4096]{1,0:T(8,128)(2,1)S(1)}, u32[]{:S(2)}, u32[]{:S(2)}) collective-permute-start(bf16[32,4096]{1,0:T(8,128)(2,1)S(1)} %get-tuple-element.79), channel_id=1, source_target_pairs={{2,4},{3,5},{4,2},{5,3},{10,12},{11,13},{12,10},{13,11},{18,20},{1... | collective-permute-start | bytes 786440 | tf_op jit(solution)/shard_map/ppermute | solution.py:20
  2.9 18.2 %collective-permute-start.2 = (bf16[32,4096]{1,0:T(8,128)(2,1)S(1)}, bf16[32,4096]{1,0:T(8,128)(2,1)S(1)}, u32[]{:S(2)}, u32[]{:S(2)}) collective-permute-start(bf16[32,4096]{1,0:T(8,128)(2,1)S(1)} %get-tuple-element.79), channel_id=1, source_target_pairs={{0,2},{1,3},{2,0},{3,1},{4,6},{5,7},{6,4},{7,5},{8,10},{9,11},{10,... | collective-permute-start | bytes 786440 | tf_op jit(solution)/shard_map/ppermute | solution.py:20
  8.4 10.1 %collective-permute-start.8 = (bf16[32,4096]{1,0:T(8,128)(2,1)S(1)}, bf16[32,4096]{1,0:T(8,128)(2,1)S(1)}, u32[]{:S(2)}, u32[]{:S(2)}) collective-permute-start(bf16[32,4096]{1,0:T(8,128)(2,1)S(1)} %get-tuple-element.80), channel_id=1, source_target_pairs={{2,4},{3,5},{4,2},{5,3},{10,12},{11,13},{12,10},{13,11},{18,20},{1... | collective-permute-start | bytes 786440 | tf_op jit(solution)/shard_map/ppermute | solution.py:20
  9.1 13.5 %collective-permute-start.3 = (bf16[32,4096]{1,0:T(8,128)(2,1)S(1)}, bf16[32,4096]{1,0:T(8,128)(2,1)}, u32[]{:S(2)}, u32[]{:S(2)}) collective-permute-start(bf16[32,4096]{1,0:T(8,128)(2,1)S(1)} %get-tuple-element.80), channel_id=1, source_target_pairs={{0,2},{1,3},{2,0},{3,1},{4,6},{5,7},{6,4},{7,5},{8,10},{9,11},{10,... | collective-permute-start | bytes 786440 | tf_op jit(solution)/shard_map/ppermute | solution.py:20
  10.8 164.4 %collective-permute-start.49 = (bf16[64,4096]{1,0:T(8,128)(2,1)}, bf16[64,4096]{1,0:T(8,128)(2,1)}, u32[]{:S(2)}, u32[]{:S(2)}) collective-permute-start(bf16[64,4096]{1,0:T(8,128)(2,1)} %bitcast.23), channel_id=1, source_target_pairs={{0,16},{16,0},{1,17},{17,1},{2,18},{18,2},{3,19},{19,3},{4,20},{20... | collective-permute-start | bytes 1572872 | tf_op jit(solution)/shard_map/ppermute | solution.py:15
  18.5 7.7 %collective-permute-start.1 = (bf16[128,1024]{1,0:T(8,128)(2,1)S(1)}, bf16[128,1024]{1,0:T(8,128)(2,1)S(1)}, u32[]{:S(2)}, u32[]{:S(2)}) collective-permute-start(bf16[128,1024]{1,0:T(8,128)(2,1)S(1)} %convolution_convert_fusion.2), channel_id=1, source_target_pairs={{0,8},{8,0},{1,9},{9,1},{2,10},{10,2},{3,11},{11,3},{4,12},{12,4},... | collective-permute-start | bytes 786440 | tf_op jit(solution)/shard_map/ppermute | solution.py:15
  21.1 31.4 %collective-permute-start.12 = (bf16[32,4096]{1,0:T(8,128)(2,1)S(1)}, bf16[32,4096]{1,0:T(8,128)(2,1)S(1)}, u32[]{:S(2)}, u32[]{:S(2)}) collective-permute-start(bf16[32,4096]{1,0:T(8,128)(2,1)S(1)} %collective-permute-done.2), channel_id=1, source_target_pairs={{2,4},{3,5},{4,2},{5,3},{10,12},{11,13},{12,10},{13,11},{18,20},{1... | collective-permute-start | bytes 786440 | tf_op jit(solution)/shard_map/ppermute | solution.py:20
  22.5 30.6 %collective-permute-start.16 = (bf16[32,4096]{1,0:T(8,128)(2,1)}, bf16[32,4096]{1,0:T(8,128)(2,1)S(1)}, u32[]{:S(2)}, u32[]{:S(2)}) collective-permute-start(bf16[32,4096]{1,0:T(8,128)(2,1)} %collective-permute-done.3), channel_id=1, source_target_pairs={{2,4},{3,5},{4,2},{5,3},{10,12},{11,13},{12,10},{13,11},{18,20},{1... | collective-permute-start | bytes 786440 | tf_op jit(solution)/shard_map/ppermute | solution.py:20
  23.2 20.5 %collective-permute-start.7 = (bf16[32,4096]{1,0:T(8,128)(2,1)S(1)}, bf16[32,4096]{1,0:T(8,128)(2,1)S(1)}, u32[]{:S(2)}, u32[]{:S(2)}) collective-permute-start(bf16[32,4096]{1,0:T(8,128)(2,1)S(1)} %collective-permute-done.6), channel_id=1, source_target_pairs={{2,0},{3,1},{4,6},{5,7},{10,8},{11,9},{12,14},{13,15},{18,16},{19,... | collective-permute-start | bytes 786440 | tf_op jit(solution)/shard_map/ppermute | solution.py:20
  28.3 14.8 %collective-permute-start.9 = (bf16[32,4096]{1,0:T(8,128)(2,1)S(1)}, bf16[32,4096]{1,0:T(8,128)(2,1)S(1)}, u32[]{:S(2)}, u32[]{:S(2)}) collective-permute-start(bf16[32,4096]{1,0:T(8,128)(2,1)S(1)} %collective-permute-done.8), channel_id=1, source_target_pairs={{2,0},{3,1},{4,6},{5,7},{10,8},{11,9},{12,14},{13,15},{18,16},{19,... | collective-permute-start | bytes 786440 | tf_op jit(solution)/shard_map/ppermute | solution.py:20
  43.1 7.8 %collective-permute-start.5 = (bf16[128,1024]{1,0:T(8,128)(2,1)S(1)}, bf16[128,1024]{1,0:T(8,128)(2,1)S(1)}, u32[]{:S(2)}, u32[]{:S(2)}) collective-permute-start(bf16[128,1024]{1,0:T(8,128)(2,1)S(1)} %convolution_convert_fusion.1), channel_id=1, source_target_pairs={{0,8},{8,0},{1,9},{9,1},{2,10},{10,2},{3,11},{11,3},{4,12},{12,4},... | collective-permute-start | bytes 786440 | tf_op jit(solution)/shard_map/ppermute | solution.py:15
  43.9 10.5 %collective-permute-start.10 = (bf16[64,4096]{1,0:T(8,128)(2,1)S(1)}, bf16[64,4096]{1,0:T(8,128)(2,1)S(1)}, u32[]{:S(2)}, u32[]{:S(2)}) collective-permute-start(bf16[64,4096]{1,0:T(8,128)(2,1)S(1)} %pad_maximum_fusion.3), channel_id=1, source_target_pairs={{0,1},{1,0},{2,3},{3,2},{4,5},{5,4},{6,7},{7,6},{8,9},{9,8},{10,11... | collective-permute-start | bytes 1572872 | tf_op jit(solution)/shard_map/ppermute | solution.py:15
  50.9 128.9 %collective-permute-start.51 = (bf16[64,4096]{1,0:T(8,128)(2,1)}, bf16[64,4096]{1,0:T(8,128)(2,1)}, u32[]{:S(2)}, u32[]{:S(2)}) collective-permute-start(bf16[64,4096]{1,0:T(8,128)(2,1)} %constant_dynamic-update-slice_fusion), channel_id=1, source_target_pairs={{0,16},{16,0},{1,17},{17,1},{2,18},{18,2},{3,19},{19,3},{4,20},{20... | collective-permute-start | bytes 1572872 | tf_op jit(solution)/shard_map/ppermute | solution.py:15
  52.5 32.0 %collective-permute-start.20 = (bf16[128,1024]{1,0:T(8,128)(2,1)S(1)}, bf16[128,1024]{1,0:T(8,128)(2,1)S(1)}, u32[]{:S(2)}, u32[]{:S(2)}) collective-permute-start(bf16[128,1024]{1,0:T(8,128)(2,1)S(1)} %get-tuple-element.74), channel_id=1, source_target_pairs={{0,16},{16,0},{1,17},{17,1},{2,18},{18,2},{3,19},{19,3},{4,20},{20... | collective-permute-start | bytes 786440 | tf_op jit(solution)/shard_map/ppermute | solution.py:15
  53.1 11.0 %collective-permute-start.13 = (bf16[32,4096]{1,0:T(8,128)(2,1)S(1)}, bf16[32,4096]{1,0:T(8,128)(2,1)S(1)}, u32[]{:S(2)}, u32[]{:S(2)}) collective-permute-start(bf16[32,4096]{1,0:T(8,128)(2,1)S(1)} %collective-permute-done.12), channel_id=1, source_target_pairs={{2,0},{3,1},{4,6},{5,7},{10,8},{11,9},{12,14},{13,15},{18,16},{19,... | collective-permute-start | bytes 786440 | tf_op jit(solution)/shard_map/ppermute | solution.py:20
  54.4 13.7 %collective-permute-start.17 = (bf16[32,4096]{1,0:T(8,128)(2,1)S(1)}, bf16[32,4096]{1,0:T(8,128)(2,1)S(1)}, u32[]{:S(2)}, u32[]{:S(2)}) collective-permute-start(bf16[32,4096]{1,0:T(8,128)(2,1)S(1)} %collective-permute-done.16), channel_id=1, source_target_pairs={{2,0},{3,1},{4,6},{5,7},{10,8},{11,9},{12,14},{13,15},{18,16},{19,... | collective-permute-start | bytes 786440 | tf_op jit(solution)/shard_map/ppermute | solution.py:20
  65.8 8.3 %collective-permute-start.11 = (bf16[128,1024]{1,0:T(8,128)(2,1)S(1)}, bf16[128,1024]{1,0:T(8,128)(2,1)S(1)}, u32[]{:S(2)}, u32[]{:S(2)}) collective-permute-start(bf16[128,1024]{1,0:T(8,128)(2,1)S(1)} %convolution_convert_fusion), channel_id=1, source_target_pairs={{0,8},{8,0},{1,9},{9,1},{2,10},{10,2},{3,11},{11,3},{4,12},{12,4},... | collective-permute-start | bytes 786440 | tf_op jit(solution)/shard_map/ppermute | solution.py:15
  68.1 15.9 %collective-permute-start.21 = (bf16[128,1024]{1,0:T(8,128)(2,1)S(1)}, bf16[128,1024]{1,0:T(8,128)(2,1)S(1)}, u32[]{:S(2)}, u32[]{:S(2)}) collective-permute-start(bf16[128,1024]{1,0:T(8,128)(2,1)S(1)} %get-tuple-element.72), channel_id=1, source_target_pairs={{0,16},{16,0},{1,17},{17,1},{2,18},{18,2},{3,19},{19,3},{4,20},{20... | collective-permute-start | bytes 786440 | tf_op jit(solution)/shard_map/ppermute | solution.py:15
  74.2 5.0 %collective-permute-start.15 = (bf16[64,1024]{1,0:T(8,128)(2,1)S(1)}, bf16[64,1024]{1,0:T(8,128)(2,1)S(1)}, u32[]{:S(2)}, u32[]{:S(2)}) collective-permute-start(bf16[64,1024]{1,0:T(8,128)(2,1)S(1)} %convolution_convert_fusion.4), channel_id=1, source_target_pairs={{0,8},{8,0},{1,9},{9,1},{2,10},{10,2},{3,11},{11,3},{4,12},{12,4},... | collective-permute-start | bytes 393224 | tf_op jit(solution)/shard_map/ppermute | solution.py:15
  80.7 9.2 %collective-permute-start.22 = (bf16[128,1024]{1,0:T(8,128)(2,1)S(1)}, bf16[128,1024]{1,0:T(8,128)(2,1)S(1)}, u32[]{:S(2)}, u32[]{:S(2)}) collective-permute-start(bf16[128,1024]{1,0:T(8,128)(2,1)S(1)} %get-tuple-element.70), channel_id=1, source_target_pairs={{0,16},{16,0},{1,17},{17,1},{2,18},{18,2},{3,19},{19,3},{4,20},{20... | collective-permute-start | bytes 786440 | tf_op jit(solution)/shard_map/ppermute | solution.py:15
  83.9 7.9 %collective-permute-start.23 = (bf16[64,1024]{1,0:T(8,128)(2,1)S(1)}, bf16[64,1024]{1,0:T(8,128)(2,1)S(1)}, u32[]{:S(2)}, u32[]{:S(2)}) collective-permute-start(bf16[64,1024]{1,0:T(8,128)(2,1)S(1)} %get-tuple-element.88), channel_id=1, source_target_pairs={{0,16},{16,0},{1,17},{17,1},{2,18},{18,2},{3,19},{19,3},{4,20},{20... | collective-permute-start | bytes 393224 | tf_op jit(solution)/shard_map/ppermute | solution.py:15
  84.5 7.4 %collective-permute-start.19 = (bf16[64,1024]{1,0:T(8,128)(2,1)S(1)}, bf16[64,1024]{1,0:T(8,128)(2,1)S(1)}, u32[]{:S(2)}, u32[]{:S(2)}) collective-permute-start(bf16[64,1024]{1,0:T(8,128)(2,1)S(1)} %convolution_convert_fusion.3), channel_id=1, source_target_pairs={{0,8},{8,0},{1,9},{9,1},{2,10},{10,2},{3,11},{11,3},{4,12},{12,4},... | collective-permute-start | bytes 393224 | tf_op jit(solution)/shard_map/ppermute | solution.py:15
  91.9 5.1 %collective-permute-start.24 = (bf16[64,1024]{1,0:T(8,128)(2,1)S(1)}, bf16[64,1024]{1,0:T(8,128)(2,1)}, u32[]{:S(2)}, u32[]{:S(2)}) collective-permute-start(bf16[64,1024]{1,0:T(8,128)(2,1)S(1)} %get-tuple-element.86), channel_id=1, source_target_pairs={{0,16},{16,0},{1,17},{17,1},{2,18},{18,2},{3,19},{19,3},{4,20},{20... | collective-permute-start | bytes 393224 | tf_op jit(solution)/shard_map/ppermute | solution.py:15
  101.9 5.6 %collective-permute-start.26 = (bf16[128,512]{1,0:T(8,128)(2,1)S(1)}, bf16[128,512]{1,0:T(8,128)(2,1)S(1)}, u32[]{:S(2)}, u32[]{:S(2)}) collective-permute-start(bf16[128,512]{1,0:T(8,128)(2,1)S(1)} %add_convert_fusion.10), channel_id=1, source_target_pairs={{0,2},{1,3},{2,0},{3,1},{4,6},{5,7},{6,4},{7,5},{8,10},{9,11},{10,... | collective-permute-start | bytes 393224 | tf_op jit(solution)/shard_map/ppermute | solution.py:15
  107.5 8.5 %collective-permute-start.27 = (bf16[128,512]{1,0:T(8,128)(2,1)S(1)}, bf16[128,512]{1,0:T(8,128)(2,1)S(1)}, u32[]{:S(2)}, u32[]{:S(2)}) collective-permute-start(bf16[128,512]{1,0:T(8,128)(2,1)S(1)} %add_convert_fusion.9), channel_id=1, source_target_pairs={{0,4},{1,5},{2,6},{3,7},{4,0},{5,1},{6,2},{7,3},{8,12},{9,13},{10,... | collective-permute-start | bytes 393224 | tf_op jit(solution)/shard_map/ppermute | solution.py:15
  116.0 5.5 %collective-permute-start.29 = (bf16[128,512]{1,0:T(8,128)(2,1)S(1)}, bf16[128,512]{1,0:T(8,128)(2,1)S(1)}, u32[]{:S(2)}, u32[]{:S(2)}) collective-permute-start(bf16[128,512]{1,0:T(8,128)(2,1)S(1)} %add_convert_fusion.8), channel_id=1, source_target_pairs={{0,8},{8,0},{1,9},{9,1},{2,10},{10,2},{3,11},{11,3},{4,12},{12,4},... | collective-permute-start | bytes 393224 | tf_op jit(solution)/shard_map/ppermute | solution.py:15
  116.6 6.4 %collective-permute-start.28 = (bf16[128,512]{1,0:T(8,128)(2,1)S(1)}, bf16[128,512]{1,0:T(8,128)(2,1)S(1)}, u32[]{:S(2)}, u32[]{:S(2)}) collective-permute-start(bf16[128,512]{1,0:T(8,128)(2,1)S(1)} %add_convert_fusion.8), channel_id=1, source_target_pairs={{0,1},{1,0},{2,3},{3,2},{4,5},{5,4},{6,7},{7,6},{8,9},{9,8},{10,11... | collective-permute-start | bytes 393224 | tf_op jit(solution)/shard_map/ppermute | solution.py:15
  116.7 63.2 %collective-permute-start.55 = (bf16[32,4096]{1,0:T(8,128)(2,1)S(1)}, bf16[32,4096]{1,0:T(8,128)(2,1)S(1)}, u32[]{:S(2)}, u32[]{:S(2)}) collective-permute-start(bf16[32,4096]{1,0:T(8,128)(2,1)S(1)} %copy-done.13), channel_id=1, source_target_pairs={{0,16},{16,0},{1,17},{17,1},{2,18},{18,2},{3,19},{19,3},{4,20},{20... | collective-permute-start | bytes 786440 | tf_op jit(solution)/shard_map/ppermute | solution.py:15
  121.5 60.2 %collective-permute-start.53 = (bf16[64,4096]{1,0:T(8,128)(2,1)S(1)}, bf16[64,4096]{1,0:T(8,128)(2,1)S(1)}, u32[]{:S(2)}, u32[]{:S(2)}) collective-permute-start(bf16[64,4096]{1,0:T(8,128)(2,1)S(1)} %copy-done.17), channel_id=1, source_target_pairs={{0,16},{16,0},{1,17},{17,1},{2,18},{18,2},{3,19},{19,3},{4,20},{20... | collective-permute-start | bytes 1572872 | tf_op jit(solution)/shard_map/ppermute | solution.py:15
  145.4 7.4 %collective-permute-start.43 = (bf16[64,2048]{1,0:T(8,128)(2,1)S(1)}, bf16[64,2048]{1,0:T(8,128)(2,1)S(1)}, u32[]{:S(2)}, u32[]{:S(2)}) collective-permute-start(bf16[64,2048]{1,0:T(8,128)(2,1)S(1)} %fusion.62), channel_id=1, source_target_pairs={{0,2},{1,3},{6,4},{7,5},{8,10},{9,11},{14,12},{15,13},{16,18},{17,... | collective-permute-start | bytes 786440 | tf_op jit(solution)/shard_map/ppermute | solution.py:20
  152.8 9.4 %collective-permute-start.47 = (bf16[64,2048]{1,0:T(8,128)(2,1)S(1)}, bf16[64,2048]{1,0:T(8,128)(2,1)S(1)}, u32[]{:S(2)}, u32[]{:S(2)}) collective-permute-start(bf16[64,2048]{1,0:T(8,128)(2,1)S(1)} %fusion.63), channel_id=1, source_target_pairs={{0,2},{1,3},{6,4},{7,5},{8,10},{9,11},{14,12},{15,13},{16,18},{17,... | collective-permute-start | bytes 786440 | tf_op jit(solution)/shard_map/ppermute | solution.py:20
  162.2 8.5 %collective-permute-start.34 = (bf16[64,2048]{1,0:T(8,128)(2,1)S(1)}, bf16[64,2048]{1,0:T(8,128)(2,1)S(1)}, u32[]{:S(2)}, u32[]{:S(2)}) collective-permute-start(bf16[64,2048]{1,0:T(8,128)(2,1)S(1)} %fusion.60), channel_id=1, source_target_pairs={{0,2},{1,3},{6,4},{7,5},{8,10},{9,11},{14,12},{15,13},{16,18},{17,... | collective-permute-start | bytes 786440 | tf_op jit(solution)/shard_map/ppermute | solution.py:20
  170.7 8.3 %collective-permute-start.38 = (bf16[64,2048]{1,0:T(8,128)(2,1)S(1)}, bf16[64,2048]{1,0:T(8,128)(2,1)S(1)}, u32[]{:S(2)}, u32[]{:S(2)}) collective-permute-start(bf16[64,2048]{1,0:T(8,128)(2,1)S(1)} %fusion.61), channel_id=1, source_target_pairs={{0,2},{1,3},{6,4},{7,5},{8,10},{9,11},{14,12},{15,13},{16,18},{17,... | collective-permute-start | bytes 786440 | tf_op jit(solution)/shard_map/ppermute | solution.py:20
  175.3 6.4 %collective-permute-start.57 = (bf16[32,4096]{1,0:T(8,128)(2,1)S(1)}, bf16[32,4096]{1,0:T(8,128)(2,1)S(1)}, u32[]{:S(2)}, u32[]{:S(2)}) collective-permute-start(bf16[32,4096]{1,0:T(8,128)(2,1)S(1)} %copy-done.15), channel_id=1, source_target_pairs={{0,16},{16,0},{1,17},{17,1},{2,18},{18,2},{3,19},{19,3},{4,20},{20... | collective-permute-start | bytes 786440 | tf_op jit(solution)/shard_map/ppermute | solution.py:15
  179.0 3.2 %collective-permute-start.36 = (bf16[64,2048]{1,0:T(8,128)(2,1)S(1)}, bf16[64,2048]{1,0:T(8,128)(2,1)S(1)}, u32[]{:S(2)}, u32[]{:S(2)}) collective-permute-start(bf16[64,2048]{1,0:T(8,128)(2,1)S(1)} %add_convert_fusion.7), channel_id=1, source_target_pairs={{2,4},{3,5},{4,2},{5,3},{10,12},{11,13},{12,10},{13,11},{18,20},{1... | collective-permute-start | bytes 786440 | tf_op jit(solution)/shard_map/ppermute | solution.py:20
  179.8 3.9 %collective-permute-start.50 = (bf16[64,4096]{1,0:T(8,128)(2,1)}, bf16[64,4096]{1,0:T(8,128)(2,1)S(1)}, u32[]{:S(2)}, u32[]{:S(2)}) collective-permute-start(bf16[64,4096]{1,0:T(8,128)(2,1)} %collective-permute-done.49), channel_id=1, source_target_pairs={{0,1},{1,0},{2,3},{3,2},{4,5},{5,4},{6,7},{7,6},{8,9},{9,8},{10,11... | collective-permute-start | bytes 1572872 | tf_op jit(solution)/shard_map/ppermute | solution.py:15
  179.9 5.5 %collective-permute-start.52 = (bf16[64,4096]{1,0:T(8,128)(2,1)}, bf16[64,4096]{1,0:T(8,128)(2,1)S(1)}, u32[]{:S(2)}, u32[]{:S(2)}) collective-permute-start(bf16[64,4096]{1,0:T(8,128)(2,1)} %collective-permute-done.51), channel_id=1, source_target_pairs={{0,1},{1,0},{2,3},{3,2},{4,5},{5,4},{6,7},{7,6},{8,9},{9,8},{10,11... | collective-permute-start | bytes 1572872 | tf_op jit(solution)/shard_map/ppermute | solution.py:15
  181.7 6.1 %collective-permute-start.56 = (bf16[32,4096]{1,0:T(8,128)(2,1)S(1)}, bf16[32,4096]{1,0:T(8,128)(2,1)S(1)}, u32[]{:S(2)}, u32[]{:S(2)}) collective-permute-start(bf16[32,4096]{1,0:T(8,128)(2,1)S(1)} %collective-permute-done.55), channel_id=1, source_target_pairs={{0,1},{1,0},{2,3},{3,2},{4,5},{5,4},{6,7},{7,6},{8,9},{9,8},{10,11... | collective-permute-start | bytes 786440 | tf_op jit(solution)/shard_map/ppermute | solution.py:15
  181.7 6.4 %collective-permute-start.58 = (bf16[32,4096]{1,0:T(8,128)(2,1)S(1)}, bf16[32,4096]{1,0:T(8,128)(2,1)S(1)}, u32[]{:S(2)}, u32[]{:S(2)}) collective-permute-start(bf16[32,4096]{1,0:T(8,128)(2,1)S(1)} %collective-permute-done.57), channel_id=1, source_target_pairs={{0,1},{1,0},{2,3},{3,2},{4,5},{5,4},{6,7},{7,6},{8,9},{9,8},{10,11... | collective-permute-start | bytes 786440 | tf_op jit(solution)/shard_map/ppermute | solution.py:15
  182.2 5.1 %collective-permute-start.54 = (bf16[64,4096]{1,0:T(8,128)(2,1)S(1)}, bf16[64,4096]{1,0:T(8,128)(2,1)S(1)}, u32[]{:S(2)}, u32[]{:S(2)}) collective-permute-start(bf16[64,4096]{1,0:T(8,128)(2,1)S(1)} %collective-permute-done.53), channel_id=1, source_target_pairs={{0,1},{1,0},{2,3},{3,2},{4,5},{5,4},{6,7},{7,6},{8,9},{9,8},{10,11... | collective-permute-start | bytes 1572872 | tf_op jit(solution)/shard_map/ppermute | solution.py:15
  183.7 25.6 %collective-permute-start.59 = (bf16[512,1024]{1,0:T(8,128)(2,1)S(1)}, bf16[512,1024]{1,0:T(8,128)(2,1)S(1)}, u32[]{:S(2)}, u32[]{:S(2)}) collective-permute-start(bf16[512,1024]{1,0:T(8,128)(2,1)S(1)} %fusion.51), channel_id=1, source_target_pairs={{0,16},{16,0},{1,17},{17,1},{2,18},{18,2},{3,19},{19,3},{4,20},{20... | collective-permute-start | bytes 3145736 | tf_op jit(solution)/shard_map/ppermute | solution.py:15
  187.0 41.7 %collective-permute-start.40 = (bf16[64,2048]{1,0:T(8,128)(2,1)S(1)}, bf16[64,2048]{1,0:T(8,128)(2,1)S(1)}, u32[]{:S(2)}, u32[]{:S(2)}) collective-permute-start(bf16[64,2048]{1,0:T(8,128)(2,1)S(1)} %constant_dynamic-slice_fusion.3), channel_id=1, source_target_pairs={{0,1},{1,0},{2,3},{3,2},{4,5},{5,4},{6,7},{7,6},{8,9},{9,8},{10,11... | collective-permute-start | bytes 786440 | tf_op jit(solution)/shard_map/ppermute | solution.py:15
  187.8 41.1 %collective-permute-start.31 = (bf16[64,2048]{1,0:T(8,128)(2,1)S(1)}, bf16[64,2048]{1,0:T(8,128)(2,1)S(1)}, u32[]{:S(2)}, u32[]{:S(2)}) collective-permute-start(bf16[64,2048]{1,0:T(8,128)(2,1)S(1)} %constant_dynamic-slice_fusion.7), channel_id=1, source_target_pairs={{0,1},{1,0},{2,3},{3,2},{4,5},{5,4},{6,7},{7,6},{8,9},{9,8},{10,11... | collective-permute-start | bytes 786440 | tf_op jit(solution)/shard_map/ppermute | solution.py:15
  188.9 39.8 %collective-permute-start.48 = (bf16[64,2048]{1,0:T(8,128)(2,1)S(1)}, bf16[64,2048]{1,0:T(8,128)(2,1)S(1)}, u32[]{:S(2)}, u32[]{:S(2)}) collective-permute-start(bf16[64,2048]{1,0:T(8,128)(2,1)S(1)} %add_convert_fusion.1), channel_id=1, source_target_pairs={{2,4},{3,5},{4,2},{5,3},{10,12},{11,13},{12,10},{13,11},{18,20},{1... | collective-permute-start | bytes 786440 | tf_op jit(solution)/shard_map/ppermute | solution.py:20
  189.6 39.3 %collective-permute-start.39 = (bf16[64,2048]{1,0:T(8,128)(2,1)S(1)}, bf16[64,2048]{1,0:T(8,128)(2,1)S(1)}, u32[]{:S(2)}, u32[]{:S(2)}) collective-permute-start(bf16[64,2048]{1,0:T(8,128)(2,1)S(1)} %add_convert_fusion.5), channel_id=1, source_target_pairs={{2,4},{3,5},{4,2},{5,3},{10,12},{11,13},{12,10},{13,11},{18,20},{1... | collective-permute-start | bytes 786440 | tf_op jit(solution)/shard_map/ppermute | solution.py:20
  209.3 19.5 %collective-permute-start.46 = (bf16[64,2048]{1,0:T(8,128)(2,1)S(1)}, bf16[64,2048]{1,0:T(8,128)(2,1)S(1)}, u32[]{:S(2)}, u32[]{:S(2)}) collective-permute-start(bf16[64,2048]{1,0:T(8,128)(2,1)S(1)} %add_convert_fusion.2), channel_id=1, source_target_pairs={{0,2},{1,3},{2,0},{3,1},{4,6},{5,7},{6,4},{7,5},{8,10},{9,11},{10,... | collective-permute-start | bytes 786440 | tf_op jit(solution)/shard_map/ppermute | solution.py:20
  228.8 7.6 %collective-permute-start.37 = (bf16[64,2048]{1,0:T(8,128)(2,1)S(1)}, bf16[64,2048]{1,0:T(8,128)(2,1)S(1)}, u32[]{:S(2)}, u32[]{:S(2)}) collective-permute-start(bf16[64,2048]{1,0:T(8,128)(2,1)S(1)} %add_convert_fusion.6), channel_id=1, source_target_pairs={{0,2},{1,3},{2,0},{3,1},{4,6},{5,7},{6,4},{7,5},{8,10},{9,11},{10,... | collective-permute-start | bytes 786440 | tf_op jit(solution)/shard_map/ppermute | solution.py:20
  (34 other events, 245.8 us)

commit v4 on v3

--- a/solution.py
+++ b/solution.py
@@ -67,13 +67,10 @@
         own = in_order(local, swap(local, "col", 1), core)
         own_part = product(own)
         halves = jnp.split(local, 2, axis=0)
-        middle, near, outward, across, last = [], [], [], [], []
-        for part in halves:
-            middle.append(chip_moves(part, MIDDLE))
-            near.append(chip_moves(part, OUTER_PAIRS))
-        for at in range(2):
-            held = after(middle[at], own_part)
-            outward.append(chip_moves(held, OUTWARD))
+        middle = chip_moves(local, MIDDLE)
+        near = [chip_moves(part, OUTER_PAIRS) for part in halves]
+        outward = chip_moves(after(middle, own_part), OUTWARD)
+        across, last = [], []
         for at in range(2):
             held = after(near[at], own_part)
             across.append(chip_moves(held, MIDDLE))
@@ -90,7 +87,7 @@
         arrivals = [
             (0, 0, [(local,)]),
             (1, 0, [(part,) for part in near]),
-            (2, 0, list(zip(middle, outward))),
+            (2, 0, [(middle, outward)]),
             (3, 0, [(across[0], last[0])]),
             (3, share // 2, [(across[1], last[1])]),
         ]
@@ -106,18 +103,15 @@
 
     pre = jnp.zeros((batch, width), jnp.float32)
     pre_other = jnp.zeros((batch, width), jnp.bfloat16)
-    streams, own_blocks, parts, sent, arrived = [], [], [], [], []
+    own_blocks, parts, arrived = [], [], []
     for at, (place, (_, _, pieces)) in enumerate(zip(places, arrivals)):
         merged = []
         for piece in pieces:
             newest = piece[-1]
             if at >= 1:
                 newest = after(newest, parts[at - 1])
-            if at >= 2:
-                newest = after(newest, sent[min(at - 2, 1)])
             merged.append(piece[0] + newest if len(piece) == 2 else newest)
         stream = jnp.concatenate(merged, axis=0) if len(merged) > 1 else merged[0]
-        streams.append(stream)
         if line and at == 0:
             block, part = own, own_part
         else:
@@ -127,13 +121,16 @@
             part = product(block)
         own_blocks.append(block)
         parts.append(part)
+    for at, place in enumerate(places):
         total = wide(parts[at])
         distance = 1
         while distance < lax.axis_size("row"):
-            total = total + wide(swap(narrow(total), "row", distance))
+            got = swap(narrow(total), "row", distance)
+            if 1 <= at < len(parts) - 1:
+                got = after(got, parts[at + 1])
+            total = total + wide(got)
             distance *= 2
-        sent.append(narrow(total))
-        arrived.append(swap(sent[at], "view", 1))
+        arrived.append(swap(narrow(total), "view", 1))
         for side, (start, size) in enumerate(place):
             rows = slice(side * size, (side + 1) * size)
             pre = lax.dynamic_update_slice(pre, total[rows], (start, 0))
@@ -222,19 +219,33 @@
             slope = lax.dynamic_slice(dpre, (starts[at], 0), (2 * share, width))
             for side in range(sides):
                 sums[at][side] = chip_sum(slope, side)
-        results, late = [], []
+        far_in, mid_in, far_out, far_across = [], [], [], []
         for side in range(sides):
-            far = sums[3][side]
-            far_in = chip_moves(narrow(far), INWARD)
-            mid = sums[2][side]
-            far_in = after(far_in, narrow(mid))
-            far_across = chip_moves(narrow(far + wide(far_in)), MIDDLE)
-            late.append(far_across)
-            mid_in = chip_moves(narrow(mid), INWARD)
-            mid_across = chip_moves(narrow(mid + wide(mid_in)), MIDDLE)
-            close = sums[1][side] + wide(far_across)
-            closed = chip_moves(narrow(close), OUTER_PAIRS)
-            results.append(narrow(sums[0][side] + wide(closed) + wide(mid_across)))
+            far = narrow(sums[3][side])
+            far_in.append(chip_moves(far, INWARD))
+        for side in range(sides):
+            mid = narrow(sums[2][side])
+            mid_in.append(chip_moves(mid, INWARD))
+            got = after(far_in[side], mid)
+            far_out.append(narrow(sums[3][side] + wide(got)))
+            far_across.append(chip_moves(far_out[side], MIDDLE))
+
+        def merge(total, got):
+            return narrow(total + wide(got))
+
+        close = merge(sums[1][0], far_across[0])
+        closed = [chip_moves(close, OUTER_PAIRS)]
+        mid_out = [merge(sums[2][side], mid_in[side]) for side in range(sides)]
+        mid_out = jnp.concatenate(mid_out, axis=1)
+        mid_across = chip_moves(mid_out, MIDDLE)
+        late = [close, far_across[1]]
+        close = merge(sums[1][1], far_across[1])
+        closed.append(chip_moves(close, OUTER_PAIRS))
+        tall = mid_out.shape[1] // sides
+        results = []
+        for side in range(sides):
+            crossed = mid_across[:, side * tall : (side + 1) * tall]
+            results.append(narrow(sums[0][side] + wide(closed[side]) + wide(crossed)))
         grad_hidden = jnp.concatenate(results, axis=1)
     else:
         grad_hidden = lax.psum_scatter(
@@ -249,23 +260,31 @@
         for place in places
         for start, size in place
     ]
-    for at, stream in enumerate(streams):
-        if at >= 2:
-            stream = after(stream, begun)
-        got = swap(stream, "view", 1)
-        if line:
-            clips += [got, swap(got, "col", 1)]
-            (first, size), (second, _) = places[at]
-            order = [
-                jnp.where(core == 0, first, second),
-                jnp.where(core == 0, second, first),
+    received = []
+    for (at, shift, pieces), place in zip(arrivals, places):
+        (first, _), (second, _) = place if line else place * 2
+        step = 0
+        for piece in pieces:
+            stream = piece[0] + piece[1] if len(piece) == 2 else piece[0]
+            size = stream.shape[0]
+            label = len(received)
+            if label >= 2:
+                stream = after(stream, begun)
+            got = swap(stream, "view", 1)
+            received.append(got)
+            order = [0]
+            clips.append(got)
+            if line:
+                clips.append(swap(got, "col", 1))
+                order = [
+                    jnp.where(core == 0, first, second) + step,
+                    jnp.where(core == 0, second, first) + step,
+                ]
+            slopes += [
+                lax.dynamic_slice(dpre_other, (start, 0), (size, width))
+                for start in order
             ]
-        else:
-            clips.append(got)
-            order, size = [0], batch
-        slopes += [
-            lax.dynamic_slice(dpre_other, (start, 0), (size, width)) for start in order
-        ]
+            step += size
     clips, slopes = jnp.concatenate(clips, axis=0), jnp.concatenate(slopes, axis=0)
     grad_weight = lax.dot_general(
         clips, slopes, (((0,), (0,)), ((), ())), preferred_element_type=jnp.float32

time: 238 us -> 234 us (0.983)
  waiting for transfers between devices: 116 us -> 101 us
  starting transfers between devices: 63 us -> 72.5 us
    ppermute x40 -> x42, waiting for transfers between devices: 72.9 us -> 56 us  [swap(): lax.ppermute(block, axis, [(at, at ^ distance) for at in range(count)])]
    ppermute x40 -> x42, starting transfers between devices: 22.5 us -> 31.4 us  [swap(): lax.ppermute(block, axis, [(at, at ^ distance) for at in range(count)])]
    unnamed x78 -> x80, local copies, waits for them, and re-layouts: 4.87 us -> 6.94 us
    ppermute x20 -> x17, waiting for transfers between devices: 43.1 us -> 45 us  [chip_moves(): return lax.ppermute(block, 'col', route)]
    ppermute x20 -> x17, starting transfers between devices: 40.5 us -> 41.1 us  [chip_moves(): return lax.ppermute(block, 'col', route)]
  transfers between devices with their start and end apart: 60 -> 59, of which waited for: 29 -> 25; matrix products, arithmetic and copies ran while one was open for 23% -> 23% of each run, Pallas kernels for 0% -> 0%
where the time goes in v4:
time: 234 us; the launch traced here: 233 us
  waiting for transfers between devices  101 us (43%)
  starting transfers between devices  72.5 us (31%)
  matrix products  36 us (15%)
  other arithmetic  10.8 us (5%)
  local copies, waits for them, and re-layouts  10.6 us (5%)
    ppermute x42, waiting for transfers between devices, swap(): lax.ppermute(block, axis, [(at, at ^ distance) for at in range(count)])  56 us
    ppermute x17, waiting for transfers between devices, chip_moves(): return lax.ppermute(block, 'col', route)  45 us
    ppermute x17, starting transfers between devices, chip_moves(): return lax.ppermute(block, 'col', route)  41.1 us
    ppermute x42, starting transfers between devices, swap(): lax.ppermute(block, axis, [(at, at ^ distance) for at in range(count)])  31.4 us
    dot_general x8, matrix products, back(): lax.dot_general(slope, weight[side * tall:(side + 1) * tall], (((1,), (1,...  12.1 us
    dot_general x1, matrix products, shards(): lax.dot_general(clips, slopes, (((0,), (0,)), ((), ())), preferred_elemen...  11.6 us
    dot_general x5, matrix products, product(): return narrow(jnp.dot(block, weight, preferred_element_type=jnp.float32))  10.6 us
    unnamed x80, local copies, waits for them, and re-layouts  6.94 us
  transfers between devices with their start and end apart: 59, of which 25 were waited for; matrix products, arithmetic and copies ran while one was open for 23% of the time, Pallas kernels for 0%

profile of v4, /device:TPU:0, one launch (start us, length us, event | category | flops | bytes accessed | tf_op | source)
XLA Modules:
  0.0 233.2 jit_solution(10662345972285997977)
XLA Ops:
  0.6 3.1 %collective-permute-start.46 = (bf16[64,4096]{1,0:T(8,128)(2,1)}, bf16[64,4096]{1,0:T(8,128)(2,1)}, u32[]{:S(2)}, u32[]{:S(2)}) collective-permute-start(bf16[64,4096]{1,0:T(8,128)(2,1)} %bitcast.22), channel_id=1, source_target_pairs={{0,16},{16,0},{1,17},{17,1},{2,18},{18,2},{3,19},{19,3},{4,20},{20... | collective-permute-start | bytes 1572872 | tf_op jit(solution)/shard_map/ppermute | solution.py:15
  5.5 4.4 %collective-permute-start.2 = (bf16[32,4096]{1,0:T(8,128)(2,1)S(1)}, bf16[32,4096]{1,0:T(8,128)(2,1)}, u32[]{:S(2)}, u32[]{:S(2)}) collective-permute-start(bf16[32,4096]{1,0:T(8,128)(2,1)S(1)} %get-tuple-element.79), channel_id=1, source_target_pairs={{0,2},{1,3},{2,0},{3,1},{4,6},{5,7},{6,4},{7,5},{8,10},{9,11},{10,... | collective-permute-start | bytes 786440 | tf_op jit(solution)/shard_map/ppermute | solution.py:20
  11.3 4.9 %convolution_convert_fusion.2 = bf16[128,1024]{1,0:T(8,128)(2,1)S(1)} fusion(bf16[4096,1024]{1,0:T(8,128)(2,1)} %param.3, bf16[64,4096]{1,0:T(8,128)(2,1)S(1)} %get-tuple-element.62, bf16[64,4096]{1,0:T(8,128)(2,1)S(1)} %get-tuple-element.61), kind=kOutput, calls=%fused_computation.48 | convolution fusion | flops 1075970048 | bytes 9699328 | tf_op jit(solution)/shard_map/dot_general | solution.py:64
  16.2 1.6 collective-permute-start.1
  17.8 4.8 %collective-permute-done.3 = bf16[32,4096]{1,0:T(8,128)(2,1)S(1)} collective-permute-done((bf16[32,4096]{1,0:T(8,128)(2,1)S(1)}, bf16[32,4096]{1,0:T(8,128)(2,1)S(1)}, u32[]{:S(2)}, u32[]{:S(2)}) %collective-permute-start.3) | collective-permute-done | bytes 262176 | tf_op jit(solution)/shard_map/ppermute | solution.py:20
  29.8 15.9 %collective-permute-done.7 = bf16[64,4096]{1,0:T(8,128)(2,1)S(1)} collective-permute-done((bf16[64,4096]{1,0:T(8,128)(2,1)S(1)}, bf16[64,4096]{1,0:T(8,128)(2,1)S(1)}, u32[]{:S(2)}, u32[]{:S(2)}) %collective-permute-start.7) | collective-permute-done | bytes 524320 | tf_op jit(solution)/shard_map/ppermute | solution.py:20
  47.9 1.5 collective-permute-start.15
  50.4 1.5 collective-permute-start.5
  53.3 4.3 %collective-permute-done.11 = bf16[32,4096]{1,0:T(8,128)(2,1)S(1)} collective-permute-done((bf16[32,4096]{1,0:T(8,128)(2,1)S(1)}, bf16[32,4096]{1,0:T(8,128)(2,1)S(1)}, u32[]{:S(2)}, u32[]{:S(2)}) %collective-permute-start.11) | collective-permute-done | bytes 262176 | tf_op jit(solution)/shard_map/ppermute | solution.py:20
  57.6 1.5 collective-permute-start.9
  60.0 1.5 collective-permute-done.12
  62.1 1.6 convolution_convert_fusion.4
  63.7 1.6 collective-permute-start.13
  67.6 1.5 collective-permute-start.20
  69.2 1.6 convolution_convert_fusion.3
  72.1 1.6 collective-permute-start.21
  73.6 3.1 %collective-permute-done.20 = bf16[128,1024]{1,0:T(8,128)(2,1)S(1)} collective-permute-done((bf16[128,1024]{1,0:T(8,128)(2,1)S(1)}, bf16[128,1024]{1,0:T(8,128)(2,1)S(1)}, u32[]{:S(2)}, u32[]{:S(2)}) %collective-permute-start.20) | collective-permute-done | bytes 262176 | tf_op jit(solution)/shard_map/ppermute | solution.py:15
  77.4 1.6 collective-permute-start.22
  79.0 6.2 %collective-permute-done.21 = bf16[64,1024]{1,0:T(8,128)(2,1)S(1)} collective-permute-done((bf16[64,1024]{1,0:T(8,128)(2,1)S(1)}, bf16[64,1024]{1,0:T(8,128)(2,1)S(1)}, u32[]{:S(2)}, u32[]{:S(2)}) %collective-permute-start.21) | collective-permute-done | bytes 131104 | tf_op jit(solution)/shard_map/ppermute | solution.py:15
  85.7 1.5 collective-permute-done.22
  92.1 3.2 %collective-permute-start.24 = (bf16[128,512]{1,0:T(8,128)(2,1)S(1)}, bf16[128,512]{1,0:T(8,128)(2,1)S(1)}, u32[]{:S(2)}, u32[]{:S(2)}) collective-permute-start(bf16[128,512]{1,0:T(8,128)(2,1)S(1)} %add_convert_fusion.10), channel_id=1, source_target_pairs={{0,2},{1,3},{2,0},{3,1},{4,6},{5,7},{6,4},{7,5},{8,10},{9,11},{10,... | collective-permute-start | bytes 393224 | tf_op jit(solution)/shard_map/ppermute | solution.py:15
  95.3 3.8 %collective-permute-done.24 = bf16[128,512]{1,0:T(8,128)(2,1)S(1)} collective-permute-done((bf16[128,512]{1,0:T(8,128)(2,1)S(1)}, bf16[128,512]{1,0:T(8,128)(2,1)S(1)}, u32[]{:S(2)}, u32[]{:S(2)}) %collective-permute-start.24) | collective-permute-done | bytes 131104 | tf_op jit(solution)/shard_map/ppermute | solution.py:15
  99.1 1.7 collective-permute-start.25
  100.9 7.0 %collective-permute-done.25 = bf16[128,512]{1,0:T(8,128)(2,1)S(1)} collective-permute-done((bf16[128,512]{1,0:T(8,128)(2,1)S(1)}, bf16[128,512]{1,0:T(8,128)(2,1)S(1)}, u32[]{:S(2)}, u32[]{:S(2)}) %collective-permute-start.25) | collective-permute-done | bytes 131104 | tf_op jit(solution)/shard_map/ppermute | solution.py:15
  110.1 2.8 %collective-permute-done.27 = bf16[128,512]{1,0:T(8,128)(2,1)S(1)} collective-permute-done((bf16[128,512]{1,0:T(8,128)(2,1)S(1)}, bf16[128,512]{1,0:T(8,128)(2,1)S(1)}, u32[]{:S(2)}, u32[]{:S(2)}) %collective-permute-start.27) | collective-permute-done | bytes 131104 | tf_op jit(solution)/shard_map/ppermute | solution.py:15
  116.6 1.5 fusion.39
  118.2 1.5 fusion.30
  119.9 1.5 fusion.27
  121.4 1.5 fusion.24
  122.9 1.5 fusion.33
  124.5 1.5 fusion.36
  126.0 1.5 fusion.21
  127.5 1.5 fusion.18
  135.4 5.2 %collective-permute-done.43 = bf16[64,2048]{1,0:T(8,128)(2,1)S(1)} collective-permute-done((bf16[64,2048]{1,0:T(8,128)(2,1)S(1)}, bf16[64,2048]{1,0:T(8,128)(2,1)S(1)}, u32[]{:S(2)}, u32[]{:S(2)}) %collective-permute-start.43) | collective-permute-done | bytes 262176 | tf_op jit(solution)/shard_map/ppermute | solution.py:20
  140.6 5.2 %collective-permute-done.32 = bf16[64,2048]{1,0:T(8,128)(2,1)S(1)} collective-permute-done((bf16[64,2048]{1,0:T(8,128)(2,1)S(1)}, bf16[64,2048]{1,0:T(8,128)(2,1)S(1)}, u32[]{:S(2)}, u32[]{:S(2)}) %collective-permute-start.32) | collective-permute-done | bytes 262176 | tf_op jit(solution)/shard_map/ppermute | solution.py:20
  145.8 4.4 %collective-permute-start.38 = (bf16[64,2048]{1,0:T(8,128)(2,1)S(1)}, bf16[64,2048]{1,0:T(8,128)(2,1)S(1)}, u32[]{:S(2)}, u32[]{:S(2)}) collective-permute-start(bf16[64,2048]{1,0:T(8,128)(2,1)S(1)} %fusion.62), channel_id=1, source_target_pairs={{0,2},{1,3},{6,4},{7,5},{8,10},{9,11},{14,12},{15,13},{16,18},{17,... | collective-permute-start | bytes 786440 | tf_op jit(solution)/shard_map/ppermute | solution.py:20
  150.3 5.3 %collective-permute-done.38 = bf16[64,2048]{1,0:T(8,128)(2,1)S(1)} collective-permute-done((bf16[64,2048]{1,0:T(8,128)(2,1)S(1)}, bf16[64,2048]{1,0:T(8,128)(2,1)S(1)}, u32[]{:S(2)}, u32[]{:S(2)}) %collective-permute-start.38) | collective-permute-done | bytes 262176 | tf_op jit(solution)/shard_map/ppermute | solution.py:20
  155.6 4.4 %collective-permute-start.36 = (bf16[64,2048]{1,0:T(8,128)(2,1)S(1)}, bf16[64,2048]{1,0:T(8,128)(2,1)S(1)}, u32[]{:S(2)}, u32[]{:S(2)}) collective-permute-start(bf16[64,2048]{1,0:T(8,128)(2,1)S(1)} %fusion.61), channel_id=1, source_target_pairs={{0,2},{1,3},{6,4},{7,5},{8,10},{9,11},{14,12},{15,13},{16,18},{17,... | collective-permute-start | bytes 786440 | tf_op jit(solution)/shard_map/ppermute | solution.py:20
  160.2 4.3 %collective-permute-done.36 = bf16[64,2048]{1,0:T(8,128)(2,1)S(1)} collective-permute-done((bf16[64,2048]{1,0:T(8,128)(2,1)S(1)}, bf16[64,2048]{1,0:T(8,128)(2,1)S(1)}, u32[]{:S(2)}, u32[]{:S(2)}) %collective-permute-start.36) | collective-permute-done | bytes 262176 | tf_op jit(solution)/shard_map/ppermute | solution.py:20
  165.4 1.6 collective-permute-start.54
  168.7 1.5 collective-permute-start.56
  171.9 2.7 %collective-permute-done.54 = bf16[32,4096]{1,0:T(8,128)(2,1)S(1)} collective-permute-done((bf16[32,4096]{1,0:T(8,128)(2,1)S(1)}, bf16[32,4096]{1,0:T(8,128)(2,1)S(1)}, u32[]{:S(2)}, u32[]{:S(2)}) %collective-permute-start.54) | collective-permute-done | bytes 262176 | tf_op jit(solution)/shard_map/ppermute | solution.py:15
  174.6 13.9 %collective-permute-done.56 = bf16[32,4096]{1,0:T(8,128)(2,1)S(1)} collective-permute-done((bf16[32,4096]{1,0:T(8,128)(2,1)S(1)}, bf16[32,4096]{1,0:T(8,128)(2,1)S(1)}, u32[]{:S(2)}, u32[]{:S(2)}) %collective-permute-start.56) | collective-permute-done | bytes 262176 | tf_op jit(solution)/shard_map/ppermute | solution.py:15
  191.1 1.6 collective-permute-start.58
  195.7 13.0 %collective-permute-start.35 = (bf16[64,2048]{1,0:T(8,128)(2,1)S(1)}, bf16[64,2048]{1,0:T(8,128)(2,1)S(1)}, u32[]{:S(2)}, u32[]{:S(2)}) collective-permute-start(bf16[64,2048]{1,0:T(8,128)(2,1)S(1)} %add_convert_fusion.6), channel_id=1, source_target_pairs={{0,2},{1,3},{2,0},{3,1},{4,6},{5,7},{6,4},{7,5},{8,10},{9,11},{10,... | collective-permute-start | bytes 786440 | tf_op jit(solution)/shard_map/ppermute | solution.py:20
  208.7 7.5 %collective-permute-done.58 = bf16[512,1024]{1,0:T(8,128)(2,1)S(1)} collective-permute-done((bf16[512,1024]{1,0:T(8,128)(2,1)S(1)}, bf16[512,1024]{1,0:T(8,128)(2,1)S(1)}, u32[]{:S(2)}, u32[]{:S(2)}) %collective-permute-start.58) | collective-permute-done | bytes 1048608 | tf_op jit(solution)/shard_map/ppermute | solution.py:15
  216.2 3.9 %collective-permute-start.45 = (bf16[64,2048]{1,0:T(8,128)(2,1)S(1)}, bf16[64,2048]{1,0:T(8,128)(2,1)S(1)}, u32[]{:S(2)}, u32[]{:S(2)}) collective-permute-start(bf16[64,2048]{1,0:T(8,128)(2,1)S(1)} %add_convert_fusion.1), channel_id=1, source_target_pairs={{0,2},{1,3},{2,0},{3,1},{4,6},{5,7},{6,4},{7,5},{8,10},{9,11},{10,... | collective-permute-start | bytes 786440 | tf_op jit(solution)/shard_map/ppermute | solution.py:20
  220.4 11.6 %convolution_multiply_fusion = f32[4096,1024]{1,0:T(8,128)} fusion(bf16[1024,4096]{1,0:T(8,128)(2,1)S(1)} %constant_dynamic-update-slice_fusion.2, bf16[1024,1024]{1,0:T(8,128)(2,1)S(1)} %constant_dynamic-update-slice_fusion.19), kind=kOutput, calls=%fused_computation | convolution fusion | flops 8594128896 | bytes 27262976 | tf_op jit(solution)/shard_map/dot_general | solution.py:289
  (253 shorter events, 49.2 us)
Async XLA Ops:
  0.6 70.2 %collective-permute-start.46 = (bf16[64,4096]{1,0:T(8,128)(2,1)}, bf16[64,4096]{1,0:T(8,128)(2,1)}, u32[]{:S(2)}, u32[]{:S(2)}) collective-permute-start(bf16[64,4096]{1,0:T(8,128)(2,1)} %bitcast.22), channel_id=1, source_target_pairs={{0,16},{16,0},{1,17},{17,1},{2,18},{18,2},{3,19},{19,3},{4,20},{20... | collective-permute-start | bytes 1572872 | tf_op jit(solution)/shard_map/ppermute | solution.py:15
  3.7 21.8 %collective-permute-start.6 = (bf16[64,4096]{1,0:T(8,128)(2,1)}, bf16[64,4096]{1,0:T(8,128)(2,1)S(1)}, u32[]{:S(2)}, u32[]{:S(2)}) collective-permute-start(bf16[64,4096]{1,0:T(8,128)(2,1)} %bitcast.23), channel_id=1, source_target_pairs={{2,4},{3,5},{4,2},{5,3},{10,12},{11,13},{12,10},{13,11},{18,20},{1... | collective-permute-start | bytes 1572872 | tf_op jit(solution)/shard_map/ppermute | solution.py:20
  4.4 5.7 %collective-permute-start = (bf16[64,4096]{1,0:T(8,128)(2,1)}, bf16[64,4096]{1,0:T(8,128)(2,1)S(1)}, u32[]{:S(2)}, u32[]{:S(2)}) collective-permute-start(bf16[64,4096]{1,0:T(8,128)(2,1)} %bitcast.24), channel_id=1, source_target_pairs={{0,1},{1,0},{2,3},{3,2},{4,5},{5,4},{6,7},{7,6},{8,9},{9,8},{10,11... | collective-permute-start | bytes 1572872 | tf_op jit(solution)/shard_map/ppermute | solution.py:15
  5.5 17.0 %collective-permute-start.2 = (bf16[32,4096]{1,0:T(8,128)(2,1)S(1)}, bf16[32,4096]{1,0:T(8,128)(2,1)}, u32[]{:S(2)}, u32[]{:S(2)}) collective-permute-start(bf16[32,4096]{1,0:T(8,128)(2,1)S(1)} %get-tuple-element.79), channel_id=1, source_target_pairs={{0,2},{1,3},{2,0},{3,1},{4,6},{5,7},{6,4},{7,5},{8,10},{9,11},{10,... | collective-permute-start | bytes 786440 | tf_op jit(solution)/shard_map/ppermute | solution.py:20
  10.0 12.6 %collective-permute-start.3 = (bf16[32,4096]{1,0:T(8,128)(2,1)S(1)}, bf16[32,4096]{1,0:T(8,128)(2,1)S(1)}, u32[]{:S(2)}, u32[]{:S(2)}) collective-permute-start(bf16[32,4096]{1,0:T(8,128)(2,1)S(1)} %get-tuple-element.80), channel_id=1, source_target_pairs={{0,2},{1,3},{2,0},{3,1},{4,6},{5,7},{6,4},{7,5},{8,10},{9,11},{10,... | collective-permute-start | bytes 786440 | tf_op jit(solution)/shard_map/ppermute | solution.py:20
  16.2 9.9 %collective-permute-start.1 = (bf16[128,1024]{1,0:T(8,128)(2,1)S(1)}, bf16[128,1024]{1,0:T(8,128)(2,1)S(1)}, u32[]{:S(2)}, u32[]{:S(2)}) collective-permute-start(bf16[128,1024]{1,0:T(8,128)(2,1)S(1)} %convolution_convert_fusion.2), channel_id=1, source_target_pairs={{0,8},{8,0},{1,9},{9,1},{2,10},{10,2},{3,11},{11,3},{4,12},{12,4},... | collective-permute-start | bytes 786440 | tf_op jit(solution)/shard_map/ppermute | solution.py:15
  23.6 4.2 %collective-permute-start.4 = (bf16[64,4096]{1,0:T(8,128)(2,1)S(1)}, bf16[64,4096]{1,0:T(8,128)(2,1)S(1)}, u32[]{:S(2)}, u32[]{:S(2)}) collective-permute-start(bf16[64,4096]{1,0:T(8,128)(2,1)S(1)} %constant_dynamic-update-slice_fusion), channel_id=1, source_target_pairs={{0,1},{1,0},{2,3},{3,2},{4,5},{5,4},{6,7},{7,6},{8,9},{9,8},{10,11... | collective-permute-start | bytes 1572872 | tf_op jit(solution)/shard_map/ppermute | solution.py:15
  24.8 21.8 %collective-permute-start.10 = (bf16[32,4096]{1,0:T(8,128)(2,1)}, bf16[32,4096]{1,0:T(8,128)(2,1)S(1)}, u32[]{:S(2)}, u32[]{:S(2)}) collective-permute-start(bf16[32,4096]{1,0:T(8,128)(2,1)} %collective-permute-done.2), channel_id=1, source_target_pairs={{2,4},{3,5},{4,2},{5,3},{10,12},{11,13},{12,10},{13,11},{18,20},{1... | collective-permute-start | bytes 786440 | tf_op jit(solution)/shard_map/ppermute | solution.py:20
  25.5 22.4 %collective-permute-start.14 = (bf16[32,4096]{1,0:T(8,128)(2,1)S(1)}, bf16[32,4096]{1,0:T(8,128)(2,1)S(1)}, u32[]{:S(2)}, u32[]{:S(2)}) collective-permute-start(bf16[32,4096]{1,0:T(8,128)(2,1)S(1)} %collective-permute-done.3), channel_id=1, source_target_pairs={{2,4},{3,5},{4,2},{5,3},{10,12},{11,13},{12,10},{13,11},{18,20},{1... | collective-permute-start | bytes 786440 | tf_op jit(solution)/shard_map/ppermute | solution.py:20
  26.1 19.5 %collective-permute-start.7 = (bf16[64,4096]{1,0:T(8,128)(2,1)S(1)}, bf16[64,4096]{1,0:T(8,128)(2,1)S(1)}, u32[]{:S(2)}, u32[]{:S(2)}) collective-permute-start(bf16[64,4096]{1,0:T(8,128)(2,1)S(1)} %collective-permute-done.6), channel_id=1, source_target_pairs={{2,0},{3,1},{4,6},{5,7},{10,8},{11,9},{12,14},{13,15},{18,16},{19,... | collective-permute-start | bytes 1572872 | tf_op jit(solution)/shard_map/ppermute | solution.py:20
  27.8 43.6 %collective-permute-start.18 = (bf16[128,1024]{1,0:T(8,128)(2,1)S(1)}, bf16[128,1024]{1,0:T(8,128)(2,1)S(1)}, u32[]{:S(2)}, u32[]{:S(2)}) collective-permute-start(bf16[128,1024]{1,0:T(8,128)(2,1)S(1)} %get-tuple-element.74), channel_id=1, source_target_pairs={{0,16},{16,0},{1,17},{17,1},{2,18},{18,2},{3,19},{19,3},{4,20},{20... | collective-permute-start | bytes 786440 | tf_op jit(solution)/shard_map/ppermute | solution.py:15
  46.5 3.9 %collective-permute-start.8 = (bf16[64,4096]{1,0:T(8,128)(2,1)S(1)}, bf16[64,4096]{1,0:T(8,128)(2,1)S(1)}, u32[]{:S(2)}, u32[]{:S(2)}) collective-permute-start(bf16[64,4096]{1,0:T(8,128)(2,1)S(1)} %get-tuple-element.64), channel_id=1, source_target_pairs={{0,1},{1,0},{2,3},{3,2},{4,5},{5,4},{6,7},{7,6},{8,9},{9,8},{10,11... | collective-permute-start | bytes 1572872 | tf_op jit(solution)/shard_map/ppermute | solution.py:15
  46.6 11.1 %collective-permute-start.11 = (bf16[32,4096]{1,0:T(8,128)(2,1)S(1)}, bf16[32,4096]{1,0:T(8,128)(2,1)S(1)}, u32[]{:S(2)}, u32[]{:S(2)}) collective-permute-start(bf16[32,4096]{1,0:T(8,128)(2,1)S(1)} %collective-permute-done.10), channel_id=1, source_target_pairs={{2,0},{3,1},{4,6},{5,7},{10,8},{11,9},{12,14},{13,15},{18,16},{19,... | collective-permute-start | bytes 786440 | tf_op jit(solution)/shard_map/ppermute | solution.py:20
  47.9 15.8 %collective-permute-start.15 = (bf16[32,4096]{1,0:T(8,128)(2,1)S(1)}, bf16[32,4096]{1,0:T(8,128)(2,1)S(1)}, u32[]{:S(2)}, u32[]{:S(2)}) collective-permute-start(bf16[32,4096]{1,0:T(8,128)(2,1)S(1)} %collective-permute-done.14), channel_id=1, source_target_pairs={{2,0},{3,1},{4,6},{5,7},{10,8},{11,9},{12,14},{13,15},{18,16},{19,... | collective-permute-start | bytes 786440 | tf_op jit(solution)/shard_map/ppermute | solution.py:20
  50.4 8.7 %collective-permute-start.5 = (bf16[128,1024]{1,0:T(8,128)(2,1)S(1)}, bf16[128,1024]{1,0:T(8,128)(2,1)S(1)}, u32[]{:S(2)}, u32[]{:S(2)}) collective-permute-start(bf16[128,1024]{1,0:T(8,128)(2,1)S(1)} %convolution_convert_fusion.1), channel_id=1, source_target_pairs={{0,8},{8,0},{1,9},{9,1},{2,10},{10,2},{3,11},{11,3},{4,12},{12,4},... | collective-permute-start | bytes 786440 | tf_op jit(solution)/shard_map/ppermute | solution.py:15
  57.6 8.4 %collective-permute-start.9 = (bf16[128,1024]{1,0:T(8,128)(2,1)S(1)}, bf16[128,1024]{1,0:T(8,128)(2,1)S(1)}, u32[]{:S(2)}, u32[]{:S(2)}) collective-permute-start(bf16[128,1024]{1,0:T(8,128)(2,1)S(1)} %convolution_convert_fusion), channel_id=1, source_target_pairs={{0,8},{8,0},{1,9},{9,1},{2,10},{10,2},{3,11},{11,3},{4,12},{12,4},... | collective-permute-start | bytes 786440 | tf_op jit(solution)/shard_map/ppermute | solution.py:15
  61.5 9.9 %collective-permute-start.19 = (bf16[128,1024]{1,0:T(8,128)(2,1)S(1)}, bf16[128,1024]{1,0:T(8,128)(2,1)S(1)}, u32[]{:S(2)}, u32[]{:S(2)}) collective-permute-start(bf16[128,1024]{1,0:T(8,128)(2,1)S(1)} %get-tuple-element.72), channel_id=1, source_target_pairs={{0,16},{16,0},{1,17},{17,1},{2,18},{18,2},{3,19},{19,3},{4,20},{20... | collective-permute-start | bytes 786440 | tf_op jit(solution)/shard_map/ppermute | solution.py:15
  63.7 8.3 %collective-permute-start.13 = (bf16[64,1024]{1,0:T(8,128)(2,1)S(1)}, bf16[64,1024]{1,0:T(8,128)(2,1)S(1)}, u32[]{:S(2)}, u32[]{:S(2)}) collective-permute-start(bf16[64,1024]{1,0:T(8,128)(2,1)S(1)} %convolution_convert_fusion.4), channel_id=1, source_target_pairs={{0,8},{8,0},{1,9},{9,1},{2,10},{10,2},{3,11},{11,3},{4,12},{12,4},... | collective-permute-start | bytes 393224 | tf_op jit(solution)/shard_map/ppermute | solution.py:15
  67.6 9.2 %collective-permute-start.20 = (bf16[128,1024]{1,0:T(8,128)(2,1)S(1)}, bf16[128,1024]{1,0:T(8,128)(2,1)S(1)}, u32[]{:S(2)}, u32[]{:S(2)}) collective-permute-start(bf16[128,1024]{1,0:T(8,128)(2,1)S(1)} %get-tuple-element.70), channel_id=1, source_target_pairs={{0,16},{16,0},{1,17},{17,1},{2,18},{18,2},{3,19},{19,3},{4,20},{20... | collective-permute-start | bytes 786440 | tf_op jit(solution)/shard_map/ppermute | solution.py:15
  70.8 97.1 %collective-permute-start.48 = (bf16[32,4096]{1,0:T(8,128)(2,1)}, bf16[32,4096]{1,0:T(8,128)(2,1)}, u32[]{:S(2)}, u32[]{:S(2)}) collective-permute-start(bf16[32,4096]{1,0:T(8,128)(2,1)} %collective-permute-done.2), channel_id=1, source_target_pairs={{0,16},{16,0},{1,17},{17,1},{2,18},{18,2},{3,19},{19,3},{4,20},{20... | collective-permute-start | bytes 786440 | tf_op jit(solution)/shard_map/ppermute | solution.py:15
  71.4 99.9 %collective-permute-start.47 = (bf16[64,4096]{1,0:T(8,128)(2,1)}, bf16[64,4096]{1,0:T(8,128)(2,1)}, u32[]{:S(2)}, u32[]{:S(2)}) collective-permute-start(bf16[64,4096]{1,0:T(8,128)(2,1)} %collective-permute-done.46), channel_id=1, source_target_pairs={{0,1},{1,0},{2,3},{3,2},{4,5},{5,4},{6,7},{7,6},{8,9},{9,8},{10,11... | collective-permute-start | bytes 1572872 | tf_op jit(solution)/shard_map/ppermute | solution.py:15
  71.4 5.9 %collective-permute-start.17 = (bf16[64,1024]{1,0:T(8,128)(2,1)S(1)}, bf16[64,1024]{1,0:T(8,128)(2,1)S(1)}, u32[]{:S(2)}, u32[]{:S(2)}) collective-permute-start(bf16[64,1024]{1,0:T(8,128)(2,1)S(1)} %convolution_convert_fusion.3), channel_id=1, source_target_pairs={{0,8},{8,0},{1,9},{9,1},{2,10},{10,2},{3,11},{11,3},{4,12},{12,4},... | collective-permute-start | bytes 393224 | tf_op jit(solution)/shard_map/ppermute | solution.py:15
  72.1 13.1 %collective-permute-start.21 = (bf16[64,1024]{1,0:T(8,128)(2,1)S(1)}, bf16[64,1024]{1,0:T(8,128)(2,1)S(1)}, u32[]{:S(2)}, u32[]{:S(2)}) collective-permute-start(bf16[64,1024]{1,0:T(8,128)(2,1)S(1)} %get-tuple-element.92), channel_id=1, source_target_pairs={{0,16},{16,0},{1,17},{17,1},{2,18},{18,2},{3,19},{19,3},{4,20},{20... | collective-permute-start | bytes 393224 | tf_op jit(solution)/shard_map/ppermute | solution.py:15
  77.4 9.9 %collective-permute-start.22 = (bf16[64,1024]{1,0:T(8,128)(2,1)S(1)}, bf16[64,1024]{1,0:T(8,128)(2,1)}, u32[]{:S(2)}, u32[]{:S(2)}) collective-permute-start(bf16[64,1024]{1,0:T(8,128)(2,1)S(1)} %get-tuple-element.90), channel_id=1, source_target_pairs={{0,16},{16,0},{1,17},{17,1},{2,18},{18,2},{3,19},{19,3},{4,20},{20... | collective-permute-start | bytes 393224 | tf_op jit(solution)/shard_map/ppermute | solution.py:15
  92.1 7.0 %collective-permute-start.24 = (bf16[128,512]{1,0:T(8,128)(2,1)S(1)}, bf16[128,512]{1,0:T(8,128)(2,1)S(1)}, u32[]{:S(2)}, u32[]{:S(2)}) collective-permute-start(bf16[128,512]{1,0:T(8,128)(2,1)S(1)} %add_convert_fusion.10), channel_id=1, source_target_pairs={{0,2},{1,3},{2,0},{3,1},{4,6},{5,7},{6,4},{7,5},{8,10},{9,11},{10,... | collective-permute-start | bytes 393224 | tf_op jit(solution)/shard_map/ppermute | solution.py:15
  99.1 8.7 %collective-permute-start.25 = (bf16[128,512]{1,0:T(8,128)(2,1)S(1)}, bf16[128,512]{1,0:T(8,128)(2,1)S(1)}, u32[]{:S(2)}, u32[]{:S(2)}) collective-permute-start(bf16[128,512]{1,0:T(8,128)(2,1)S(1)} %add_convert_fusion.9), channel_id=1, source_target_pairs={{0,4},{1,5},{2,6},{3,7},{4,0},{5,1},{6,2},{7,3},{8,12},{9,13},{10,... | collective-permute-start | bytes 393224 | tf_op jit(solution)/shard_map/ppermute | solution.py:15
  107.9 5.0 %collective-permute-start.27 = (bf16[128,512]{1,0:T(8,128)(2,1)S(1)}, bf16[128,512]{1,0:T(8,128)(2,1)S(1)}, u32[]{:S(2)}, u32[]{:S(2)}) collective-permute-start(bf16[128,512]{1,0:T(8,128)(2,1)S(1)} %add_convert_fusion.8), channel_id=1, source_target_pairs={{0,8},{8,0},{1,9},{9,1},{2,10},{10,2},{3,11},{11,3},{4,12},{12,4},... | collective-permute-start | bytes 393224 | tf_op jit(solution)/shard_map/ppermute | solution.py:15
  109.0 3.9 %collective-permute-start.26 = (bf16[128,512]{1,0:T(8,128)(2,1)S(1)}, bf16[128,512]{1,0:T(8,128)(2,1)S(1)}, u32[]{:S(2)}, u32[]{:S(2)}) collective-permute-start(bf16[128,512]{1,0:T(8,128)(2,1)S(1)} %add_convert_fusion.8), channel_id=1, source_target_pairs={{0,1},{1,0},{2,3},{3,2},{4,5},{5,4},{6,7},{7,6},{8,9},{9,8},{10,11... | collective-permute-start | bytes 393224 | tf_op jit(solution)/shard_map/ppermute | solution.py:15
  109.0 62.4 %collective-permute-start.50 = (bf16[32,4096]{1,0:T(8,128)(2,1)S(1)}, bf16[32,4096]{1,0:T(8,128)(2,1)S(1)}, u32[]{:S(2)}, u32[]{:S(2)}) collective-permute-start(bf16[32,4096]{1,0:T(8,128)(2,1)S(1)} %copy-done.14), channel_id=1, source_target_pairs={{0,16},{16,0},{1,17},{17,1},{2,18},{18,2},{3,19},{19,3},{4,20},{20... | collective-permute-start | bytes 786440 | tf_op jit(solution)/shard_map/ppermute | solution.py:15
  132.6 8.0 %collective-permute-start.43 = (bf16[64,2048]{1,0:T(8,128)(2,1)S(1)}, bf16[64,2048]{1,0:T(8,128)(2,1)S(1)}, u32[]{:S(2)}, u32[]{:S(2)}) collective-permute-start(bf16[64,2048]{1,0:T(8,128)(2,1)S(1)} %fusion.63), channel_id=1, source_target_pairs={{0,2},{1,3},{6,4},{7,5},{8,10},{9,11},{14,12},{15,13},{16,18},{17,... | collective-permute-start | bytes 786440 | tf_op jit(solution)/shard_map/ppermute | solution.py:20
  134.0 11.8 %collective-permute-start.32 = (bf16[64,2048]{1,0:T(8,128)(2,1)S(1)}, bf16[64,2048]{1,0:T(8,128)(2,1)S(1)}, u32[]{:S(2)}, u32[]{:S(2)}) collective-permute-start(bf16[64,2048]{1,0:T(8,128)(2,1)S(1)} %fusion.60), channel_id=1, source_target_pairs={{0,2},{1,3},{6,4},{7,5},{8,10},{9,11},{14,12},{15,13},{16,18},{17,... | collective-permute-start | bytes 786440 | tf_op jit(solution)/shard_map/ppermute | solution.py:20
  140.6 24.8 %collective-permute-start.30 = (bf16[64,2048]{1,0:T(8,128)(2,1)S(1)}, bf16[64,2048]{1,0:T(8,128)(2,1)S(1)}, u32[]{:S(2)}, u32[]{:S(2)}) collective-permute-start(bf16[64,2048]{1,0:T(8,128)(2,1)S(1)} %constant_dynamic-slice_fusion.6), channel_id=1, source_target_pairs={{0,1},{1,0},{2,3},{3,2},{4,5},{5,4},{6,7},{7,6},{8,9},{9,8},{10,11... | collective-permute-start | bytes 786440 | tf_op jit(solution)/shard_map/ppermute | solution.py:15
  145.8 9.8 %collective-permute-start.38 = (bf16[64,2048]{1,0:T(8,128)(2,1)S(1)}, bf16[64,2048]{1,0:T(8,128)(2,1)S(1)}, u32[]{:S(2)}, u32[]{:S(2)}) collective-permute-start(bf16[64,2048]{1,0:T(8,128)(2,1)S(1)} %fusion.62), channel_id=1, source_target_pairs={{0,2},{1,3},{6,4},{7,5},{8,10},{9,11},{14,12},{15,13},{16,18},{17,... | collective-permute-start | bytes 786440 | tf_op jit(solution)/shard_map/ppermute | solution.py:20
  155.6 8.9 %collective-permute-start.36 = (bf16[64,2048]{1,0:T(8,128)(2,1)S(1)}, bf16[64,2048]{1,0:T(8,128)(2,1)S(1)}, u32[]{:S(2)}, u32[]{:S(2)}) collective-permute-start(bf16[64,2048]{1,0:T(8,128)(2,1)S(1)} %fusion.61), channel_id=1, source_target_pairs={{0,2},{1,3},{6,4},{7,5},{8,10},{9,11},{14,12},{15,13},{16,18},{17,... | collective-permute-start | bytes 786440 | tf_op jit(solution)/shard_map/ppermute | solution.py:20
  165.4 9.2 %collective-permute-start.54 = (bf16[32,4096]{1,0:T(8,128)(2,1)S(1)}, bf16[32,4096]{1,0:T(8,128)(2,1)S(1)}, u32[]{:S(2)}, u32[]{:S(2)}) collective-permute-start(bf16[32,4096]{1,0:T(8,128)(2,1)S(1)} %copy-done.15), channel_id=1, source_target_pairs={{0,16},{16,0},{1,17},{17,1},{2,18},{18,2},{3,19},{19,3},{4,20},{20... | collective-permute-start | bytes 786440 | tf_op jit(solution)/shard_map/ppermute | solution.py:15
  167.0 21.5 %collective-permute-start.52 = (bf16[64,4096]{1,0:T(8,128)(2,1)S(1)}, bf16[64,4096]{1,0:T(8,128)(2,1)S(1)}, u32[]{:S(2)}, u32[]{:S(2)}) collective-permute-start(bf16[64,4096]{1,0:T(8,128)(2,1)S(1)} %copy-done.12), channel_id=1, source_target_pairs={{0,16},{16,0},{1,17},{17,1},{2,18},{18,2},{3,19},{19,3},{4,20},{20... | collective-permute-start | bytes 1572872 | tf_op jit(solution)/shard_map/ppermute | solution.py:15
  168.7 19.8 %collective-permute-start.56 = (bf16[32,4096]{1,0:T(8,128)(2,1)S(1)}, bf16[32,4096]{1,0:T(8,128)(2,1)S(1)}, u32[]{:S(2)}, u32[]{:S(2)}) collective-permute-start(bf16[32,4096]{1,0:T(8,128)(2,1)S(1)} %copy-done.16), channel_id=1, source_target_pairs={{0,16},{16,0},{1,17},{17,1},{2,18},{18,2},{3,19},{19,3},{4,20},{20... | collective-permute-start | bytes 786440 | tf_op jit(solution)/shard_map/ppermute | solution.py:15
  171.3 19.8 %collective-permute-start.49 = (bf16[32,4096]{1,0:T(8,128)(2,1)}, bf16[32,4096]{1,0:T(8,128)(2,1)S(1)}, u32[]{:S(2)}, u32[]{:S(2)}) collective-permute-start(bf16[32,4096]{1,0:T(8,128)(2,1)} %collective-permute-done.48), channel_id=1, source_target_pairs={{0,1},{1,0},{2,3},{3,2},{4,5},{5,4},{6,7},{7,6},{8,9},{9,8},{10,11... | collective-permute-start | bytes 786440 | tf_op jit(solution)/shard_map/ppermute | solution.py:15
  171.4 21.3 %collective-permute-start.51 = (bf16[32,4096]{1,0:T(8,128)(2,1)S(1)}, bf16[32,4096]{1,0:T(8,128)(2,1)S(1)}, u32[]{:S(2)}, u32[]{:S(2)}) collective-permute-start(bf16[32,4096]{1,0:T(8,128)(2,1)S(1)} %collective-permute-done.50), channel_id=1, source_target_pairs={{0,1},{1,0},{2,3},{3,2},{4,5},{5,4},{6,7},{7,6},{8,9},{9,8},{10,11... | collective-permute-start | bytes 786440 | tf_op jit(solution)/shard_map/ppermute | solution.py:15
  174.6 18.9 %collective-permute-start.55 = (bf16[32,4096]{1,0:T(8,128)(2,1)S(1)}, bf16[32,4096]{1,0:T(8,128)(2,1)S(1)}, u32[]{:S(2)}, u32[]{:S(2)}) collective-permute-start(bf16[32,4096]{1,0:T(8,128)(2,1)S(1)} %collective-permute-done.54), channel_id=1, source_target_pairs={{0,1},{1,0},{2,3},{3,2},{4,5},{5,4},{6,7},{7,6},{8,9},{9,8},{10,11... | collective-permute-start | bytes 786440 | tf_op jit(solution)/shard_map/ppermute | solution.py:15
  188.5 5.1 %collective-permute-start.57 = (bf16[32,4096]{1,0:T(8,128)(2,1)S(1)}, bf16[32,4096]{1,0:T(8,128)(2,1)S(1)}, u32[]{:S(2)}, u32[]{:S(2)}) collective-permute-start(bf16[32,4096]{1,0:T(8,128)(2,1)S(1)} %collective-permute-done.56), channel_id=1, source_target_pairs={{0,1},{1,0},{2,3},{3,2},{4,5},{5,4},{6,7},{7,6},{8,9},{9,8},{10,11... | collective-permute-start | bytes 786440 | tf_op jit(solution)/shard_map/ppermute | solution.py:15
  188.5 4.4 %collective-permute-start.53 = (bf16[64,4096]{1,0:T(8,128)(2,1)S(1)}, bf16[64,4096]{1,0:T(8,128)(2,1)S(1)}, u32[]{:S(2)}, u32[]{:S(2)}) collective-permute-start(bf16[64,4096]{1,0:T(8,128)(2,1)S(1)} %collective-permute-done.52), channel_id=1, source_target_pairs={{0,1},{1,0},{2,3},{3,2},{4,5},{5,4},{6,7},{7,6},{8,9},{9,8},{10,11... | collective-permute-start | bytes 1572872 | tf_op jit(solution)/shard_map/ppermute | solution.py:15
  191.1 25.1 %collective-permute-start.58 = (bf16[512,1024]{1,0:T(8,128)(2,1)S(1)}, bf16[512,1024]{1,0:T(8,128)(2,1)S(1)}, u32[]{:S(2)}, u32[]{:S(2)}) collective-permute-start(bf16[512,1024]{1,0:T(8,128)(2,1)S(1)} %fusion.51), channel_id=1, source_target_pairs={{0,16},{16,0},{1,17},{17,1},{2,18},{18,2},{3,19},{19,3},{4,20},{20... | collective-permute-start | bytes 3145736 | tf_op jit(solution)/shard_map/ppermute | solution.py:15
  192.7 39.3 %collective-permute-start.40 = (bf16[64,2048]{1,0:T(8,128)(2,1)S(1)}, bf16[64,2048]{1,0:T(8,128)(2,1)S(1)}, u32[]{:S(2)}, u32[]{:S(2)}) collective-permute-start(bf16[64,2048]{1,0:T(8,128)(2,1)S(1)} %constant_dynamic-slice_fusion.2), channel_id=1, source_target_pairs={{0,1},{1,0},{2,3},{3,2},{4,5},{5,4},{6,7},{7,6},{8,9},{9,8},{10,11... | collective-permute-start | bytes 786440 | tf_op jit(solution)/shard_map/ppermute | solution.py:15
  193.5 38.5 %collective-permute-start.29 = (bf16[64,2048]{1,0:T(8,128)(2,1)S(1)}, bf16[64,2048]{1,0:T(8,128)(2,1)S(1)}, u32[]{:S(2)}, u32[]{:S(2)}) collective-permute-start(bf16[64,2048]{1,0:T(8,128)(2,1)S(1)} %constant_dynamic-slice_fusion.7), channel_id=1, source_target_pairs={{0,1},{1,0},{2,3},{3,2},{4,5},{5,4},{6,7},{7,6},{8,9},{9,8},{10,11... | collective-permute-start | bytes 786440 | tf_op jit(solution)/shard_map/ppermute | solution.py:15
  194.7 37.3 %collective-permute-start.39 = (bf16[64,4096]{1,0:T(8,128)(2,1)S(1)}, bf16[64,4096]{1,0:T(8,128)(2,1)S(1)}, u32[]{:S(2)}, u32[]{:S(2)}) collective-permute-start(bf16[64,4096]{1,0:T(8,128)(2,1)S(1)} %pad_maximum_fusion.5), channel_id=1, source_target_pairs={{2,4},{3,5},{4,2},{5,3},{10,12},{11,13},{12,10},{13,11},{18,20},{1... | collective-permute-start | bytes 1572872 | tf_op jit(solution)/shard_map/ppermute | solution.py:20
  195.7 36.4 %collective-permute-start.35 = (bf16[64,2048]{1,0:T(8,128)(2,1)S(1)}, bf16[64,2048]{1,0:T(8,128)(2,1)S(1)}, u32[]{:S(2)}, u32[]{:S(2)}) collective-permute-start(bf16[64,2048]{1,0:T(8,128)(2,1)S(1)} %add_convert_fusion.6), channel_id=1, source_target_pairs={{0,2},{1,3},{2,0},{3,1},{4,6},{5,7},{6,4},{7,5},{8,10},{9,11},{10,... | collective-permute-start | bytes 786440 | tf_op jit(solution)/shard_map/ppermute | solution.py:20
  216.2 15.8 %collective-permute-start.45 = (bf16[64,2048]{1,0:T(8,128)(2,1)S(1)}, bf16[64,2048]{1,0:T(8,128)(2,1)S(1)}, u32[]{:S(2)}, u32[]{:S(2)}) collective-permute-start(bf16[64,2048]{1,0:T(8,128)(2,1)S(1)} %add_convert_fusion.1), channel_id=1, source_target_pairs={{0,2},{1,3},{2,0},{3,1},{4,6},{5,7},{6,4},{7,5},{8,10},{9,11},{10,... | collective-permute-start | bytes 786440 | tf_op jit(solution)/shard_map/ppermute | solution.py:20
  (32 other events, 173.9 us)
